TPU v7x, 32 devices: a whole 2x2x4 slice. The times are simulated.
32 devices in a mesh: tm: 8 (over z, x), state: 4 (over y, core).
Axes of the slice: x: 2, y: 2, z: 4, core: 2. Of those that a mesh axis runs over, the one named last changes fastest.
Arguments:
- dyn_cols: int32 [256, 8, 3], P('tm', 'state'), may hold values from 0 to 7, as said below
- dyn_vals: bfloat16 [256, 8, 64, 192], P('tm', 'state'), may hold values from -1 to 1
- obs_blocks: int32 [256, 2], P('tm'), may hold values from 0 to 7
- obs_op: bfloat16 [256, 64, 128], P('tm'), may hold values from -0.75 to 0.75
- obs_counts: int32 [256], P('tm'), may hold values from 32 to 128, as said below
- obs_values: float32 [256, 128], P('tm'), may hold values from -6 to 6
- gain: bfloat16 [256, 512, 128], P('tm', 'state'), may hold values from -0.0078125 to 0.0078125
- sources: float32 [256, 512], P('tm', 'state'), may hold values from -0.625 to 0.625
- prior: float32 [512], replicated, may hold values from -6 to 6
Outputs:
- filtered: float32 [256, 512], P('tm', 'state')
Inputs may be any that keep to these rules, and one draw needn't show every extreme that they name: `dyn_cols`: for every step and block row i, the first entry is i itself and the 3 entries are distinct block columns. `obs_counts`: some step has all 128 observations present.
All inputs are finite; a program needn't handle non-finite values.
Results may differ from a plain program's by a relative error of at most 0.0003.
The roundings to bfloat16 on the way count: a program that leaves them out, or rounds other values in their place, can miss the bound.
Values may be sent and summed in bfloat16 or wider, within the bound.
No kernel may reach another device: no remote copies, remote signals or barrier semaphores. Data moves between devices by JAX's collectives and lax.ppermute only.
A program may use at most 128 MiB of HBM per device.

v0:
```python
import functools

import jax
import jax.numpy as jnp
from jax import lax
from jax.experimental import pallas as pl
from jax.experimental.pallas import tpu as pltpu
from jax.sharding import PartitionSpec as P


BF = jnp.bfloat16
F32 = jnp.float32
VMEM_LIMIT = 8 * 1024 * 1024
ROWS = 16


def nt(a, b):
    return lax.dot_general(a, b, (((1,), (1,)), ((), ())), preferred_element_type=F32)


def nn(a, b):
    return lax.dot_general(a, b, (((1,), (0,)), ((), ())), preferred_element_type=F32)


def tn(a, b):
    return lax.dot_general(a, b, (((0,), (0,)), ((), ())), preferred_element_type=F32)


def split3(row):
    hi = row.astype(BF).astype(F32)
    rest = row - hi
    mid = rest.astype(BF).astype(F32)
    low = rest - mid
    at = lax.broadcasted_iota(jnp.int32, (ROWS, row.shape[1]), 0)
    zero = jnp.zeros((), F32)
    return jnp.where(at == 0, hi, jnp.where(at == 1, mid, jnp.where(at == 2, low, zero))).astype(BF)


def turn(block, by):
    return jnp.concatenate([block[:, by:], block[:, :by]], axis=1)


def fold(rows):
    return jnp.sum(rows, axis=0, keepdims=True)


def vmem(n):
    return [pl.BlockSpec(memory_space=pltpu.VMEM)] * n


def pack_kernel(parts, pairs, bs, chunk, table, s_ref, tm_ref, *refs):
    vals, gains = refs[:parts], refs[parts : 2 * parts]
    refs = refs[2 * parts :]
    if table:
        source_ref, cols_ref = refs[:2]
        refs = refs[2:]
        tables = refs[parts:]
        for d in range(parts):
            tables[d][...] = jnp.zeros(tables[d].shape, F32)
            begin = pl.multiple_of((s_ref[0] ^ d) * chunk, chunk)
            tables[d][:chunk, :] = source_ref[pl.ds(begin, chunk), :]
            for e in range(cols_ref.shape[0]):
                for i in range(cols_ref.shape[1]):
                    at = chunk + e * cols_ref.shape[1] + i
                    line = cols_ref[e, i : i + 1, :].astype(F32)
                    tables[d][at : at + 1, : line.shape[1]] = line
    outs = refs[:parts]
    for d in range(parts):
        for q in range(pairs):
            for i in range(2):
                outs[d][0, q, i * bs : (i + 1) * bs, :] = vals[d][0, 2 * q + i, :, : 2 * bs]
            base = 2 * bs
            third = jnp.concatenate(
                [vals[d][0, 2 * q, :, 2 * bs :], vals[d][0, 2 * q + 1, :, 2 * bs :]], axis=1
            )
            outs[d][0, q, base : base + bs, :] = third
            base = 3 * bs
            outs[d][0, q, base : base + 2 * bs, :] = gains[d][0, q * 2 * bs : (q + 1) * 2 * bs, :]


def pack(position, span, dyn_vals, gain, parts, chunk, first, count, table=()):
    _, lb, bs, width = dyn_vals.shape
    rows, obs = gain.shape[1:]
    pairs = lb // 2

    def from_part(d, trail):
        return lambda j, s, t: ((s[0] ^ d) * chunk + first + j,) + (0,) * trail

    shape = (count, pairs, 5 * bs, 2 * bs)
    tables = [jax.ShapeDtypeStruct((chunk + 3 * lb, lb * bs), F32)] * (parts if table else 0)
    return pl.pallas_call(
        functools.partial(pack_kernel, parts, pairs, bs, chunk, bool(table)),
        grid_spec=pltpu.PrefetchScalarGridSpec(
            num_scalar_prefetch=2,
            grid=(count,),
            in_specs=[pl.BlockSpec((1, lb, bs, width), from_part(d, 3)) for d in range(parts)]
            + [pl.BlockSpec((1, rows, obs), from_part(d, 2)) for d in range(parts)]
            + vmem(len(table)),
            out_specs=[pl.BlockSpec((1,) + shape[1:], lambda j, s, t: (j, 0, 0, 0))] * parts
            + vmem(len(tables)),
        ),
        out_shape=[jax.ShapeDtypeStruct(shape, BF)] * parts + tables,
        compiler_params=pltpu.CompilerParams(vmem_limit_bytes=VMEM_LIMIT),
    )(position, span, *([dyn_vals] * parts), *([gain] * parts), *table)


def chunk_kernel(
    parts, pairs, bs, chunk, first, count, s_ref, tm_ref, blocks_ref, counts_ref, *refs
):
    cols, refs = refs[:parts], refs[parts:]
    data, small = refs[:parts], refs[parts : 2 * parts]
    op_ref, values_ref, prior_ref, hi_in, lo_in, vec_in = refs[2 * parts : 2 * parts + 6]
    elements, offsets, hi_ref, lo_ref, vec_ref = refs[2 * parts + 6 : 2 * parts + 11]
    dyn, gains, source, chosen = refs[2 * parts + 11 :]
    s = s_ref[0]
    ns = parts * pairs * 2 * bs
    lane = lax.broadcasted_iota(jnp.int32, (bs, 2 * bs), 1)
    left = lane < bs
    zero = jnp.zeros((), BF)
    tiles = parts * pairs
    lane_row = lax.broadcasted_iota(jnp.int32, (1, 2 * bs), 1)
    slot = lax.broadcasted_iota(jnp.int32, (2 * bs, 1), 0)
    for d in range(parts):
        for q in range(pairs):
            source[(s ^ d) * pairs + q] = small[d][:chunk, q * 2 * bs : (q + 1) * 2 * bs]
    for j in range(count):
        here = first + j
        k = s * chunk + here
        dyn[...] = jnp.zeros(dyn.shape, BF)
        for d in range(parts):
            for q in range(pairs):
                group = (s ^ d) * pairs + q
                gains[pl.ds(pl.multiple_of(group * 2 * bs, 2 * bs), 2 * bs), :] = data[d][
                    j, q, 3 * bs : 5 * bs, :
                ]
                third = data[d][j, q, 2 * bs : 3 * bs, :]
                third_turned = turn(third, bs)
                for i in range(2):
                    both = data[d][j, q, i * bs : (i + 1) * bs, :]
                    both_turned = turn(both, bs)
                    lefts = (both, both_turned, third if i == 0 else third_turned)
                    rights = (both_turned, both, third_turned if i == 0 else third)
                    row = pl.multiple_of(group * 2 * bs + i * bs, bs)
                    for e in range(3):
                        column = cols[d][chunk + e * 2 * pairs + 2 * q + i, k].astype(jnp.int32)
                        side = column % 2
                        value = jnp.where(
                            side == 0,
                            jnp.where(left, lefts[e], zero),
                            jnp.where(left, zero, rights[e]),
                        )
                        dyn[side * tiles + column // 2, pl.ds(row, bs), :] = value
        operator = op_ref[k].astype(F32)
        diagonal = jnp.concatenate(
            [jnp.where(left, operator, 0.0), jnp.where(left, 0.0, operator)], axis=0
        ).astype(BF)
        picks = []
        for o in range(2):
            block = blocks_ref[o, k]
            for tile in range(tiles):
                found = pl.ds(pl.multiple_of(block * bs, bs), bs)
                chosen[o * bs : (o + 1) * bs, tile * 2 * bs : (tile + 1) * 2 * bs] = (
                    dyn[tile, found, :] + dyn[tiles + tile, found, :]
                )
            row = source[block // 2, pl.ds(here, 1), :]
            turned = pltpu.roll(row, bs, 1)
            picks.append(jnp.where(block % 2 == o, row, turned))
        image = tn(diagonal, chosen[...])
        masked = jnp.where(slot < counts_ref[k], image, 0.0).astype(BF)
        pick = jnp.where(lane_row < bs, picks[0], picks[1])
        source_image = fold(nn(split3(pick), diagonal)).astype(BF).astype(F32)
        innovation = jnp.where(
            lane_row < counts_ref[k], values_ref[pl.ds(k, 1), :] - source_image, 0.0
        )
        shift = fold(nt(split3(innovation), gains[...]))
        shift = shift + jnp.concatenate(
            [source[g, pl.ds(here, 1), :] for g in range(parts * pairs)], axis=1
        )
        offsets[j] = jnp.broadcast_to(shift, (8, ns))
        for g in range(parts * pairs):
            rows = slice(g * 2 * bs, (g + 1) * 2 * bs)
            correction = nn(gains[rows, :], masked)
            for tile in range(tiles):
                lanes = slice(tile * 2 * bs, (tile + 1) * 2 * bs)
                forward = (dyn[tile, rows, :] + dyn[tiles + tile, rows, :]).astype(F32)
                elements[j, rows, lanes] = (forward - correction[:, lanes]).astype(BF)
    if first == 0:
        begin = jnp.logical_and(s == 0, tm_ref[0] == 0)
        vec = jnp.where(begin, prior_ref[...], 0.0)
    else:
        vec = vec_in[...]
    step_rows = 256 if ns % 256 == 0 else ns
    for j in range(count):
        element = elements[j]
        vec = fold(nt(split3(vec), element)) + offsets[j, 0:1, :]
        for r in range(0, ns, step_rows):
            rows = slice(r, r + step_rows)
            if first == 0 and j == 0:
                across = lax.broadcasted_iota(jnp.int32, (step_rows, ns), 1)
                down = lax.broadcasted_iota(jnp.int32, (step_rows, ns), 0) + r
                unit = jnp.where(across == down, 1.0, 0.0).astype(BF)
                hi_ref[rows, :] = nt(unit, element).astype(BF)
                lo_ref[rows, :] = jnp.zeros((step_rows, ns), BF)
                continue
            if j == 0:
                hi, lo = hi_in[rows, :], lo_in[rows, :]
            else:
                hi, lo = hi_ref[rows, :], lo_ref[rows, :]
            if first == 0 and j == 1:
                moved = nt(hi, element)
            else:
                moved = nt(hi, element) + nt(lo, element)
            top = moved.astype(BF)
            hi_ref[rows, :] = top
            lo_ref[rows, :] = (moved - top.astype(F32)).astype(BF)
    vec_ref[...] = vec


def chunk_piece(
    position, span, blocks, counts, data, small, obs_op, obs_values, prior, state, chunk, first, count
):
    parts = len(data)
    pairs, _, width = data[0].shape[1:]
    bs = width // 2
    ns = parts * pairs * width
    if state is None:
        state = (data[0], data[0], prior)
    return pl.pallas_call(
        functools.partial(chunk_kernel, parts, pairs, bs, chunk, first, count),
        grid_spec=pltpu.PrefetchScalarGridSpec(
            num_scalar_prefetch=4,
            grid=(),
            in_specs=[pl.BlockSpec(memory_space=pltpu.SMEM)] * parts + vmem(2 * parts + 6),
            out_specs=vmem(5),
            scratch_shapes=[
                pltpu.VMEM((2 * parts * pairs, ns, width), BF),
                pltpu.VMEM((ns, width), BF),
                pltpu.VMEM((parts * pairs, chunk, width), F32),
                pltpu.VMEM((width, ns), BF),
            ],
        ),
        out_shape=[
            jax.ShapeDtypeStruct((count, ns, ns), BF),
            jax.ShapeDtypeStruct((count, 8, ns), F32),
            jax.ShapeDtypeStruct((ns, ns), BF),
            jax.ShapeDtypeStruct((ns, ns), BF),
            jax.ShapeDtypeStruct((1, ns), F32),
        ],
        compiler_params=pltpu.CompilerParams(vmem_limit_bytes=VMEM_LIMIT),
    )(
        position, span, blocks, counts, *small, *data, *small, obs_op, obs_values, prior, *state,
    )


def apply_map(row, hi, lo):
    parts = split3(row)
    return fold(nn(parts, hi) + nn(parts, lo))


def join_kernel(hi_one, lo_one, hi_two, lo_two, hi_ref, lo_ref):
    ns = hi_ref.shape[0]
    step = 256 if ns % 256 == 0 else ns
    for r in range(0, ns, step):
        rows = slice(r, r + step)
        product = nn(hi_one[rows, :], hi_two[...]) + (
            nn(hi_one[rows, :], lo_two[...]) + nn(lo_one[rows, :], hi_two[...])
        )
        top = product.astype(BF)
        hi_ref[rows, :] = top
        lo_ref[rows, :] = (product - top.astype(F32)).astype(BF)


def join(one, two):
    return pl.pallas_call(
        join_kernel,
        in_specs=vmem(4),
        out_specs=vmem(2),
        out_shape=[jax.ShapeDtypeStruct(x.shape, BF) for x in two],
        compiler_params=pltpu.CompilerParams(vmem_limit_bytes=VMEM_LIMIT),
        name="join",
    )(*one, *two)


def hop_kernel(row_ref, hi_ref, lo_ref, vec_ref, out_ref):
    out_ref[...] = apply_map(row_ref[...], hi_ref[...], lo_ref[...]) + vec_ref[...]


def hop(row, hi, lo, vec):
    return pl.pallas_call(
        hop_kernel,
        in_specs=vmem(4),
        out_specs=vmem(1)[0],
        out_shape=jax.ShapeDtypeStruct(row.shape, F32),
        compiler_params=pltpu.CompilerParams(vmem_limit_bytes=VMEM_LIMIT),
        name="hop",
    )(row, hi, lo, vec)


def span_kernel(leaders, whole, early, s_ref, tm_ref, row_ref, direct_ref, *refs):
    maps, out_ref = [refs[3 * n : 3 * n + 3] for n in range(leaders)], refs[3 * leaders]
    for mine in range(leaders):

        @pl.when(s_ref[0] // 2 == mine)
        def _():
            current = row_ref[...]
            for p in range(leaders if whole else mine):
                hi, lo, vec = maps[p ^ mine]
                current = apply_map(current, hi[...], lo[...]) + vec[...]
            if not whole:
                current = jnp.where(tm_ref[0] < early, direct_ref[...], current)
            out_ref[...] = current


def span_hop(position, span, row, direct, maps, whole, early):
    leaders = len(maps)
    return pl.pallas_call(
        functools.partial(span_kernel, leaders, whole, early),
        grid_spec=pltpu.PrefetchScalarGridSpec(
            num_scalar_prefetch=2,
            grid=(),
            in_specs=vmem(2 + 3 * leaders),
            out_specs=vmem(1)[0],
        ),
        out_shape=jax.ShapeDtypeStruct(row.shape, F32),
        compiler_params=pltpu.CompilerParams(vmem_limit_bytes=VMEM_LIMIT),
        name="span_hop" if whole else "lead",
    )(position, span, row, direct, *[m for trio in maps for m in trio])


def sweep_kernel(pieces, parts, s_ref, tm_ref, *refs):
    own_ref, told_ref, prior_ref, hi, lo, vec = refs[:6]
    refs = refs[6:]
    elements, offsets = refs[:pieces], refs[pieces : 2 * pieces]
    outs = refs[2 * pieces : 2 * pieces + parts]
    current_ref, spread = refs[2 * pieces + parts :]
    s = s_ref[0]
    begin = jnp.logical_and(s == 0, tm_ref[0] == 0)

    @pl.when(s % 2 == 0)
    def _():
        current_ref[...] = told_ref[...] + jnp.where(begin, prior_ref[...], 0.0)

    @pl.when(s % 2 == 1)
    def _():
        current_ref[...] = apply_map(own_ref[...], hi[...], lo[...]) + vec[...]

    current = current_ref[...]
    at = 0
    width = spread.shape[2]
    for p in range(pieces):
        for j in range(elements[p].shape[0]):
            current = fold(nt(split3(current), elements[p][j])) + offsets[p][j, 0:1, :]
            for d in range(parts):
                spread[d, at : at + 1, :] = current[:, d * width : (d + 1) * width]
            at += 1
    for d in range(parts):
        outs[d][...] = spread[s ^ d]


def sweep(position, span, own, told, prior, even, elements, offsets, parts):
    ns = own.shape[1]
    pieces = len(elements)
    chunk = sum(e.shape[0] for e in elements)
    width = ns // parts
    return pl.pallas_call(
        functools.partial(sweep_kernel, pieces, parts),
        grid_spec=pltpu.PrefetchScalarGridSpec(
            num_scalar_prefetch=2,
            grid=(),
            in_specs=vmem(6 + 2 * pieces),
            out_specs=vmem(parts),
            scratch_shapes=[
                pltpu.VMEM((1, ns), F32),
                pltpu.VMEM((parts, chunk, width), F32),
            ],
        ),
        out_shape=[jax.ShapeDtypeStruct((chunk, width), F32)] * parts,
        compiler_params=pltpu.CompilerParams(vmem_limit_bytes=VMEM_LIMIT),
        name="sweep",
    )(position, span, own, told, prior, *even, *elements, *offsets)


PIECES = 4


def piece_sizes(chunk):
    base, more = divmod(chunk, PIECES)
    return [base + 1] * more + [base] * (PIECES - more)


def means(dyn_cols, dyn_vals, obs_blocks, obs_op, obs_counts, obs_values, gain, sources, prior):
    steps, _, _, _ = dyn_vals.shape
    parts = lax.axis_size("state")
    spans = lax.axis_size("tm")
    chunk = steps // parts
    ns = prior.shape[0]
    s = lax.axis_index("state")
    t = lax.axis_index("tm")
    position = s.reshape(1).astype(jnp.int32)
    span = t.reshape(1).astype(jnp.int32)
    prior_row = prior.reshape(1, ns)

    def across(x, d):
        return lax.ppermute(x, "state", [(i, i ^ d) for i in range(parts)])

    def send(x, pairs):
        return lax.ppermute(x, ("tm", "state"), [(a * parts + b, c * parts + e) for (a, b), (c, e) in pairs])

    order = sorted(range(1, parts), reverse=True)
    sizes = piece_sizes(chunk)
    firsts = [sum(sizes[:n]) for n in range(len(sizes))]
    vals_far = pltpu.with_memory_space_constraint(dyn_vals, pltpu.HBM)
    gain_far = pltpu.with_memory_space_constraint(gain, pltpu.HBM)
    pieces = []
    for n, (first, size) in enumerate(zip(firsts, sizes)):
        source_arrays = (vals_far, gain_far) if n == 0 else (dyn_vals, gain)
        table = (sources, dyn_cols.transpose(2, 1, 0)) if n == 0 else ()
        packed = pack(position, span, *source_arrays, parts, chunk, first, size, table)
        arrived = {0: packed[0]}
        for d in order:
            arrived[d] = across(packed[d], d)
        pieces.append([arrived[d] for d in range(parts)])
        if n == 0:
            small = {0: packed[parts]}
            for d in order:
                small[d] = across(packed[parts + d], d)
            small = [small[d] for d in range(parts)]

    state = None
    elements, offsets = [], []
    for first, size, data in zip(firsts, sizes, pieces):
        element, offset, *state = chunk_piece(
            position, span, obs_blocks.T, obs_counts, data, small, obs_op, obs_values,
            prior_row, state, chunk, first, size,
        )
        elements.append(element)
        offsets.append(offset)
    hi, lo, vec = state

    leads = [2 * p + 1 for p in range(parts // 2)]
    to_lead = [((a, l - 1), (a, l)) for a in range(spans) for l in leads]
    vec_even = send(vec, to_lead)
    hi_even = send(hi, to_lead)
    lo_even = send(lo, to_lead)
    pair_vec = hop(vec_even, hi, lo, vec)
    pair_hi, pair_lo = join((hi_even, lo_even), (hi, lo))
    pair = (pair_hi, pair_lo, pair_vec)

    early = min(2, spans - 1)
    maps = [pair]
    for d in range(2, parts, 2):
        pairs = [((a, l), (a, l ^ d)) for a in range(early, spans) for l in leads]
        far = []
        for x in pair:
            far.append(send(x, pairs))
        maps.append(tuple(far))

    direct = jnp.zeros((1, ns), F32)
    entry = jnp.zeros((1, ns), F32)
    current = pair_vec
    for g in range(early):
        for p in range(1, len(leads)):
            arriving = send(current, [((g, leads[p - 1]), (g, leads[p]))])
            direct = direct + arriving
            current = hop(arriving, *pair)
        if g + 1 < early:
            arriving = send(current, [((g, leads[-1]), (g + 1, leads[0]))])
            direct = direct + arriving
            current = hop(arriving, *pair)
        else:
            for l in leads:
                entry = entry + send(current, [((g, leads[-1]), (g + 1, l))])

    arriving = entry
    for h in range(early, spans - 1):
        current = span_hop(position, span, arriving, direct, maps, True, early)
        arriving = send(current, [((h, l), (h + 1, l)) for l in leads])
        entry = entry + arriving

    own = span_hop(position, span, entry, direct, maps, False, early)
    told = send(own, [(b, a) for a, b in to_lead])
    mine = sweep(
        position, span, own, told, prior_row, (hi_even, lo_even, vec_even), elements, offsets, parts
    )
    got = [mine[0]] + [across(mine[d], d) for d in range(1, parts)]
    bit = 1
    while bit < parts:
        swapped = [got[d ^ bit] for d in range(parts)]
        got = [jnp.where((s & bit) != 0, b, a) for a, b in zip(got, swapped)]
        bit *= 2
    return jnp.concatenate(got, axis=0)


def solution(mesh):
    return jax.shard_map(
        means,
        mesh=mesh,
        in_specs=(
            P("tm", "state", None),
            P("tm", "state", None, None),
            P("tm", None),
            P("tm", None, None),
            P("tm"),
            P("tm", None),
            P("tm", "state", None),
            P("tm", "state"),
            P(),
        ),
        out_specs=P("tm", "state"),
        check_vma=False,
    )
```

profile of v0, /device:TPU:26, one launch (start us, length us, event | category | flops | bytes accessed | tf_op | source)
XLA Modules:
  0.0 97.3 jit_solution(9826606138244344484)
XLA Ops:
  0.0 1.6 %copy-done = bf16[32,2,64,192]{3,2,1,0:T(8,128)(2,1)S(1)} copy-done((bf16[32,2,64,192]{3,2,1,0:T(8,128)(2,1)S(1)}, bf16[32,2,64,192]{3,2,1,0:T(8,128)(2,1)}, u32[]{:S(2)}) %copy-start) | copy-done | bytes 1572888
  1.6 1.2 %copy-done.2 = bf16[32,128,128]{2,1,0:T(8,128)(2,1)S(1)} copy-done((bf16[32,128,128]{2,1,0:T(8,128)(2,1)S(1)}, bf16[32,128,128]{2,1,0:T(8,128)(2,1)}, u32[]{:S(2)}) %copy-start.2) | copy-done | bytes 1048600
  4.0 1.5 %shard_map.91 = (bf16[2,1,320,128]{3,2,1,0:T(8,128)(2,1)S(1)}, bf16[2,1,320,128]{3,2,1,0:T(8,128)(2,1)S(1)}, bf16[2,1,320,128]{3,2,1,0:T(8,128)(2,1)S(1)}, bf16[...) custom-call(s32[1]{0:T(128)} %bitcast.s_ref, ...), custom_call_target="tpu_custom_call" | custom-call | tf_op jit(solution)/shard_map/pallas_call | solution.py:91
  5.6 1.6 %collective-permute-start.1 = (f32[14,128]{1,0:T(8,128)S(1)}, f32[14,128]{1,0:T(8,128)S(1)}, u32[]{:S(2)}, u32[]{:S(2)}) collective-permute-start(f32[14,128]{1,0:T(8,128)S(1)} %get-tuple-element.53), channel_id=1, source_target_pairs={{0,2},{1,3},{2,0},{3,1},{4,6},{5,7},{6,4},{7,5},{8,10},{9,11},{10,... | collective-permute-start | bytes 21512 | tf_op jit(solution)/shard_map/ppermute | solution.py:404
  7.4 1.5 %collective-permute-start.10 = (bf16[2,1,320,128]{3,2,1,0:T(8,128)(2,1)S(1)}, bf16[2,1,320,128]{3,2,1,0:T(8,128)(2,1)S(1)}, u32[]{:S(2)}, u32[]{:S(2)}) collective-permute-start(bf16[2,1,320,128]{3,2,1,0:T(8,128)(2,1)S(1)} %get-tuple-element.65), channel_id=1, source_target_pairs={{0,2},{1,3},{2,0},{3,1},{4,6},{5,7},{6,4},{7,5},{8,10},{9,11},{10,... | collective-permute-start | bytes 491528 | tf_op jit(solution)/shard_map/ppermute | solution.py:404
  10.2 0.7 collective-permute-start.12
  11.5 1.0 %collective-permute-start.14 = (bf16[2,1,320,128]{3,2,1,0:T(8,128)(2,1)S(1)}, bf16[2,1,320,128]{3,2,1,0:T(8,128)(2,1)S(1)}, u32[]{:S(2)}, u32[]{:S(2)}) collective-permute-start(bf16[2,1,320,128]{3,2,1,0:T(8,128)(2,1)S(1)} %get-tuple-element.70), channel_id=1, source_target_pairs={{0,3},{1,2},{2,1},{3,0},{4,7},{5,6},{6,5},{7,4},{8,11},{9,10},{10,... | collective-permute-start | bytes 491528 | tf_op jit(solution)/shard_map/ppermute | solution.py:404
  12.7 1.8 %collective-permute-done.10.refs_6_ = bf16[2,1,320,128]{3,2,1,0:T(8,128)(2,1)S(1)} collective-permute-done((bf16[2,1,320,128]{3,2,1,0:T(8,128)(2,1)S(1)}, bf16[2,1,320,128]{3,2,1,0:T(8,128)(2,1)S(1)}, u32[]{:S(2)}, u32[]{:S(2)}) %collective-permute-start.10) | collective-permute-done | bytes 163872 | tf_op jit(solution)/shard_map/ppermute | solution.py:404
  14.5 1.5 %collective-permute-start.7 = (bf16[2,1,320,128]{3,2,1,0:T(8,128)(2,1)S(1)}, bf16[2,1,320,128]{3,2,1,0:T(8,128)(2,1)S(1)}, u32[]{:S(2)}, u32[]{:S(2)}) collective-permute-start(bf16[2,1,320,128]{3,2,1,0:T(8,128)(2,1)S(1)} %get-tuple-element.61), channel_id=1, source_target_pairs={{0,2},{1,3},{2,0},{3,1},{4,6},{5,7},{6,4},{7,5},{8,10},{9,11},{10,... | collective-permute-start | bytes 491528 | tf_op jit(solution)/shard_map/ppermute | solution.py:404
  16.0 1.0 %collective-permute-done.11.refs_7_ = bf16[2,1,320,128]{3,2,1,0:T(8,128)(2,1)S(1)} collective-permute-done((bf16[2,1,320,128]{3,2,1,0:T(8,128)(2,1)S(1)}, bf16[2,1,320,128]{3,2,1,0:T(8,128)(2,1)S(1)}, u32[]{:S(2)}, u32[]{:S(2)}) %collective-permute-start.11) | collective-permute-done | bytes 163872 | tf_op jit(solution)/shard_map/ppermute | solution.py:404
  17.1 1.9 %collective-permute-start.8 = (bf16[2,1,320,128]{3,2,1,0:T(8,128)(2,1)S(1)}, bf16[2,1,320,128]{3,2,1,0:T(8,128)(2,1)S(1)}, u32[]{:S(2)}, u32[]{:S(2)}) collective-permute-start(bf16[2,1,320,128]{3,2,1,0:T(8,128)(2,1)S(1)} %get-tuple-element.62), channel_id=1, source_target_pairs={{0,3},{1,2},{2,1},{3,0},{4,7},{5,6},{6,5},{7,4},{8,11},{9,10},{10,... | collective-permute-start | bytes 491528 | tf_op jit(solution)/shard_map/ppermute | solution.py:404
  19.0 2.6 %collective-permute-done.13.refs_6_ = bf16[2,1,320,128]{3,2,1,0:T(8,128)(2,1)S(1)} collective-permute-done((bf16[2,1,320,128]{3,2,1,0:T(8,128)(2,1)S(1)}, bf16[2,1,320,128]{3,2,1,0:T(8,128)(2,1)S(1)}, u32[]{:S(2)}, u32[]{:S(2)}) %collective-permute-start.13) | collective-permute-done | bytes 163872 | tf_op jit(solution)/shard_map/ppermute | solution.py:404
  21.5 1.5 %collective-permute-start.4 = (bf16[2,1,320,128]{3,2,1,0:T(8,128)(2,1)S(1)}, bf16[2,1,320,128]{3,2,1,0:T(8,128)(2,1)S(1)}, u32[]{:S(2)}, u32[]{:S(2)}) collective-permute-start(bf16[2,1,320,128]{3,2,1,0:T(8,128)(2,1)S(1)} %get-tuple-element.57), channel_id=1, source_target_pairs={{0,2},{1,3},{2,0},{3,1},{4,6},{5,7},{6,4},{7,5},{8,10},{9,11},{10,... | collective-permute-start | bytes 491528 | tf_op jit(solution)/shard_map/ppermute | solution.py:404
  23.0 1.0 %collective-permute-done.14.refs_7_ = bf16[2,1,320,128]{3,2,1,0:T(8,128)(2,1)S(1)} collective-permute-done((bf16[2,1,320,128]{3,2,1,0:T(8,128)(2,1)S(1)}, bf16[2,1,320,128]{3,2,1,0:T(8,128)(2,1)S(1)}, u32[]{:S(2)}, u32[]{:S(2)}) %collective-permute-start.14) | collective-permute-done | bytes 163872 | tf_op jit(solution)/shard_map/ppermute | solution.py:404
  24.1 1.9 %collective-permute-start.5 = (bf16[2,1,320,128]{3,2,1,0:T(8,128)(2,1)S(1)}, bf16[2,1,320,128]{3,2,1,0:T(8,128)(2,1)S(1)}, u32[]{:S(2)}, u32[]{:S(2)}) collective-permute-start(bf16[2,1,320,128]{3,2,1,0:T(8,128)(2,1)S(1)} %get-tuple-element.58), channel_id=1, source_target_pairs={{0,3},{1,2},{2,1},{3,0},{4,7},{5,6},{6,5},{7,4},{8,11},{9,10},{10,... | collective-permute-start | bytes 491528 | tf_op jit(solution)/shard_map/ppermute | solution.py:404
  26.0 4.2 %shard_map.95 = (bf16[2,512,512]{2,1,0:T(8,128)(2,1)S(1)}, f32[2,8,512]{2,1,0:T(8,128)S(1)}, bf16[512,512]{1,0:T(8,128)(2,1)S(1)}, bf16[512,512]{1,0:T(8,128)(2,1)S(1)}, f32[1,512]{1,0:T(1,128)S(1)}) custom-call(s32[1]{0:T(128)} %bitcast.s_ref, s32[1]{0:T(128)} %bitcast.1.tm_ref, s32[2,32]{1,0:T(2,128)S(1)} %bitcast.11, s32[32]{0:T(128)S(1)} %copy-done.9, ...), custom_call_target="tpu_custom_call" | custom-call | tf_op jit(solution)/shard_map/pallas_call | solution.py:228
  30.2 4.7 %shard_map.96 = (bf16[2,512,512]{2,1,0:T(8,128)(2,1)S(1)}, f32[2,8,512]{2,1,0:T(8,128)S(1)}, bf16[512,512]{1,0:T(8,128)(2,1)S(1)}, bf16[512,512]{1,0:T(8,128)(2,1)S(1)}, f32[1,512]{1,0:T(1,128)S(1)}) custom-call(s32[1]{0:T(128)} %bitcast.s_ref, s32[1]{0:T(128)} %bitcast.1.tm_ref, s32[2,32]{1,0:T(2,128)S(1)} %bitcast.12, s32[32]{0:T(128)S(1)} %copy-done.9, ...), custom_call_target="tpu_custom_call" | custom-call | tf_op jit(solution)/shard_map/pallas_call | solution.py:228
  35.0 4.7 %shard_map.97 = (bf16[2,512,512]{2,1,0:T(8,128)(2,1)S(1)}, f32[2,8,512]{2,1,0:T(8,128)S(1)}, bf16[512,512]{1,0:T(8,128)(2,1)S(1)}, bf16[512,512]{1,0:T(8,128)(2,1)S(1)}, f32[1,512]{1,0:T(1,128)S(1)}) custom-call(s32[1]{0:T(128)} %bitcast.s_ref, s32[1]{0:T(128)} %bitcast.1.tm_ref, s32[2,32]{1,0:T(2,128)S(1)} %bitcast.13, s32[32]{0:T(128)S(1)} %copy-done.9, ...), custom_call_target="tpu_custom_call" | custom-call | tf_op jit(solution)/shard_map/pallas_call | solution.py:228
  39.8 4.7 %shard_map.98 = (bf16[2,512,512]{2,1,0:T(8,128)(2,1)S(1)}, f32[2,8,512]{2,1,0:T(8,128)S(1)}, bf16[512,512]{1,0:T(8,128)(2,1)S(1)}, bf16[512,512]{1,0:T(8,128)(2,1)S(1)}, f32[1,512]{1,0:T(1,128)S(1)}) custom-call(s32[1]{0:T(128)} %bitcast.s_ref, s32[1]{0:T(128)} %bitcast.1.tm_ref, s32[2,32]{1,0:T(2,128)S(1)} %bitcast.14, s32[32]{0:T(128)S(1)} %copy-done.9, ...), custom_call_target="tpu_custom_call" | custom-call | tf_op jit(solution)/shard_map/pallas_call | solution.py:228
  44.5 1.5 %collective-permute-start.17 = (bf16[512,512]{1,0:T(8,128)(2,1)S(1)}, bf16[512,512]{1,0:T(8,128)(2,1)S(1)}, u32[]{:S(2)}, u32[]{:S(2)}) collective-permute-start(bf16[512,512]{1,0:T(8,128)(2,1)S(1)} %get-tuple-element.81.hi_ref.hi_two), channel_id=1, source_target_pairs={{0,1},{2,3},{4,5},{6,7},{8,9},{10,11},{12,13},{14,15},{16,17},{18,... | collective-permute-start | bytes 1572872 | tf_op jit(solution)/shard_map/ppermute | solution.py:407
  46.0 1.4 %collective-permute-start.18 = (bf16[512,512]{1,0:T(8,128)(2,1)S(1)}, bf16[512,512]{1,0:T(8,128)(2,1)S(1)}, u32[]{:S(2)}, u32[]{:S(2)}) collective-permute-start(bf16[512,512]{1,0:T(8,128)(2,1)S(1)} %get-tuple-element.82.lo_ref.lo_two), channel_id=1, source_target_pairs={{0,1},{2,3},{4,5},{6,7},{8,9},{10,11},{12,13},{14,15},{16,17},{18,... | collective-permute-start | bytes 1572872 | tf_op jit(solution)/shard_map/ppermute | solution.py:407
  47.5 1.4 %collective-permute-done.18.lo_one.refs_4_ = bf16[512,512]{1,0:T(8,128)(2,1)S(1)} collective-permute-done((bf16[512,512]{1,0:T(8,128)(2,1)S(1)}, bf16[512,512]{1,0:T(8,128)(2,1)S(1)}, u32[]{:S(2)}, u32[]{:S(2)}) %collective-permute-start.18) | collective-permute-done | bytes 524320 | tf_op jit(solution)/shard_map/ppermute | solution.py:407
  48.9 1.0 %join.1 = (bf16[512,512]{1,0:T(8,128)(2,1)S(1)}, bf16[512,512]{1,0:T(8,128)(2,1)S(1)}) custom-call(bf16[512,512]{1,0:T(8,128)(2,1)S(1)} %collective-permute-done.17.hi_one.refs_3_, bf16[512,512]{1,0:T(8,128)(2,1)S(1)} %collective-permute-done.18.lo_one.refs_4_, bf16[512,512]{1,0:T(8,128)(2,1)S(1)} %get-tuple-element.81.hi_ref.hi_two, ...), custom_call_target="tpu_custom_call" | custom-call | tf_op jit(solution)/shard_map/join/pallas_call | solution.py:274
  49.9 0.7 collective-permute-start.23
  51.3 6.2 %collective-permute-start.15 = (f32[1,512]{1,0:T(1,128)S(1)}, f32[1,512]{1,0:T(1,128)S(1)}, u32[]{:S(2)}, u32[]{:S(2)}) collective-permute-start(f32[1,512]{1,0:T(1,128)S(1)} %get-tuple-element.80.vec_ref), channel_id=1, source_target_pairs={{0,1},{2,3},{4,5},{6,7},{8,9},{10,11},{12,13},{14,15},{16,17},{18,... | collective-permute-start | bytes 6152 | tf_op jit(solution)/shard_map/ppermute | solution.py:407
  57.5 0.8 collective-permute-done.15.row_ref.refs_5_
  69.6 1.3 %collective-permute-start.31 = (f32[1,512]{1,0:T(1,128)S(1)}, f32[1,512]{1,0:T(1,128)S(1)}, u32[]{:S(2)}, u32[]{:S(2)}) collective-permute-start(f32[1,512]{1,0:T(1,128)S(1)} %lead.1.refs_0_), channel_id=1, source_target_pairs={{1,0},{3,2},{5,4},{7,6},{9,8},{11,10},{13,12},{15,14},{17,16},{19,... | collective-permute-start | bytes 6152 | tf_op jit(solution)/shard_map/ppermute | solution.py:407
  70.9 18.4 %collective-permute-done.31.refs_1_ = f32[1,512]{1,0:T(1,128)S(1)} collective-permute-done((f32[1,512]{1,0:T(1,128)S(1)}, f32[1,512]{1,0:T(1,128)S(1)}, u32[]{:S(2)}, u32[]{:S(2)}) %collective-permute-start.31) | collective-permute-done | bytes 2080 | tf_op jit(solution)/shard_map/ppermute | solution.py:407
  89.3 1.7 %sweep.1 = (f32[8,128]{1,0:T(8,128)S(1)}, f32[8,128]{1,0:T(8,128)S(1)}, f32[8,128]{1,0:T(8,128)S(1)}, f32[8,128]{1,0:T(8,128)S(1)}) custom-call(s32[1]{0:T(128)} %bitcast.s_ref, s32[1]{0:T(128)} %bitcast.1.tm_ref, f32[1,512]{1,0:T(1,128)S(1)} %lead.1.refs_0_, f32[1,512]{1,0:T(1,128)S(1)} %collective-permute-done.31.refs_1_, f32[1,512]{1,0:T(1,128)S(1)} %bitcast.10, ...), custom_call_target="tpu_custom_call" | custom-call | tf_op jit(solution)/shard_map/sweep/pallas_call | solution.py:365
  90.9 2.1 %collective-permute-start.32 = (f32[8,128]{1,0:T(8,128)S(1)}, f32[8,128]{1,0:T(8,128)S(1)}, u32[]{:S(2)}, u32[]{:S(2)}) collective-permute-start(f32[8,128]{1,0:T(8,128)S(1)} %get-tuple-element.93), channel_id=1, source_target_pairs={{0,3},{1,2},{2,1},{3,0},{4,7},{5,6},{6,5},{7,4},{8,11},{9,10},{10,... | collective-permute-start | bytes 12296 | tf_op jit(solution)/shard_map/ppermute | solution.py:404
  93.3 1.1 %collective-permute-done.32 = f32[8,128]{1,0:T(8,128)S(1)} collective-permute-done((f32[8,128]{1,0:T(8,128)S(1)}, f32[8,128]{1,0:T(8,128)S(1)}, u32[]{:S(2)}, u32[]{:S(2)}) %collective-permute-start.32) | collective-permute-done | bytes 4128 | tf_op jit(solution)/shard_map/ppermute | solution.py:404
  94.4 2.3 %collective-permute-done.33 = f32[8,128]{1,0:T(8,128)S(1)} collective-permute-done((f32[8,128]{1,0:T(8,128)S(1)}, f32[8,128]{1,0:T(8,128)S(1)}, u32[]{:S(2)}, u32[]{:S(2)}) %collective-permute-start.33) | collective-permute-done | bytes 4128 | tf_op jit(solution)/shard_map/ppermute | solution.py:404
  (85 shorter events, 16.1 us)
Async XLA Ops:
  3.1 7.9 %collective-permute-start.6 = (bf16[2,1,320,128]{3,2,1,0:T(8,128)(2,1)S(1)}, bf16[2,1,320,128]{3,2,1,0:T(8,128)(2,1)S(1)}, u32[]{:S(2)}, u32[]{:S(2)}) collective-permute-start(bf16[2,1,320,128]{3,2,1,0:T(8,128)(2,1)S(1)} %get-tuple-element.60), channel_id=1, source_target_pairs={{0,1},{1,0},{2,3},{3,2},{4,5},{5,4},{6,7},{7,6},{8,9},{9,8},{10,11... | collective-permute-start | bytes 491528 | tf_op jit(solution)/shard_map/ppermute | solution.py:404
  3.4 8.0 %collective-permute-start.9 = (bf16[2,1,320,128]{3,2,1,0:T(8,128)(2,1)S(1)}, bf16[2,1,320,128]{3,2,1,0:T(8,128)(2,1)S(1)}, u32[]{:S(2)}, u32[]{:S(2)}) collective-permute-start(bf16[2,1,320,128]{3,2,1,0:T(8,128)(2,1)S(1)} %get-tuple-element.64), channel_id=1, source_target_pairs={{0,1},{1,0},{2,3},{3,2},{4,5},{5,4},{6,7},{7,6},{8,9},{9,8},{10,11... | collective-permute-start | bytes 491528 | tf_op jit(solution)/shard_map/ppermute | solution.py:404
  5.5 1.9 %collective-permute-start = (f32[14,128]{1,0:T(8,128)S(1)}, f32[14,128]{1,0:T(8,128)S(1)}, u32[]{:S(2)}, u32[]{:S(2)}) collective-permute-start(f32[14,128]{1,0:T(8,128)S(1)} %get-tuple-element.52), channel_id=1, source_target_pairs={{0,1},{1,0},{2,3},{3,2},{4,5},{5,4},{6,7},{7,6},{8,9},{9,8},{10,11... | collective-permute-start | bytes 21512 | tf_op jit(solution)/shard_map/ppermute | solution.py:404
  5.6 3.7 %collective-permute-start.1 = (f32[14,128]{1,0:T(8,128)S(1)}, f32[14,128]{1,0:T(8,128)S(1)}, u32[]{:S(2)}, u32[]{:S(2)}) collective-permute-start(f32[14,128]{1,0:T(8,128)S(1)} %get-tuple-element.53), channel_id=1, source_target_pairs={{0,2},{1,3},{2,0},{3,1},{4,6},{5,7},{6,4},{7,5},{8,10},{9,11},{10,... | collective-permute-start | bytes 21512 | tf_op jit(solution)/shard_map/ppermute | solution.py:404
  7.2 3.1 %collective-permute-start.2 = (f32[14,128]{1,0:T(8,128)S(1)}, f32[14,128]{1,0:T(8,128)S(1)}, u32[]{:S(2)}, u32[]{:S(2)}) collective-permute-start(f32[14,128]{1,0:T(8,128)S(1)} %get-tuple-element.54), channel_id=1, source_target_pairs={{0,3},{1,2},{2,1},{3,0},{4,7},{5,6},{6,5},{7,4},{8,11},{9,10},{10,... | collective-permute-start | bytes 21512 | tf_op jit(solution)/shard_map/ppermute | solution.py:404
  7.4 7.1 %collective-permute-start.10 = (bf16[2,1,320,128]{3,2,1,0:T(8,128)(2,1)S(1)}, bf16[2,1,320,128]{3,2,1,0:T(8,128)(2,1)S(1)}, u32[]{:S(2)}, u32[]{:S(2)}) collective-permute-start(bf16[2,1,320,128]{3,2,1,0:T(8,128)(2,1)S(1)} %get-tuple-element.65), channel_id=1, source_target_pairs={{0,2},{1,3},{2,0},{3,1},{4,6},{5,7},{6,4},{7,5},{8,10},{9,11},{10,... | collective-permute-start | bytes 491528 | tf_op jit(solution)/shard_map/ppermute | solution.py:404
  9.3 7.8 %collective-permute-start.11 = (bf16[2,1,320,128]{3,2,1,0:T(8,128)(2,1)S(1)}, bf16[2,1,320,128]{3,2,1,0:T(8,128)(2,1)S(1)}, u32[]{:S(2)}, u32[]{:S(2)}) collective-permute-start(bf16[2,1,320,128]{3,2,1,0:T(8,128)(2,1)S(1)} %get-tuple-element.66), channel_id=1, source_target_pairs={{0,3},{1,2},{2,1},{3,0},{4,7},{5,6},{6,5},{7,4},{8,11},{9,10},{10,... | collective-permute-start | bytes 491528 | tf_op jit(solution)/shard_map/ppermute | solution.py:404
  10.2 8.7 %collective-permute-start.12 = (bf16[2,1,320,128]{3,2,1,0:T(8,128)(2,1)S(1)}, bf16[2,1,320,128]{3,2,1,0:T(8,128)(2,1)S(1)}, u32[]{:S(2)}, u32[]{:S(2)}) collective-permute-start(bf16[2,1,320,128]{3,2,1,0:T(8,128)(2,1)S(1)} %get-tuple-element.68), channel_id=1, source_target_pairs={{0,1},{1,0},{2,3},{3,2},{4,5},{5,4},{6,7},{7,6},{8,9},{9,8},{10,11... | collective-permute-start | bytes 491528 | tf_op jit(solution)/shard_map/ppermute | solution.py:404
  11.0 10.6 %collective-permute-start.13 = (bf16[2,1,320,128]{3,2,1,0:T(8,128)(2,1)S(1)}, bf16[2,1,320,128]{3,2,1,0:T(8,128)(2,1)S(1)}, u32[]{:S(2)}, u32[]{:S(2)}) collective-permute-start(bf16[2,1,320,128]{3,2,1,0:T(8,128)(2,1)S(1)} %get-tuple-element.69), channel_id=1, source_target_pairs={{0,2},{1,3},{2,0},{3,1},{4,6},{5,7},{6,4},{7,5},{8,10},{9,11},{10,... | collective-permute-start | bytes 491528 | tf_op jit(solution)/shard_map/ppermute | solution.py:404
  11.5 12.6 %collective-permute-start.14 = (bf16[2,1,320,128]{3,2,1,0:T(8,128)(2,1)S(1)}, bf16[2,1,320,128]{3,2,1,0:T(8,128)(2,1)S(1)}, u32[]{:S(2)}, u32[]{:S(2)}) collective-permute-start(bf16[2,1,320,128]{3,2,1,0:T(8,128)(2,1)S(1)} %get-tuple-element.70), channel_id=1, source_target_pairs={{0,3},{1,2},{2,1},{3,0},{4,7},{5,6},{6,5},{7,4},{8,11},{9,10},{10,... | collective-permute-start | bytes 491528 | tf_op jit(solution)/shard_map/ppermute | solution.py:404
  14.5 20.5 %collective-permute-start.7 = (bf16[2,1,320,128]{3,2,1,0:T(8,128)(2,1)S(1)}, bf16[2,1,320,128]{3,2,1,0:T(8,128)(2,1)S(1)}, u32[]{:S(2)}, u32[]{:S(2)}) collective-permute-start(bf16[2,1,320,128]{3,2,1,0:T(8,128)(2,1)S(1)} %get-tuple-element.61), channel_id=1, source_target_pairs={{0,2},{1,3},{2,0},{3,1},{4,6},{5,7},{6,4},{7,5},{8,10},{9,11},{10,... | collective-permute-start | bytes 491528 | tf_op jit(solution)/shard_map/ppermute | solution.py:404
  17.1 17.9 %collective-permute-start.8 = (bf16[2,1,320,128]{3,2,1,0:T(8,128)(2,1)S(1)}, bf16[2,1,320,128]{3,2,1,0:T(8,128)(2,1)S(1)}, u32[]{:S(2)}, u32[]{:S(2)}) collective-permute-start(bf16[2,1,320,128]{3,2,1,0:T(8,128)(2,1)S(1)} %get-tuple-element.62), channel_id=1, source_target_pairs={{0,3},{1,2},{2,1},{3,0},{4,7},{5,6},{6,5},{7,4},{8,11},{9,10},{10,... | collective-permute-start | bytes 491528 | tf_op jit(solution)/shard_map/ppermute | solution.py:404
  19.0 20.8 %collective-permute-start.3 = (bf16[2,1,320,128]{3,2,1,0:T(8,128)(2,1)S(1)}, bf16[2,1,320,128]{3,2,1,0:T(8,128)(2,1)S(1)}, u32[]{:S(2)}, u32[]{:S(2)}) collective-permute-start(bf16[2,1,320,128]{3,2,1,0:T(8,128)(2,1)S(1)} %get-tuple-element.56), channel_id=1, source_target_pairs={{0,1},{1,0},{2,3},{3,2},{4,5},{5,4},{6,7},{7,6},{8,9},{9,8},{10,11... | collective-permute-start | bytes 491528 | tf_op jit(solution)/shard_map/ppermute | solution.py:404
  21.5 18.2 %collective-permute-start.4 = (bf16[2,1,320,128]{3,2,1,0:T(8,128)(2,1)S(1)}, bf16[2,1,320,128]{3,2,1,0:T(8,128)(2,1)S(1)}, u32[]{:S(2)}, u32[]{:S(2)}) collective-permute-start(bf16[2,1,320,128]{3,2,1,0:T(8,128)(2,1)S(1)} %get-tuple-element.57), channel_id=1, source_target_pairs={{0,2},{1,3},{2,0},{3,1},{4,6},{5,7},{6,4},{7,5},{8,10},{9,11},{10,... | collective-permute-start | bytes 491528 | tf_op jit(solution)/shard_map/ppermute | solution.py:404
  24.1 15.7 %collective-permute-start.5 = (bf16[2,1,320,128]{3,2,1,0:T(8,128)(2,1)S(1)}, bf16[2,1,320,128]{3,2,1,0:T(8,128)(2,1)S(1)}, u32[]{:S(2)}, u32[]{:S(2)}) collective-permute-start(bf16[2,1,320,128]{3,2,1,0:T(8,128)(2,1)S(1)} %get-tuple-element.58), channel_id=1, source_target_pairs={{0,3},{1,2},{2,1},{3,0},{4,7},{5,6},{6,5},{7,4},{8,11},{9,10},{10,... | collective-permute-start | bytes 491528 | tf_op jit(solution)/shard_map/ppermute | solution.py:404
  44.5 3.0 %collective-permute-start.17 = (bf16[512,512]{1,0:T(8,128)(2,1)S(1)}, bf16[512,512]{1,0:T(8,128)(2,1)S(1)}, u32[]{:S(2)}, u32[]{:S(2)}) collective-permute-start(bf16[512,512]{1,0:T(8,128)(2,1)S(1)} %get-tuple-element.81.hi_ref.hi_two), channel_id=1, source_target_pairs={{0,1},{2,3},{4,5},{6,7},{8,9},{10,11},{12,13},{14,15},{16,17},{18,... | collective-permute-start | bytes 1572872 | tf_op jit(solution)/shard_map/ppermute | solution.py:407
  46.0 2.9 %collective-permute-start.18 = (bf16[512,512]{1,0:T(8,128)(2,1)S(1)}, bf16[512,512]{1,0:T(8,128)(2,1)S(1)}, u32[]{:S(2)}, u32[]{:S(2)}) collective-permute-start(bf16[512,512]{1,0:T(8,128)(2,1)S(1)} %get-tuple-element.82.lo_ref.lo_two), channel_id=1, source_target_pairs={{0,1},{2,3},{4,5},{6,7},{8,9},{10,11},{12,13},{14,15},{16,17},{18,... | collective-permute-start | bytes 1572872 | tf_op jit(solution)/shard_map/ppermute | solution.py:407
  49.9 13.6 %collective-permute-start.23 = (bf16[512,512]{1,0:T(8,128)(2,1)S(1)}, bf16[512,512]{1,0:T(8,128)(2,1)S(1)}, u32[]{:S(2)}, u32[]{:S(2)}) collective-permute-start(bf16[512,512]{1,0:T(8,128)(2,1)S(1)} %get-tuple-element.83.hi_ref.refs_0_), channel_id=1, source_target_pairs={{9,11},{11,9},{13,15},{15,13},{17,19},{19,17},{21,23},{23,21},{25,... | collective-permute-start | bytes 1572872 | tf_op jit(solution)/shard_map/ppermute | solution.py:407
  50.6 12.9 %collective-permute-start.24 = (bf16[512,512]{1,0:T(8,128)(2,1)S(1)}, bf16[512,512]{1,0:T(8,128)(2,1)S(1)}, u32[]{:S(2)}, u32[]{:S(2)}) collective-permute-start(bf16[512,512]{1,0:T(8,128)(2,1)S(1)} %get-tuple-element.84.lo_ref.refs_1_), channel_id=1, source_target_pairs={{9,11},{11,9},{13,15},{15,13},{17,19},{19,17},{21,23},{23,21},{25,... | collective-permute-start | bytes 1572872 | tf_op jit(solution)/shard_map/ppermute | solution.py:407
  51.3 7.0 %collective-permute-start.15 = (f32[1,512]{1,0:T(1,128)S(1)}, f32[1,512]{1,0:T(1,128)S(1)}, u32[]{:S(2)}, u32[]{:S(2)}) collective-permute-start(f32[1,512]{1,0:T(1,128)S(1)} %get-tuple-element.80.vec_ref), channel_id=1, source_target_pairs={{0,1},{2,3},{4,5},{6,7},{8,9},{10,11},{12,13},{14,15},{16,17},{18,... | collective-permute-start | bytes 6152 | tf_op jit(solution)/shard_map/ppermute | solution.py:407
  58.5 0.7 collective-permute-start.16
  59.5 0.7 collective-permute-start.19
  60.4 1.3 %collective-permute-start.20 = (f32[1,512]{1,0:T(1,128)S(1)}, f32[1,512]{1,0:T(1,128)S(1)}, u32[]{:S(2)}, u32[]{:S(2)}) collective-permute-start(f32[1,512]{1,0:T(1,128)S(1)} %hop.6), channel_id=1, source_target_pairs={{5,7}} | collective-permute-start | bytes 6152 | tf_op jit(solution)/shard_map/ppermute | solution.py:407
  61.1 2.3 %collective-permute-start.25 = (f32[1,512]{1,0:T(1,128)S(1)}, f32[1,512]{1,0:T(1,128)S(1)}, u32[]{:S(2)}, u32[]{:S(2)}) collective-permute-start(f32[1,512]{1,0:T(1,128)S(1)} %hop.4.vec_ref.refs_2_), channel_id=1, source_target_pairs={{9,11},{11,9},{13,15},{15,13},{17,19},{19,17},{21,23},{23,21},{25,... | collective-permute-start | bytes 6152 | tf_op jit(solution)/shard_map/ppermute | solution.py:407
  62.1 1.4 %collective-permute-start.21 = (f32[1,512]{1,0:T(1,128)S(1)}, f32[1,512]{1,0:T(1,128)S(1)}, u32[]{:S(2)}, u32[]{:S(2)}) collective-permute-start(f32[1,512]{1,0:T(1,128)S(1)} %hop.7), channel_id=1, source_target_pairs={{7,9}} | collective-permute-start | bytes 6152 | tf_op jit(solution)/shard_map/ppermute | solution.py:407
  62.7 0.7 collective-permute-start.22
  64.0 0.7 collective-permute-start.26
  65.2 0.7 collective-permute-start.27
  69.6 19.7 %collective-permute-start.31 = (f32[1,512]{1,0:T(1,128)S(1)}, f32[1,512]{1,0:T(1,128)S(1)}, u32[]{:S(2)}, u32[]{:S(2)}) collective-permute-start(f32[1,512]{1,0:T(1,128)S(1)} %lead.1.refs_0_), channel_id=1, source_target_pairs={{1,0},{3,2},{5,4},{7,6},{9,8},{11,10},{13,12},{15,14},{17,16},{19,... | collective-permute-start | bytes 6152 | tf_op jit(solution)/shard_map/ppermute | solution.py:407
  90.9 3.5 %collective-permute-start.32 = (f32[8,128]{1,0:T(8,128)S(1)}, f32[8,128]{1,0:T(8,128)S(1)}, u32[]{:S(2)}, u32[]{:S(2)}) collective-permute-start(f32[8,128]{1,0:T(8,128)S(1)} %get-tuple-element.93), channel_id=1, source_target_pairs={{0,3},{1,2},{2,1},{3,0},{4,7},{5,6},{6,5},{7,4},{8,11},{9,10},{10,... | collective-permute-start | bytes 12296 | tf_op jit(solution)/shard_map/ppermute | solution.py:404
  93.1 3.6 %collective-permute-start.33 = (f32[8,128]{1,0:T(8,128)S(1)}, f32[8,128]{1,0:T(8,128)S(1)}, u32[]{:S(2)}, u32[]{:S(2)}) collective-permute-start(f32[8,128]{1,0:T(8,128)S(1)} %get-tuple-element.94), channel_id=1, source_target_pairs={{0,2},{1,3},{2,0},{3,1},{4,6},{5,7},{6,4},{7,5},{8,10},{9,11},{10,... | collective-permute-start | bytes 12296 | tf_op jit(solution)/shard_map/ppermute | solution.py:404
  93.1 3.6 %collective-permute-start.34 = (f32[8,128]{1,0:T(8,128)S(1)}, f32[8,128]{1,0:T(8,128)S(1)}, u32[]{:S(2)}, u32[]{:S(2)}) collective-permute-start(f32[8,128]{1,0:T(8,128)S(1)} %get-tuple-element.95), channel_id=1, source_target_pairs={{0,1},{1,0},{2,3},{3,2},{4,5},{5,4},{6,7},{7,6},{8,9},{9,8},{10,11... | collective-permute-start | bytes 12296 | tf_op jit(solution)/shard_map/ppermute | solution.py:404
  (14 other events, 96.4 us)
where the time goes:
time: 97.7 us; the launch traced here: 97.3 us
  starting transfers between devices  34.9 us (36%)
  waiting for transfers between devices  31.4 us (32%)
  Pallas kernels  27 us (28%)
  local copies, waits for them, and re-layouts  2.86 us (3%)
    ppermute x17, waiting for transfers between devices, send(): lax.ppermute(x, ('tm', 'state'), [(a * parts + b, c * parts + e) for (a,...  20.7 us
    ppermute x17, starting transfers between devices, send(): lax.ppermute(x, ('tm', 'state'), [(a * parts + b, c * parts + e) for (a,...  19 us
    pallas_call x4, Pallas kernels, chunk_piece(): pl.pallas_call(functools.partial(chunk_kernel, parts, pairs, bs, chunk, f...  18.4 us
    ppermute x18, starting transfers between devices, across(): return lax.ppermute(x, 'state', [(i, i ^ d) for i in range(parts)])  15.8 us
    ppermute x18, waiting for transfers between devices, across(): return lax.ppermute(x, 'state', [(i, i ^ d) for i in range(parts)])  10.7 us
    unnamed x22, local copies, waits for them, and re-layouts  2.86 us
    pallas_call x6, Pallas kernels, span_hop(): pl.pallas_call(functools.partial(span_kernel, leaders, whole, early), gri...  2.63 us
    pallas_call x4, Pallas kernels, pack(): pl.pallas_call(functools.partial(pack_kernel, parts, pairs, bs, chunk, bo...  2.23 us
  transfers between devices with their start and end apart: 35, of which 12 were waited for; matrix products, arithmetic and copies ran while one was open for 0% of the time, Pallas kernels for 17%

commit v1 on v0

--- a/solution.py
+++ b/solution.py
@@ -10,7 +10,7 @@
 
 BF = jnp.bfloat16
 F32 = jnp.float32
-VMEM_LIMIT = 8 * 1024 * 1024
+VMEM_LIMIT = 12 * 1024 * 1024
 ROWS = 16
 
 
@@ -34,6 +34,10 @@
     at = lax.broadcasted_iota(jnp.int32, (ROWS, row.shape[1]), 0)
     zero = jnp.zeros((), F32)
     return jnp.where(at == 0, hi, jnp.where(at == 1, mid, jnp.where(at == 2, low, zero))).astype(BF)
+
+
+def step_of(ns):
+    return 256 if ns % 256 == 0 else ns
 
 
 def turn(block, by):
@@ -104,14 +108,37 @@
     )(position, span, *([dyn_vals] * parts), *([gain] * parts), *table)
 
 
+def plan_kernel(parts, chunk, *refs):
+    small, blocks, counts, out_ref = refs[:parts], refs[parts], refs[parts + 1], refs[parts + 2]
+    steps = counts.shape[1]
+    each = small[0].shape[0] - chunk
+    for d in range(parts):
+        out_ref[d * each : (d + 1) * each, :] = small[d][chunk:, :steps].astype(jnp.int32)
+    out_ref[parts * each : parts * each + 2, :] = blocks[...]
+    out_ref[parts * each + 2 : parts * each + 3, :] = counts[...]
+
+
+def plan_of(small, blocks, counts, chunk):
+    parts = len(small)
+    each = small[0].shape[0] - chunk
+    return pl.pallas_call(
+        functools.partial(plan_kernel, parts, chunk),
+        in_specs=vmem(parts + 2),
+        out_specs=vmem(1)[0],
+        out_shape=jax.ShapeDtypeStruct((parts * each + 3, counts.shape[1]), jnp.int32),
+        compiler_params=pltpu.CompilerParams(vmem_limit_bytes=VMEM_LIMIT),
+        name="plan",
+    )(*small, blocks, counts)
+
+
 def chunk_kernel(
-    parts, pairs, bs, chunk, first, count, s_ref, tm_ref, blocks_ref, counts_ref, *refs
+    parts, pairs, bs, chunk, first, count, s_ref, tm_ref, plan_ref, *refs
 ):
-    cols, refs = refs[:parts], refs[parts:]
+    each = 6 * pairs
     data, small = refs[:parts], refs[parts : 2 * parts]
-    op_ref, values_ref, prior_ref, hi_in, lo_in, vec_in = refs[2 * parts : 2 * parts + 6]
-    elements, offsets, hi_ref, lo_ref, vec_ref = refs[2 * parts + 6 : 2 * parts + 11]
-    dyn, gains, source, chosen = refs[2 * parts + 11 :]
+    op_ref, values_ref, prior_ref, map_in, vec_in = refs[2 * parts : 2 * parts + 5]
+    elements, offsets, map_ref, vec_ref = refs[2 * parts + 5 : 2 * parts + 9]
+    dyn, gains, source, chosen = refs[2 * parts + 9 :]
     s = s_ref[0]
     ns = parts * pairs * 2 * bs
     lane = lax.broadcasted_iota(jnp.int32, (bs, 2 * bs), 1)
@@ -141,36 +168,45 @@
                     lefts = (both, both_turned, third if i == 0 else third_turned)
                     rights = (both_turned, both, third_turned if i == 0 else third)
                     row = pl.multiple_of(group * 2 * bs + i * bs, bs)
+                    placed = [jnp.where(left, both, zero) if i == 0 else jnp.where(left, zero, both_turned)]
+                    at = [group]
+                    for e in range(1, 3):
+                        column = plan_ref[d * each + e * 2 * pairs + 2 * q + i, k]
+                        at.append(column >> 1)
+                        placed.append(
+                            jnp.where(
+                                (column & 1) == 0,
+                                jnp.where(left, lefts[e], zero),
+                                jnp.where(left, zero, rights[e]),
+                            )
+                        )
                     for e in range(3):
-                        column = cols[d][chunk + e * 2 * pairs + 2 * q + i, k].astype(jnp.int32)
-                        side = column % 2
-                        value = jnp.where(
-                            side == 0,
-                            jnp.where(left, lefts[e], zero),
-                            jnp.where(left, zero, rights[e]),
-                        )
-                        dyn[side * tiles + column // 2, pl.ds(row, bs), :] = value
+                        value = placed[e]
+                        for f in range(3):
+                            if f != e:
+                                value = value + jnp.where(at[e] == at[f], placed[f], zero)
+                        dyn[at[e], pl.ds(row, bs), :] = value
         operator = op_ref[k].astype(F32)
         diagonal = jnp.concatenate(
             [jnp.where(left, operator, 0.0), jnp.where(left, 0.0, operator)], axis=0
         ).astype(BF)
         picks = []
         for o in range(2):
-            block = blocks_ref[o, k]
+            block = plan_ref[parts * each + o, k]
             for tile in range(tiles):
                 found = pl.ds(pl.multiple_of(block * bs, bs), bs)
                 chosen[o * bs : (o + 1) * bs, tile * 2 * bs : (tile + 1) * 2 * bs] = (
-                    dyn[tile, found, :] + dyn[tiles + tile, found, :]
+                    dyn[tile, found, :]
                 )
-            row = source[block // 2, pl.ds(here, 1), :]
+            row = source[block >> 1, pl.ds(here, 1), :]
             turned = pltpu.roll(row, bs, 1)
-            picks.append(jnp.where(block % 2 == o, row, turned))
+            picks.append(jnp.where((block & 1) == o, row, turned))
         image = tn(diagonal, chosen[...])
-        masked = jnp.where(slot < counts_ref[k], image, 0.0).astype(BF)
+        masked = jnp.where(slot < plan_ref[parts * each + 2, k], image, 0.0).astype(BF)
         pick = jnp.where(lane_row < bs, picks[0], picks[1])
         source_image = fold(nn(split3(pick), diagonal)).astype(BF).astype(F32)
         innovation = jnp.where(
-            lane_row < counts_ref[k], values_ref[pl.ds(k, 1), :] - source_image, 0.0
+            lane_row < plan_ref[parts * each + 2, k], values_ref[pl.ds(k, 1), :] - source_image, 0.0
         )
         shift = fold(nt(split3(innovation), gains[...]))
         shift = shift + jnp.concatenate(
@@ -182,58 +218,52 @@
             correction = nn(gains[rows, :], masked)
             for tile in range(tiles):
                 lanes = slice(tile * 2 * bs, (tile + 1) * 2 * bs)
-                forward = (dyn[tile, rows, :] + dyn[tiles + tile, rows, :]).astype(F32)
+                forward = dyn[tile, rows, :].astype(F32)
                 elements[j, rows, lanes] = (forward - correction[:, lanes]).astype(BF)
     if first == 0:
         begin = jnp.logical_and(s == 0, tm_ref[0] == 0)
         vec = jnp.where(begin, prior_ref[...], 0.0)
     else:
         vec = vec_in[...]
-    step_rows = 256 if ns % 256 == 0 else ns
     for j in range(count):
         element = elements[j]
         vec = fold(nt(split3(vec), element)) + offsets[j, 0:1, :]
-        for r in range(0, ns, step_rows):
-            rows = slice(r, r + step_rows)
+        held = map_in if j == 0 else map_ref
+        for r in range(0, ns, step_of(ns)):
+            rows, below = slice(r, r + step_of(ns)), slice(ns + r, ns + r + step_of(ns))
             if first == 0 and j == 0:
-                across = lax.broadcasted_iota(jnp.int32, (step_rows, ns), 1)
-                down = lax.broadcasted_iota(jnp.int32, (step_rows, ns), 0) + r
+                across = lax.broadcasted_iota(jnp.int32, (step_of(ns), ns), 1)
+                down = lax.broadcasted_iota(jnp.int32, (step_of(ns), ns), 0) + r
                 unit = jnp.where(across == down, 1.0, 0.0).astype(BF)
-                hi_ref[rows, :] = nt(unit, element).astype(BF)
-                lo_ref[rows, :] = jnp.zeros((step_rows, ns), BF)
+                map_ref[rows, :] = nt(unit, element).astype(BF)
                 continue
-            if j == 0:
-                hi, lo = hi_in[rows, :], lo_in[rows, :]
-            else:
-                hi, lo = hi_ref[rows, :], lo_ref[rows, :]
-            if first == 0 and j == 1:
-                moved = nt(hi, element)
-            else:
-                moved = nt(hi, element) + nt(lo, element)
+            moved = nt(held[rows, :], element)
+            if first > 0 or j > 1:
+                moved = moved + nt(held[below, :], element)
             top = moved.astype(BF)
-            hi_ref[rows, :] = top
-            lo_ref[rows, :] = (moved - top.astype(F32)).astype(BF)
+            map_ref[rows, :] = top
+            map_ref[below, :] = (moved - top.astype(F32)).astype(BF)
     vec_ref[...] = vec
 
 
 def chunk_piece(
-    position, span, blocks, counts, data, small, obs_op, obs_values, prior, state, chunk, first, count
+    position, span, plan, data, small, obs_op, obs_values, prior, state, chunk, first, count
 ):
     parts = len(data)
     pairs, _, width = data[0].shape[1:]
     bs = width // 2
     ns = parts * pairs * width
     if state is None:
-        state = (data[0], data[0], prior)
+        state = (data[0], prior)
     return pl.pallas_call(
         functools.partial(chunk_kernel, parts, pairs, bs, chunk, first, count),
         grid_spec=pltpu.PrefetchScalarGridSpec(
-            num_scalar_prefetch=4,
+            num_scalar_prefetch=3,
             grid=(),
-            in_specs=[pl.BlockSpec(memory_space=pltpu.SMEM)] * parts + vmem(2 * parts + 6),
-            out_specs=vmem(5),
+            in_specs=vmem(2 * parts + 5),
+            out_specs=vmem(4),
             scratch_shapes=[
-                pltpu.VMEM((2 * parts * pairs, ns, width), BF),
+                pltpu.VMEM((parts * pairs, ns, width), BF),
                 pltpu.VMEM((ns, width), BF),
                 pltpu.VMEM((parts * pairs, chunk, width), F32),
                 pltpu.VMEM((width, ns), BF),
@@ -242,70 +272,75 @@
         out_shape=[
             jax.ShapeDtypeStruct((count, ns, ns), BF),
             jax.ShapeDtypeStruct((count, 8, ns), F32),
-            jax.ShapeDtypeStruct((ns, ns), BF),
-            jax.ShapeDtypeStruct((ns, ns), BF),
+            jax.ShapeDtypeStruct((2 * ns, ns), BF),
             jax.ShapeDtypeStruct((1, ns), F32),
         ],
         compiler_params=pltpu.CompilerParams(vmem_limit_bytes=VMEM_LIMIT),
     )(
-        position, span, blocks, counts, *small, *data, *small, obs_op, obs_values, prior, *state,
+        position, span, plan, *data, *small, obs_op, obs_values, prior, *state,
     )
 
 
-def apply_map(row, hi, lo):
+def apply_map(row, held):
+    ns = held.shape[1]
     parts = split3(row)
-    return fold(nn(parts, hi) + nn(parts, lo))
-
-
-def join_kernel(hi_one, lo_one, hi_two, lo_two, hi_ref, lo_ref):
-    ns = hi_ref.shape[0]
-    step = 256 if ns % 256 == 0 else ns
-    for r in range(0, ns, step):
-        rows = slice(r, r + step)
-        product = nn(hi_one[rows, :], hi_two[...]) + (
-            nn(hi_one[rows, :], lo_two[...]) + nn(lo_one[rows, :], hi_two[...])
+    return fold(nn(parts, held[:ns, :]) + nn(parts, held[ns : 2 * ns, :]))
+
+
+def join_kernel(one, two, vec_ref, out_ref):
+    ns = one.shape[1]
+    for r in range(0, ns, step_of(ns)):
+        rows, below = slice(r, r + step_of(ns)), slice(ns + r, ns + r + step_of(ns))
+        product = nn(one[rows, :], two[:ns, :]) + (
+            nn(one[rows, :], two[ns : 2 * ns, :]) + nn(one[below, :], two[:ns, :])
         )
         top = product.astype(BF)
-        hi_ref[rows, :] = top
-        lo_ref[rows, :] = (product - top.astype(F32)).astype(BF)
-
-
-def join(one, two):
+        out_ref[rows, :] = top
+        out_ref[below, :] = (product - top.astype(F32)).astype(BF)
+    out_ref[2 * ns :, :] = split3(vec_ref[...])
+
+
+def join(one, two, vec):
+    ns = one.shape[1]
     return pl.pallas_call(
         join_kernel,
-        in_specs=vmem(4),
-        out_specs=vmem(2),
-        out_shape=[jax.ShapeDtypeStruct(x.shape, BF) for x in two],
+        in_specs=vmem(3),
+        out_specs=vmem(1)[0],
+        out_shape=jax.ShapeDtypeStruct((2 * ns + ROWS, ns), BF),
         compiler_params=pltpu.CompilerParams(vmem_limit_bytes=VMEM_LIMIT),
         name="join",
-    )(*one, *two)
-
-
-def hop_kernel(row_ref, hi_ref, lo_ref, vec_ref, out_ref):
-    out_ref[...] = apply_map(row_ref[...], hi_ref[...], lo_ref[...]) + vec_ref[...]
-
-
-def hop(row, hi, lo, vec):
+    )(one, two, vec)
+
+
+def hop_kernel(row_ref, *refs):
+    current, out_ref = row_ref[...], refs[-1]
+    for n in range(0, len(refs) - 1, 2):
+        current = apply_map(current, refs[n]) + refs[n + 1][...]
+    out_ref[...] = current
+
+
+def hop(row, *maps):
     return pl.pallas_call(
         hop_kernel,
-        in_specs=vmem(4),
+        in_specs=vmem(1 + len(maps)),
         out_specs=vmem(1)[0],
         out_shape=jax.ShapeDtypeStruct(row.shape, F32),
         compiler_params=pltpu.CompilerParams(vmem_limit_bytes=VMEM_LIMIT),
         name="hop",
-    )(row, hi, lo, vec)
+    )(row, *maps)
 
 
 def span_kernel(leaders, whole, early, s_ref, tm_ref, row_ref, direct_ref, *refs):
-    maps, out_ref = [refs[3 * n : 3 * n + 3] for n in range(leaders)], refs[3 * leaders]
+    maps, out_ref = refs[:leaders], refs[leaders]
+    ns = out_ref.shape[1]
     for mine in range(leaders):
 
         @pl.when(s_ref[0] // 2 == mine)
         def _():
             current = row_ref[...]
             for p in range(leaders if whole else mine):
-                hi, lo, vec = maps[p ^ mine]
-                current = apply_map(current, hi[...], lo[...]) + vec[...]
+                held = maps[p ^ mine]
+                current = apply_map(current, held) + fold(held[2 * ns :, :].astype(F32))
             if not whole:
                 current = jnp.where(tm_ref[0] < early, direct_ref[...], current)
             out_ref[...] = current
@@ -318,18 +353,18 @@
         grid_spec=pltpu.PrefetchScalarGridSpec(
             num_scalar_prefetch=2,
             grid=(),
-            in_specs=vmem(2 + 3 * leaders),
+            in_specs=vmem(2 + leaders),
             out_specs=vmem(1)[0],
         ),
         out_shape=jax.ShapeDtypeStruct(row.shape, F32),
         compiler_params=pltpu.CompilerParams(vmem_limit_bytes=VMEM_LIMIT),
         name="span_hop" if whole else "lead",
-    )(position, span, row, direct, *[m for trio in maps for m in trio])
+    )(position, span, row, direct, *maps)
 
 
 def sweep_kernel(pieces, parts, s_ref, tm_ref, *refs):
-    own_ref, told_ref, prior_ref, hi, lo, vec = refs[:6]
-    refs = refs[6:]
+    own_ref, told_ref, prior_ref, map_ref, vec_ref = refs[:5]
+    refs = refs[5:]
     elements, offsets = refs[:pieces], refs[pieces : 2 * pieces]
     outs = refs[2 * pieces : 2 * pieces + parts]
     current_ref, spread = refs[2 * pieces + parts :]
@@ -342,7 +377,7 @@
 
     @pl.when(s % 2 == 1)
     def _():
-        current_ref[...] = apply_map(own_ref[...], hi[...], lo[...]) + vec[...]
+        current_ref[...] = apply_map(own_ref[...], map_ref) + vec_ref[...]
 
     current = current_ref[...]
     at = 0
@@ -367,7 +402,7 @@
         grid_spec=pltpu.PrefetchScalarGridSpec(
             num_scalar_prefetch=2,
             grid=(),
-            in_specs=vmem(6 + 2 * pieces),
+            in_specs=vmem(5 + 2 * pieces),
             out_specs=vmem(parts),
             scratch_shapes=[
                 pltpu.VMEM((1, ns), F32),
@@ -380,12 +415,33 @@
     )(position, span, own, told, prior, *even, *elements, *offsets)
 
 
-PIECES = 4
+def gather_kernel(parts, s_ref, *refs):
+    blocks, out_ref = refs[:parts], refs[parts]
+    rows = blocks[0].shape[0]
+    for d in range(parts):
+        out_ref[pl.ds(pl.multiple_of((s_ref[0] ^ d) * rows, rows), rows), :] = blocks[d][...]
+
+
+def gather(position, blocks):
+    rows, width = blocks[0].shape
+    parts = len(blocks)
+    return pl.pallas_call(
+        functools.partial(gather_kernel, parts),
+        grid_spec=pltpu.PrefetchScalarGridSpec(
+            num_scalar_prefetch=1, grid=(), in_specs=vmem(parts), out_specs=vmem(1)[0]
+        ),
+        out_shape=jax.ShapeDtypeStruct((parts * rows, width), F32),
+        compiler_params=pltpu.CompilerParams(vmem_limit_bytes=VMEM_LIMIT),
+        name="gather",
+    )(position, *blocks)
+
+
+PIECES = 5
 
 
 def piece_sizes(chunk):
-    base, more = divmod(chunk, PIECES)
-    return [base + 1] * more + [base] * (PIECES - more)
+    base, more = divmod(chunk - 2, PIECES - 2)
+    return [base + 1] * more + [base] * (PIECES - 2 - more) + [1, 1]
 
 
 def means(dyn_cols, dyn_vals, obs_blocks, obs_op, obs_counts, obs_values, gain, sources, prior):
@@ -414,46 +470,43 @@
     pieces = []
     for n, (first, size) in enumerate(zip(firsts, sizes)):
         source_arrays = (vals_far, gain_far) if n == 0 else (dyn_vals, gain)
-        table = (sources, dyn_cols.transpose(2, 1, 0)) if n == 0 else ()
+        table = (sources, dyn_cols.transpose(2, 1, 0)) if n == 1 else ()
         packed = pack(position, span, *source_arrays, parts, chunk, first, size, table)
         arrived = {0: packed[0]}
         for d in order:
             arrived[d] = across(packed[d], d)
         pieces.append([arrived[d] for d in range(parts)])
-        if n == 0:
+        if n == 1:
             small = {0: packed[parts]}
             for d in order:
                 small[d] = across(packed[parts + d], d)
             small = [small[d] for d in range(parts)]
 
+    plan = plan_of(small, obs_blocks.T, obs_counts.reshape(1, steps), chunk)
     state = None
     elements, offsets = [], []
     for first, size, data in zip(firsts, sizes, pieces):
         element, offset, *state = chunk_piece(
-            position, span, obs_blocks.T, obs_counts, data, small, obs_op, obs_values,
+            position, span, plan, data, small, obs_op, obs_values,
             prior_row, state, chunk, first, size,
         )
         elements.append(element)
         offsets.append(offset)
-    hi, lo, vec = state
+    chunk_map, vec = state
 
     leads = [2 * p + 1 for p in range(parts // 2)]
     to_lead = [((a, l - 1), (a, l)) for a in range(spans) for l in leads]
     vec_even = send(vec, to_lead)
-    hi_even = send(hi, to_lead)
-    lo_even = send(lo, to_lead)
-    pair_vec = hop(vec_even, hi, lo, vec)
-    pair_hi, pair_lo = join((hi_even, lo_even), (hi, lo))
-    pair = (pair_hi, pair_lo, pair_vec)
+    map_even = send(chunk_map, to_lead)
+    both = (map_even, vec_even, chunk_map, vec)
+    pair_vec = hop(vec_even, chunk_map, vec)
+    pair = join(map_even, chunk_map, pair_vec)
 
     early = min(2, spans - 1)
     maps = [pair]
     for d in range(2, parts, 2):
         pairs = [((a, l), (a, l ^ d)) for a in range(early, spans) for l in leads]
-        far = []
-        for x in pair:
-            far.append(send(x, pairs))
-        maps.append(tuple(far))
+        maps.append(send(pair, pairs))
 
     direct = jnp.zeros((1, ns), F32)
     entry = jnp.zeros((1, ns), F32)
@@ -462,11 +515,11 @@
         for p in range(1, len(leads)):
             arriving = send(current, [((g, leads[p - 1]), (g, leads[p]))])
             direct = direct + arriving
-            current = hop(arriving, *pair)
+            current = hop(arriving, *both)
         if g + 1 < early:
             arriving = send(current, [((g, leads[-1]), (g + 1, leads[0]))])
             direct = direct + arriving
-            current = hop(arriving, *pair)
+            current = hop(arriving, *both)
         else:
             for l in leads:
                 entry = entry + send(current, [((g, leads[-1]), (g + 1, l))])
@@ -480,15 +533,12 @@
     own = span_hop(position, span, entry, direct, maps, False, early)
     told = send(own, [(b, a) for a, b in to_lead])
     mine = sweep(
-        position, span, own, told, prior_row, (hi_even, lo_even, vec_even), elements, offsets, parts
+        position, span, own, told, prior_row, (map_even, vec_even), elements, offsets, parts
     )
-    got = [mine[0]] + [across(mine[d], d) for d in range(1, parts)]
-    bit = 1
-    while bit < parts:
-        swapped = [got[d ^ bit] for d in range(parts)]
-        got = [jnp.where((s & bit) != 0, b, a) for a, b in zip(got, swapped)]
-        bit *= 2
-    return jnp.concatenate(got, axis=0)
+    got = {0: mine[0]}
+    for d in order:
+        got[d] = across(mine[d], d)
+    return gather(position, [got[d] for d in range(parts)])
 
 
 def solution(mesh):

time: 97.7 us -> 99.3 us (1.016)
  the two profiles are of different devices: /device:TPU:26 before, /device:TPU:27 now
where the time goes in v1:
time: 99.3 us; the launch traced here: 98.9 us
  waiting for transfers between devices  41.6 us (42%)
  starting transfers between devices  31.6 us (32%)
  Pallas kernels  25.2 us (25%)
    ppermute x14, waiting for transfers between devices, send(): lax.ppermute(x, ('tm', 'state'), [(a * parts + b, c * parts + e) for (a,...  23.1 us
    ppermute x21, waiting for transfers between devices, across(): return lax.ppermute(x, 'state', [(i, i ^ d) for i in range(parts)])  18.5 us
    ppermute x21, starting transfers between devices, across(): return lax.ppermute(x, 'state', [(i, i ^ d) for i in range(parts)])  17.6 us
    pallas_call x5, Pallas kernels, chunk_piece(): pl.pallas_call(functools.partial(chunk_kernel, parts, pairs, bs, chunk, f...  15.1 us
    ppermute x14, starting transfers between devices, send(): lax.ppermute(x, ('tm', 'state'), [(a * parts + b, c * parts + e) for (a,...  13.9 us
    pallas_call x6, Pallas kernels, span_hop(): pl.pallas_call(functools.partial(span_kernel, leaders, whole, early), gri...  2.61 us
    pallas_call x5, Pallas kernels, pack(): pl.pallas_call(functools.partial(pack_kernel, parts, pairs, bs, chunk, bo...  2.16 us
  transfers between devices with their start and end apart: 35, of which 14 were waited for; matrix products, arithmetic and copies ran while one was open for 0% of the time, Pallas kernels for 15%

profile of v1, /device:TPU:27, one launch (start us, length us, event | category | flops | bytes accessed | tf_op | source)
XLA Modules:
  0.0 98.9 jit_solution(16403556420953284724)
XLA Ops:
  0.0 1.5 %shard_map.95 = (bf16[2,1,320,128]{3,2,1,0:T(8,128)(2,1)S(1)}, bf16[2,1,320,128]{3,2,1,0:T(8,128)(2,1)S(1)}, bf16[2,1,320,128]{3,2,1,0:T(8,128)(2,1)S(1)}, bf16[2,1,320,128]{3,2,1,0:T(8,128)(2,1)S(1)}) custom-call(s32[1]{0:T(128)} %bitcast.s_ref, s32[1]{0:T(128)} %bitcast.1.tm_ref, bf16[32,2,64,192]{3,2,1,0:T(8,128)(2,1)} %refs_3_.9, ...), custom_call_target="tpu_custom_call" | custom-call | tf_op jit(solution)/shard_map/pallas_call | solution.py:95
  2.2 1.2 %collective-permute-start.16 = (bf16[2,1,320,128]{3,2,1,0:T(8,128)(2,1)S(1)}, bf16[2,1,320,128]{3,2,1,0:T(8,128)(2,1)S(1)}, u32[]{:S(2)}, u32[]{:S(2)}) collective-permute-start(bf16[2,1,320,128]{3,2,1,0:T(8,128)(2,1)S(1)} %get-tuple-element.75), channel_id=1, source_target_pairs={{0,2},{1,3},{2,0},{3,1},{4,6},{5,7},{6,4},{7,5},{8,10},{9,11},{10,... | collective-permute-start | bytes 491528 | tf_op jit(solution)/shard_map/ppermute | solution.py:460
  5.9 1.2 %collective-permute-start.1 = (f32[14,128]{1,0:T(8,128)S(1)}, f32[14,128]{1,0:T(8,128)S(1)}, u32[]{:S(2)}, u32[]{:S(2)}) collective-permute-start(f32[14,128]{1,0:T(8,128)S(1)} %get-tuple-element.55), channel_id=1, source_target_pairs={{0,2},{1,3},{2,0},{3,1},{4,6},{5,7},{6,4},{7,5},{8,10},{9,11},{10,... | collective-permute-start | bytes 21512 | tf_op jit(solution)/shard_map/ppermute | solution.py:460
  7.2 4.3 %collective-permute-done.1.refs_2_.refs_6_ = f32[14,128]{1,0:T(8,128)S(1)} collective-permute-done((f32[14,128]{1,0:T(8,128)S(1)}, f32[14,128]{1,0:T(8,128)S(1)}, u32[]{:S(2)}, u32[]{:S(2)}) %collective-permute-start.1) | collective-permute-done | bytes 7200 | tf_op jit(solution)/shard_map/ppermute | solution.py:460
  11.4 2.2 %collective-permute-start.2 = (f32[14,128]{1,0:T(8,128)S(1)}, f32[14,128]{1,0:T(8,128)S(1)}, u32[]{:S(2)}, u32[]{:S(2)}) collective-permute-start(f32[14,128]{1,0:T(8,128)S(1)} %get-tuple-element.56), channel_id=1, source_target_pairs={{0,3},{1,2},{2,1},{3,0},{4,7},{5,6},{6,5},{7,4},{8,11},{9,10},{10,... | collective-permute-start | bytes 21512 | tf_op jit(solution)/shard_map/ppermute | solution.py:460
  13.8 1.5 %collective-permute-done.2.refs_3_.refs_7_ = f32[14,128]{1,0:T(8,128)S(1)} collective-permute-done((f32[14,128]{1,0:T(8,128)S(1)}, f32[14,128]{1,0:T(8,128)S(1)}, u32[]{:S(2)}, u32[]{:S(2)}) %collective-permute-start.2) | collective-permute-done | bytes 7200 | tf_op jit(solution)/shard_map/ppermute | solution.py:460
  15.6 0.9 collective-permute-done.6.refs_1_
  16.6 1.2 %collective-permute-start.10 = (bf16[2,1,320,128]{3,2,1,0:T(8,128)(2,1)S(1)}, bf16[2,1,320,128]{3,2,1,0:T(8,128)(2,1)S(1)}, u32[]{:S(2)}, u32[]{:S(2)}) collective-permute-start(bf16[2,1,320,128]{3,2,1,0:T(8,128)(2,1)S(1)} %get-tuple-element.67), channel_id=1, source_target_pairs={{0,2},{1,3},{2,0},{3,1},{4,6},{5,7},{6,4},{7,5},{8,10},{9,11},{10,... | collective-permute-start | bytes 491528 | tf_op jit(solution)/shard_map/ppermute | solution.py:460
  18.6 1.3 %collective-permute-start.13 = (bf16[2,1,320,128]{3,2,1,0:T(8,128)(2,1)S(1)}, bf16[2,1,320,128]{3,2,1,0:T(8,128)(2,1)S(1)}, u32[]{:S(2)}, u32[]{:S(2)}) collective-permute-start(bf16[2,1,320,128]{3,2,1,0:T(8,128)(2,1)S(1)} %get-tuple-element.71), channel_id=1, source_target_pairs={{0,2},{1,3},{2,0},{3,1},{4,6},{5,7},{6,4},{7,5},{8,10},{9,11},{10,... | collective-permute-start | bytes 491528 | tf_op jit(solution)/shard_map/ppermute | solution.py:460
  20.9 1.1 %collective-permute-done.10.refs_2_ = bf16[2,1,320,128]{3,2,1,0:T(8,128)(2,1)S(1)} collective-permute-done((bf16[2,1,320,128]{3,2,1,0:T(8,128)(2,1)S(1)}, bf16[2,1,320,128]{3,2,1,0:T(8,128)(2,1)S(1)}, u32[]{:S(2)}, u32[]{:S(2)}) %collective-permute-start.10) | collective-permute-done | bytes 163872 | tf_op jit(solution)/shard_map/ppermute | solution.py:460
  22.0 1.2 %collective-permute-start.7 = (bf16[1,1,320,128]{3,2,1,0:T(8,128)(2,1)S(1)}, bf16[1,1,320,128]{3,2,1,0:T(8,128)(2,1)S(1)}, u32[]{:S(2)}, u32[]{:S(2)}) collective-permute-start(bf16[1,1,320,128]{3,2,1,0:T(8,128)(2,1)S(1)} %get-tuple-element.63), channel_id=1, source_target_pairs={{0,2},{1,3},{2,0},{3,1},{4,6},{5,7},{6,4},{7,5},{8,10},{9,11},{10,... | collective-permute-start | bytes 245768 | tf_op jit(solution)/shard_map/ppermute | solution.py:460
  23.2 3.6 %collective-permute-done.11.refs_3_ = bf16[2,1,320,128]{3,2,1,0:T(8,128)(2,1)S(1)} collective-permute-done((bf16[2,1,320,128]{3,2,1,0:T(8,128)(2,1)S(1)}, bf16[2,1,320,128]{3,2,1,0:T(8,128)(2,1)S(1)}, u32[]{:S(2)}, u32[]{:S(2)}) %collective-permute-start.11) | collective-permute-done | bytes 163872 | tf_op jit(solution)/shard_map/ppermute | solution.py:460
  27.0 1.4 %collective-permute-start.3 = (bf16[1,1,320,128]{3,2,1,0:T(8,128)(2,1)S(1)}, bf16[1,1,320,128]{3,2,1,0:T(8,128)(2,1)S(1)}, u32[]{:S(2)}, u32[]{:S(2)}) collective-permute-start(bf16[1,1,320,128]{3,2,1,0:T(8,128)(2,1)S(1)} %get-tuple-element.58), channel_id=1, source_target_pairs={{0,1},{1,0},{2,3},{3,2},{4,5},{5,4},{6,7},{7,6},{8,9},{9,8},{10,11... | collective-permute-start | bytes 245768 | tf_op jit(solution)/shard_map/ppermute | solution.py:460
  29.0 1.2 %collective-permute-start.4 = (bf16[1,1,320,128]{3,2,1,0:T(8,128)(2,1)S(1)}, bf16[1,1,320,128]{3,2,1,0:T(8,128)(2,1)S(1)}, u32[]{:S(2)}, u32[]{:S(2)}) collective-permute-start(bf16[1,1,320,128]{3,2,1,0:T(8,128)(2,1)S(1)} %get-tuple-element.59), channel_id=1, source_target_pairs={{0,2},{1,3},{2,0},{3,1},{4,6},{5,7},{6,4},{7,5},{8,10},{9,11},{10,... | collective-permute-start | bytes 245768 | tf_op jit(solution)/shard_map/ppermute | solution.py:460
  30.2 3.6 %collective-permute-done.14.refs_3_ = bf16[2,1,320,128]{3,2,1,0:T(8,128)(2,1)S(1)} collective-permute-done((bf16[2,1,320,128]{3,2,1,0:T(8,128)(2,1)S(1)}, bf16[2,1,320,128]{3,2,1,0:T(8,128)(2,1)S(1)}, u32[]{:S(2)}, u32[]{:S(2)}) %collective-permute-start.14) | collective-permute-done | bytes 163872 | tf_op jit(solution)/shard_map/ppermute | solution.py:460
  34.0 3.0 %shard_map.96 = (bf16[2,512,512]{2,1,0:T(8,128)(2,1)S(1)}, f32[2,8,512]{2,1,0:T(8,128)S(1)}, bf16[1024,512]{1,0:T(8,128)(2,1)S(1)}, f32[1,512]{1,0:T(1,128)S(1)}) custom-call(s32[1]{0:T(128)} %bitcast.s_ref, s32[1]{0:T(128)} %bitcast.1.tm_ref, s32[27,32]{1,0:T(8,128)S(1)} %plan.1.plan_ref, bf16[2,1,320,128]{3,2,1,0:T(8,128)(2,1)S(1)} %get-tuple-element.73.refs_0_.refs_11_, ...), custom_call_target="tpu_custom_call" | custom-call | tf_op jit(solution)/shard_map/pallas_call | solution.py:258
  37.1 3.6 %shard_map.97 = (bf16[2,512,512]{2,1,0:T(8,128)(2,1)S(1)}, f32[2,8,512]{2,1,0:T(8,128)S(1)}, bf16[1024,512]{1,0:T(8,128)(2,1)S(1)}, f32[1,512]{1,0:T(1,128)S(1)}) custom-call(s32[1]{0:T(128)} %bitcast.s_ref, s32[1]{0:T(128)} %bitcast.1.tm_ref, s32[27,32]{1,0:T(8,128)S(1)} %plan.1.plan_ref, bf16[2,1,320,128]{3,2,1,0:T(8,128)(2,1)S(1)} %get-tuple-element.69.refs_0_, ...), custom_call_target="tpu_custom_call" | custom-call | tf_op jit(solution)/shard_map/pallas_call | solution.py:258
  40.7 3.6 %shard_map.98 = (bf16[2,512,512]{2,1,0:T(8,128)(2,1)S(1)}, f32[2,8,512]{2,1,0:T(8,128)S(1)}, bf16[1024,512]{1,0:T(8,128)(2,1)S(1)}, f32[1,512]{1,0:T(1,128)S(1)}) custom-call(s32[1]{0:T(128)} %bitcast.s_ref, s32[1]{0:T(128)} %bitcast.1.tm_ref, s32[27,32]{1,0:T(8,128)S(1)} %plan.1.plan_ref, bf16[2,1,320,128]{3,2,1,0:T(8,128)(2,1)S(1)} %get-tuple-element.65.refs_0_, ...), custom_call_target="tpu_custom_call" | custom-call | tf_op jit(solution)/shard_map/pallas_call | solution.py:258
  44.4 2.4 %shard_map.99 = (bf16[1,512,512]{2,1,0:T(8,128)(2,1)S(1)}, f32[1,8,512]{2,1,0:T(8,128)S(1)}, bf16[1024,512]{1,0:T(8,128)(2,1)S(1)}, f32[1,512]{1,0:T(1,128)S(1)}) custom-call(s32[1]{0:T(128)} %bitcast.s_ref, s32[1]{0:T(128)} %bitcast.1.tm_ref, s32[27,32]{1,0:T(8,128)S(1)} %plan.1.plan_ref, bf16[1,1,320,128]{3,2,1,0:T(8,128)(2,1)S(1)} %get-tuple-element.61.refs_0_, ...), custom_call_target="tpu_custom_call" | custom-call | tf_op jit(solution)/shard_map/pallas_call | solution.py:258
  46.8 2.4 %shard_map.100 = (bf16[1,512,512]{2,1,0:T(8,128)(2,1)S(1)}, f32[1,8,512]{2,1,0:T(8,128)S(1)}, bf16[1024,512]{1,0:T(8,128)(2,1)S(1)}, f32[1,512]{1,0:T(1,128)S(1)}) custom-call(s32[1]{0:T(128)} %bitcast.s_ref, s32[1]{0:T(128)} %bitcast.1.tm_ref, s32[27,32]{1,0:T(8,128)S(1)} %plan.1.plan_ref, bf16[1,1,320,128]{3,2,1,0:T(8,128)(2,1)S(1)} %get-tuple-element.57.refs_0_, ...), custom_call_target="tpu_custom_call" | custom-call | tf_op jit(solution)/shard_map/pallas_call | solution.py:258
  49.3 1.3 %collective-permute-start.20 = (bf16[1024,512]{1,0:T(8,128)(2,1)S(1)}, bf16[1024,512]{1,0:T(8,128)(2,1)S(1)}, u32[]{:S(2)}, u32[]{:S(2)}) collective-permute-start(bf16[1024,512]{1,0:T(8,128)(2,1)S(1)} %get-tuple-element.86.refs_0_.refs_2_.two), channel_id=1, source_target_pairs={{0,1},{2,3},{4,5},{6,7},{8,9},{10,11},{12,13},{14,15},{16,17},{18,... | collective-permute-start | bytes 3145736 | tf_op jit(solution)/shard_map/ppermute | solution.py:463
  50.6 1.3 %collective-permute-start.18 = (f32[1,512]{1,0:T(1,128)S(1)}, f32[1,512]{1,0:T(1,128)S(1)}, u32[]{:S(2)}, u32[]{:S(2)}) collective-permute-start(f32[1,512]{1,0:T(1,128)S(1)} %get-tuple-element.85.refs_1_.refs_3_), channel_id=1, source_target_pairs={{0,1},{2,3},{4,5},{6,7},{8,9},{10,11},{12,13},{14,15},{16,17},{18,... | collective-permute-start | bytes 6152 | tf_op jit(solution)/shard_map/ppermute | solution.py:463
  51.9 2.3 %collective-permute-done.18.row_ref.refs_1_.refs_4_ = f32[1,512]{1,0:T(1,128)S(1)} collective-permute-done((f32[1,512]{1,0:T(1,128)S(1)}, f32[1,512]{1,0:T(1,128)S(1)}, u32[]{:S(2)}, u32[]{:S(2)}) %collective-permute-start.18) | collective-permute-done | bytes 2080 | tf_op jit(solution)/shard_map/ppermute | solution.py:463
  54.4 1.0 join.1.refs_0_
  55.4 2.6 %collective-permute-start.25 = (bf16[1040,512]{1,0:T(8,128)(2,1)S(1)}, bf16[1040,512]{1,0:T(8,128)(2,1)S(1)}, u32[]{:S(2)}, u32[]{:S(2)}) collective-permute-start(bf16[1040,512]{1,0:T(8,128)(2,1)S(1)} %join.1.refs_0_), channel_id=1, source_target_pairs={{9,11},{11,9},{13,15},{15,13},{17,19},{19,17},{21,23},{23,21},{25,... | collective-permute-start | bytes 3194888 | tf_op jit(solution)/shard_map/ppermute | solution.py:463
  63.2 7.9 %collective-permute-done.25.refs_1_ = bf16[1040,512]{1,0:T(8,128)(2,1)S(1)} collective-permute-done((bf16[1040,512]{1,0:T(8,128)(2,1)S(1)}, bf16[1040,512]{1,0:T(8,128)(2,1)S(1)}, u32[]{:S(2)}, u32[]{:S(2)}) %collective-permute-start.25) | collective-permute-done | bytes 1064992 | tf_op jit(solution)/shard_map/ppermute | solution.py:463
  76.5 1.3 %collective-permute-start.30 = (f32[1,512]{1,0:T(1,128)S(1)}, f32[1,512]{1,0:T(1,128)S(1)}, u32[]{:S(2)}, u32[]{:S(2)}) collective-permute-start(f32[1,512]{1,0:T(1,128)S(1)} %span_hop.9), channel_id=1, source_target_pairs={{25,29},{27,31}} | collective-permute-start | bytes 6152 | tf_op jit(solution)/shard_map/ppermute | solution.py:463
  77.8 12.1 %collective-permute-done.30 = f32[1,512]{1,0:T(1,128)S(1)} collective-permute-done((f32[1,512]{1,0:T(1,128)S(1)}, f32[1,512]{1,0:T(1,128)S(1)}, u32[]{:S(2)}, u32[]{:S(2)}) %collective-permute-start.30) | collective-permute-done | bytes 2080 | tf_op jit(solution)/shard_map/ppermute | solution.py:463
  89.9 1.3 %collective-permute-start.31 = (f32[1,512]{1,0:T(1,128)S(1)}, f32[1,512]{1,0:T(1,128)S(1)}, u32[]{:S(2)}, u32[]{:S(2)}) collective-permute-start(f32[1,512]{1,0:T(1,128)S(1)} %lead.1.refs_0_), channel_id=1, source_target_pairs={{1,0},{3,2},{5,4},{7,6},{9,8},{11,10},{13,12},{15,14},{17,16},{19,... | collective-permute-start | bytes 6152 | tf_op jit(solution)/shard_map/ppermute | solution.py:463
  92.0 1.9 %sweep.1 = (f32[8,128]{1,0:T(8,128)S(1)}, f32[8,128]{1,0:T(8,128)S(1)}, f32[8,128]{1,0:T(8,128)S(1)}, f32[8,128]{1,0:T(8,128)S(1)}) custom-call(s32[1]{0:T(128)} %bitcast.s_ref, s32[1]{0:T(128)} %bitcast.1.tm_ref, f32[1,512]{1,0:T(1,128)S(1)} %lead.1.refs_0_, f32[1,512]{1,0:T(1,128)S(1)} %collective-permute-done.31.refs_1_, f32[1,512]{1,0:T(1,128)S(1)} %bitcast.12, ...), custom_call_target="tpu_custom_call" | custom-call | tf_op jit(solution)/shard_map/sweep/pallas_call | solution.py:400
  94.9 1.2 %collective-permute-start.34 = (f32[8,128]{1,0:T(8,128)S(1)}, f32[8,128]{1,0:T(8,128)S(1)}, u32[]{:S(2)}, u32[]{:S(2)}) collective-permute-start(f32[8,128]{1,0:T(8,128)S(1)} %get-tuple-element.100), channel_id=1, source_target_pairs={{0,3},{1,2},{2,1},{3,0},{4,7},{5,6},{6,5},{7,4},{8,11},{9,10},{10,... | collective-permute-start | bytes 12296 | tf_op jit(solution)/shard_map/ppermute | solution.py:460
  96.5 1.7 %collective-permute-done.34.refs_3_ = f32[8,128]{1,0:T(8,128)S(1)} collective-permute-done((f32[8,128]{1,0:T(8,128)S(1)}, f32[8,128]{1,0:T(8,128)S(1)}, u32[]{:S(2)}, u32[]{:S(2)}) %collective-permute-start.34) | collective-permute-done | bytes 4128 | tf_op jit(solution)/shard_map/ppermute | solution.py:460
  (83 shorter events, 19.7 us)
Async XLA Ops:
  1.5 16.3 %collective-permute-start.15 = (bf16[2,1,320,128]{3,2,1,0:T(8,128)(2,1)S(1)}, bf16[2,1,320,128]{3,2,1,0:T(8,128)(2,1)S(1)}, u32[]{:S(2)}, u32[]{:S(2)}) collective-permute-start(bf16[2,1,320,128]{3,2,1,0:T(8,128)(2,1)S(1)} %get-tuple-element.74), channel_id=1, source_target_pairs={{0,1},{1,0},{2,3},{3,2},{4,5},{5,4},{6,7},{7,6},{8,9},{9,8},{10,11... | collective-permute-start | bytes 491528 | tf_op jit(solution)/shard_map/ppermute | solution.py:460
  2.2 16.3 %collective-permute-start.16 = (bf16[2,1,320,128]{3,2,1,0:T(8,128)(2,1)S(1)}, bf16[2,1,320,128]{3,2,1,0:T(8,128)(2,1)S(1)}, u32[]{:S(2)}, u32[]{:S(2)}) collective-permute-start(bf16[2,1,320,128]{3,2,1,0:T(8,128)(2,1)S(1)} %get-tuple-element.75), channel_id=1, source_target_pairs={{0,2},{1,3},{2,0},{3,1},{4,6},{5,7},{6,4},{7,5},{8,10},{9,11},{10,... | collective-permute-start | bytes 491528 | tf_op jit(solution)/shard_map/ppermute | solution.py:460
  3.5 15.1 %collective-permute-start.17 = (bf16[2,1,320,128]{3,2,1,0:T(8,128)(2,1)S(1)}, bf16[2,1,320,128]{3,2,1,0:T(8,128)(2,1)S(1)}, u32[]{:S(2)}, u32[]{:S(2)}) collective-permute-start(bf16[2,1,320,128]{3,2,1,0:T(8,128)(2,1)S(1)} %get-tuple-element.76), channel_id=1, source_target_pairs={{0,3},{1,2},{2,1},{3,0},{4,7},{5,6},{6,5},{7,4},{8,11},{9,10},{10,... | collective-permute-start | bytes 491528 | tf_op jit(solution)/shard_map/ppermute | solution.py:460
  4.2 15.7 %collective-permute-start.9 = (bf16[2,1,320,128]{3,2,1,0:T(8,128)(2,1)S(1)}, bf16[2,1,320,128]{3,2,1,0:T(8,128)(2,1)S(1)}, u32[]{:S(2)}, u32[]{:S(2)}) collective-permute-start(bf16[2,1,320,128]{3,2,1,0:T(8,128)(2,1)S(1)} %get-tuple-element.66), channel_id=1, source_target_pairs={{0,1},{1,0},{2,3},{3,2},{4,5},{5,4},{6,7},{7,6},{8,9},{9,8},{10,11... | collective-permute-start | bytes 491528 | tf_op jit(solution)/shard_map/ppermute | solution.py:460
  4.7 1.3 %collective-permute-start = (f32[14,128]{1,0:T(8,128)S(1)}, f32[14,128]{1,0:T(8,128)S(1)}, u32[]{:S(2)}, u32[]{:S(2)}) collective-permute-start(f32[14,128]{1,0:T(8,128)S(1)} %get-tuple-element.54), channel_id=1, source_target_pairs={{0,1},{1,0},{2,3},{3,2},{4,5},{5,4},{6,7},{7,6},{8,9},{9,8},{10,11... | collective-permute-start | bytes 21512 | tf_op jit(solution)/shard_map/ppermute | solution.py:460
  5.9 5.5 %collective-permute-start.1 = (f32[14,128]{1,0:T(8,128)S(1)}, f32[14,128]{1,0:T(8,128)S(1)}, u32[]{:S(2)}, u32[]{:S(2)}) collective-permute-start(f32[14,128]{1,0:T(8,128)S(1)} %get-tuple-element.55), channel_id=1, source_target_pairs={{0,2},{1,3},{2,0},{3,1},{4,6},{5,7},{6,4},{7,5},{8,10},{9,11},{10,... | collective-permute-start | bytes 21512 | tf_op jit(solution)/shard_map/ppermute | solution.py:460
  11.4 3.8 %collective-permute-start.2 = (f32[14,128]{1,0:T(8,128)S(1)}, f32[14,128]{1,0:T(8,128)S(1)}, u32[]{:S(2)}, u32[]{:S(2)}) collective-permute-start(f32[14,128]{1,0:T(8,128)S(1)} %get-tuple-element.56), channel_id=1, source_target_pairs={{0,3},{1,2},{2,1},{3,0},{4,7},{5,6},{6,5},{7,4},{8,11},{9,10},{10,... | collective-permute-start | bytes 21512 | tf_op jit(solution)/shard_map/ppermute | solution.py:460
  15.2 1.3 %collective-permute-start.6 = (bf16[1,1,320,128]{3,2,1,0:T(8,128)(2,1)S(1)}, bf16[1,1,320,128]{3,2,1,0:T(8,128)(2,1)S(1)}, u32[]{:S(2)}, u32[]{:S(2)}) collective-permute-start(bf16[1,1,320,128]{3,2,1,0:T(8,128)(2,1)S(1)} %get-tuple-element.62), channel_id=1, source_target_pairs={{0,1},{1,0},{2,3},{3,2},{4,5},{5,4},{6,7},{7,6},{8,9},{9,8},{10,11... | collective-permute-start | bytes 245768 | tf_op jit(solution)/shard_map/ppermute | solution.py:460
  16.6 5.4 %collective-permute-start.10 = (bf16[2,1,320,128]{3,2,1,0:T(8,128)(2,1)S(1)}, bf16[2,1,320,128]{3,2,1,0:T(8,128)(2,1)S(1)}, u32[]{:S(2)}, u32[]{:S(2)}) collective-permute-start(bf16[2,1,320,128]{3,2,1,0:T(8,128)(2,1)S(1)} %get-tuple-element.67), channel_id=1, source_target_pairs={{0,2},{1,3},{2,0},{3,1},{4,6},{5,7},{6,4},{7,5},{8,10},{9,11},{10,... | collective-permute-start | bytes 491528 | tf_op jit(solution)/shard_map/ppermute | solution.py:460
  17.8 9.0 %collective-permute-start.11 = (bf16[2,1,320,128]{3,2,1,0:T(8,128)(2,1)S(1)}, bf16[2,1,320,128]{3,2,1,0:T(8,128)(2,1)S(1)}, u32[]{:S(2)}, u32[]{:S(2)}) collective-permute-start(bf16[2,1,320,128]{3,2,1,0:T(8,128)(2,1)S(1)} %get-tuple-element.68), channel_id=1, source_target_pairs={{0,3},{1,2},{2,1},{3,0},{4,7},{5,6},{6,5},{7,4},{8,11},{9,10},{10,... | collective-permute-start | bytes 491528 | tf_op jit(solution)/shard_map/ppermute | solution.py:460
  18.6 8.4 %collective-permute-start.12 = (bf16[2,1,320,128]{3,2,1,0:T(8,128)(2,1)S(1)}, bf16[2,1,320,128]{3,2,1,0:T(8,128)(2,1)S(1)}, u32[]{:S(2)}, u32[]{:S(2)}) collective-permute-start(bf16[2,1,320,128]{3,2,1,0:T(8,128)(2,1)S(1)} %get-tuple-element.70), channel_id=1, source_target_pairs={{0,1},{1,0},{2,3},{3,2},{4,5},{5,4},{6,7},{7,6},{8,9},{9,8},{10,11... | collective-permute-start | bytes 491528 | tf_op jit(solution)/shard_map/ppermute | solution.py:460
  18.6 10.4 %collective-permute-start.13 = (bf16[2,1,320,128]{3,2,1,0:T(8,128)(2,1)S(1)}, bf16[2,1,320,128]{3,2,1,0:T(8,128)(2,1)S(1)}, u32[]{:S(2)}, u32[]{:S(2)}) collective-permute-start(bf16[2,1,320,128]{3,2,1,0:T(8,128)(2,1)S(1)} %get-tuple-element.71), channel_id=1, source_target_pairs={{0,2},{1,3},{2,0},{3,1},{4,6},{5,7},{6,4},{7,5},{8,10},{9,11},{10,... | collective-permute-start | bytes 491528 | tf_op jit(solution)/shard_map/ppermute | solution.py:460
  19.9 13.9 %collective-permute-start.14 = (bf16[2,1,320,128]{3,2,1,0:T(8,128)(2,1)S(1)}, bf16[2,1,320,128]{3,2,1,0:T(8,128)(2,1)S(1)}, u32[]{:S(2)}, u32[]{:S(2)}) collective-permute-start(bf16[2,1,320,128]{3,2,1,0:T(8,128)(2,1)S(1)} %get-tuple-element.72), channel_id=1, source_target_pairs={{0,3},{1,2},{2,1},{3,0},{4,7},{5,6},{6,5},{7,4},{8,11},{9,10},{10,... | collective-permute-start | bytes 491528 | tf_op jit(solution)/shard_map/ppermute | solution.py:460
  22.0 22.4 %collective-permute-start.7 = (bf16[1,1,320,128]{3,2,1,0:T(8,128)(2,1)S(1)}, bf16[1,1,320,128]{3,2,1,0:T(8,128)(2,1)S(1)}, u32[]{:S(2)}, u32[]{:S(2)}) collective-permute-start(bf16[1,1,320,128]{3,2,1,0:T(8,128)(2,1)S(1)} %get-tuple-element.63), channel_id=1, source_target_pairs={{0,2},{1,3},{2,0},{3,1},{4,6},{5,7},{6,4},{7,5},{8,10},{9,11},{10,... | collective-permute-start | bytes 245768 | tf_op jit(solution)/shard_map/ppermute | solution.py:460
  26.8 17.5 %collective-permute-start.8 = (bf16[1,1,320,128]{3,2,1,0:T(8,128)(2,1)S(1)}, bf16[1,1,320,128]{3,2,1,0:T(8,128)(2,1)S(1)}, u32[]{:S(2)}, u32[]{:S(2)}) collective-permute-start(bf16[1,1,320,128]{3,2,1,0:T(8,128)(2,1)S(1)} %get-tuple-element.64), channel_id=1, source_target_pairs={{0,3},{1,2},{2,1},{3,0},{4,7},{5,6},{6,5},{7,4},{8,11},{9,10},{10,... | collective-permute-start | bytes 245768 | tf_op jit(solution)/shard_map/ppermute | solution.py:460
  27.0 19.8 %collective-permute-start.3 = (bf16[1,1,320,128]{3,2,1,0:T(8,128)(2,1)S(1)}, bf16[1,1,320,128]{3,2,1,0:T(8,128)(2,1)S(1)}, u32[]{:S(2)}, u32[]{:S(2)}) collective-permute-start(bf16[1,1,320,128]{3,2,1,0:T(8,128)(2,1)S(1)} %get-tuple-element.58), channel_id=1, source_target_pairs={{0,1},{1,0},{2,3},{3,2},{4,5},{5,4},{6,7},{7,6},{8,9},{9,8},{10,11... | collective-permute-start | bytes 245768 | tf_op jit(solution)/shard_map/ppermute | solution.py:460
  29.0 17.8 %collective-permute-start.4 = (bf16[1,1,320,128]{3,2,1,0:T(8,128)(2,1)S(1)}, bf16[1,1,320,128]{3,2,1,0:T(8,128)(2,1)S(1)}, u32[]{:S(2)}, u32[]{:S(2)}) collective-permute-start(bf16[1,1,320,128]{3,2,1,0:T(8,128)(2,1)S(1)} %get-tuple-element.59), channel_id=1, source_target_pairs={{0,2},{1,3},{2,0},{3,1},{4,6},{5,7},{6,4},{7,5},{8,10},{9,11},{10,... | collective-permute-start | bytes 245768 | tf_op jit(solution)/shard_map/ppermute | solution.py:460
  33.8 13.0 %collective-permute-start.5 = (bf16[1,1,320,128]{3,2,1,0:T(8,128)(2,1)S(1)}, bf16[1,1,320,128]{3,2,1,0:T(8,128)(2,1)S(1)}, u32[]{:S(2)}, u32[]{:S(2)}) collective-permute-start(bf16[1,1,320,128]{3,2,1,0:T(8,128)(2,1)S(1)} %get-tuple-element.60), channel_id=1, source_target_pairs={{0,3},{1,2},{2,1},{3,0},{4,7},{5,6},{6,5},{7,4},{8,11},{9,10},{10,... | collective-permute-start | bytes 245768 | tf_op jit(solution)/shard_map/ppermute | solution.py:460
  49.3 5.2 %collective-permute-start.20 = (bf16[1024,512]{1,0:T(8,128)(2,1)S(1)}, bf16[1024,512]{1,0:T(8,128)(2,1)S(1)}, u32[]{:S(2)}, u32[]{:S(2)}) collective-permute-start(bf16[1024,512]{1,0:T(8,128)(2,1)S(1)} %get-tuple-element.86.refs_0_.refs_2_.two), channel_id=1, source_target_pairs={{0,1},{2,3},{4,5},{6,7},{8,9},{10,11},{12,13},{14,15},{16,17},{18,... | collective-permute-start | bytes 3145736 | tf_op jit(solution)/shard_map/ppermute | solution.py:463
  50.6 3.6 %collective-permute-start.18 = (f32[1,512]{1,0:T(1,128)S(1)}, f32[1,512]{1,0:T(1,128)S(1)}, u32[]{:S(2)}, u32[]{:S(2)}) collective-permute-start(f32[1,512]{1,0:T(1,128)S(1)} %get-tuple-element.85.refs_1_.refs_3_), channel_id=1, source_target_pairs={{0,1},{2,3},{4,5},{6,7},{8,9},{10,11},{12,13},{14,15},{16,17},{18,... | collective-permute-start | bytes 6152 | tf_op jit(solution)/shard_map/ppermute | solution.py:463
  55.4 15.7 %collective-permute-start.25 = (bf16[1040,512]{1,0:T(8,128)(2,1)S(1)}, bf16[1040,512]{1,0:T(8,128)(2,1)S(1)}, u32[]{:S(2)}, u32[]{:S(2)}) collective-permute-start(bf16[1040,512]{1,0:T(8,128)(2,1)S(1)} %join.1.refs_0_), channel_id=1, source_target_pairs={{9,11},{11,9},{13,15},{15,13},{17,19},{19,17},{21,23},{23,21},{25,... | collective-permute-start | bytes 3194888 | tf_op jit(solution)/shard_map/ppermute | solution.py:463
  58.1 0.9 collective-permute-start.19
  59.4 0.7 collective-permute-start.21
  61.8 1.4 %collective-permute-start.24 = (f32[1,512]{1,0:T(1,128)S(1)}, f32[1,512]{1,0:T(1,128)S(1)}, u32[]{:S(2)}, u32[]{:S(2)}) collective-permute-start(f32[1,512]{1,0:T(1,128)S(1)} %hop.7), channel_id=1, source_target_pairs={{7,11}} | collective-permute-start | bytes 6152 | tf_op jit(solution)/shard_map/ppermute | solution.py:463
  62.5 0.7 collective-permute-start.23
  72.9 0.7 collective-permute-start.27
  74.1 0.7 collective-permute-start.28
  76.5 13.4 %collective-permute-start.30 = (f32[1,512]{1,0:T(1,128)S(1)}, f32[1,512]{1,0:T(1,128)S(1)}, u32[]{:S(2)}, u32[]{:S(2)}) collective-permute-start(f32[1,512]{1,0:T(1,128)S(1)} %span_hop.9), channel_id=1, source_target_pairs={{25,29},{27,31}} | collective-permute-start | bytes 6152 | tf_op jit(solution)/shard_map/ppermute | solution.py:463
  89.9 2.1 %collective-permute-start.31 = (f32[1,512]{1,0:T(1,128)S(1)}, f32[1,512]{1,0:T(1,128)S(1)}, u32[]{:S(2)}, u32[]{:S(2)}) collective-permute-start(f32[1,512]{1,0:T(1,128)S(1)} %lead.1.refs_0_), channel_id=1, source_target_pairs={{1,0},{3,2},{5,4},{7,6},{9,8},{11,10},{13,12},{15,14},{17,16},{19,... | collective-permute-start | bytes 6152 | tf_op jit(solution)/shard_map/ppermute | solution.py:463
  93.9 2.2 %collective-permute-start.32 = (f32[8,128]{1,0:T(8,128)S(1)}, f32[8,128]{1,0:T(8,128)S(1)}, u32[]{:S(2)}, u32[]{:S(2)}) collective-permute-start(f32[8,128]{1,0:T(8,128)S(1)} %get-tuple-element.98), channel_id=1, source_target_pairs={{0,1},{1,0},{2,3},{3,2},{4,5},{5,4},{6,7},{7,6},{8,9},{9,8},{10,11... | collective-permute-start | bytes 12296 | tf_op jit(solution)/shard_map/ppermute | solution.py:460
  94.1 2.5 %collective-permute-start.33 = (f32[8,128]{1,0:T(8,128)S(1)}, f32[8,128]{1,0:T(8,128)S(1)}, u32[]{:S(2)}, u32[]{:S(2)}) collective-permute-start(f32[8,128]{1,0:T(8,128)S(1)} %get-tuple-element.99), channel_id=1, source_target_pairs={{0,2},{1,3},{2,0},{3,1},{4,6},{5,7},{6,4},{7,5},{8,10},{9,11},{10,... | collective-permute-start | bytes 12296 | tf_op jit(solution)/shard_map/ppermute | solution.py:460
  94.9 3.4 %collective-permute-start.34 = (f32[8,128]{1,0:T(8,128)S(1)}, f32[8,128]{1,0:T(8,128)S(1)}, u32[]{:S(2)}, u32[]{:S(2)}) collective-permute-start(f32[8,128]{1,0:T(8,128)S(1)} %get-tuple-element.100), channel_id=1, source_target_pairs={{0,3},{1,2},{2,1},{3,0},{4,7},{5,6},{6,5},{7,4},{8,11},{9,10},{10,... | collective-permute-start | bytes 12296 | tf_op jit(solution)/shard_map/ppermute | solution.py:460
  (12 other events, 82.6 us)

commit v2 on v1

--- a/solution.py
+++ b/solution.py
@@ -236,6 +236,7 @@
                 down = lax.broadcasted_iota(jnp.int32, (step_of(ns), ns), 0) + r
                 unit = jnp.where(across == down, 1.0, 0.0).astype(BF)
                 map_ref[rows, :] = nt(unit, element).astype(BF)
+                map_ref[below, :] = jnp.zeros((step_of(ns), ns), BF)
                 continue
             moved = nt(held[rows, :], element)
             if first > 0 or j > 1:
@@ -244,6 +245,7 @@
             map_ref[rows, :] = top
             map_ref[below, :] = (moved - top.astype(F32)).astype(BF)
     vec_ref[...] = vec
+    map_ref[2 * ns :, :] = split3(vec)
 
 
 def chunk_piece(
@@ -272,7 +274,7 @@
         out_shape=[
             jax.ShapeDtypeStruct((count, ns, ns), BF),
             jax.ShapeDtypeStruct((count, 8, ns), F32),
-            jax.ShapeDtypeStruct((2 * ns, ns), BF),
+            jax.ShapeDtypeStruct((2 * ns + ROWS, ns), BF),
             jax.ShapeDtypeStruct((1, ns), F32),
         ],
         compiler_params=pltpu.CompilerParams(vmem_limit_bytes=VMEM_LIMIT),
@@ -284,10 +286,11 @@
 def apply_map(row, held):
     ns = held.shape[1]
     parts = split3(row)
-    return fold(nn(parts, held[:ns, :]) + nn(parts, held[ns : 2 * ns, :]))
-
-
-def join_kernel(one, two, vec_ref, out_ref):
+    moved = fold(nn(parts, held[:ns, :]) + nn(parts, held[ns : 2 * ns, :]))
+    return moved + fold(held[2 * ns :, :].astype(F32))
+
+
+def join_kernel(one, two, out_ref):
     ns = one.shape[1]
     for r in range(0, ns, step_of(ns)):
         rows, below = slice(r, r + step_of(ns)), slice(ns + r, ns + r + step_of(ns))
@@ -297,26 +300,25 @@
         top = product.astype(BF)
         out_ref[rows, :] = top
         out_ref[below, :] = (product - top.astype(F32)).astype(BF)
-    out_ref[2 * ns :, :] = split3(vec_ref[...])
-
-
-def join(one, two, vec):
-    ns = one.shape[1]
+    out_ref[2 * ns :, :] = split3(apply_map(fold(one[2 * ns :, :].astype(F32)), two))
+
+
+def join(one, two):
     return pl.pallas_call(
         join_kernel,
-        in_specs=vmem(3),
+        in_specs=vmem(2),
         out_specs=vmem(1)[0],
-        out_shape=jax.ShapeDtypeStruct((2 * ns + ROWS, ns), BF),
+        out_shape=jax.ShapeDtypeStruct(two.shape, BF),
         compiler_params=pltpu.CompilerParams(vmem_limit_bytes=VMEM_LIMIT),
         name="join",
-    )(one, two, vec)
+    )(one, two)
 
 
 def hop_kernel(row_ref, *refs):
-    current, out_ref = row_ref[...], refs[-1]
-    for n in range(0, len(refs) - 1, 2):
-        current = apply_map(current, refs[n]) + refs[n + 1][...]
-    out_ref[...] = current
+    current = row_ref[...]
+    for held in refs[:-1]:
+        current = apply_map(current, held)
+    refs[-1][...] = current
 
 
 def hop(row, *maps):
@@ -330,41 +332,72 @@
     )(row, *maps)
 
 
-def span_kernel(leaders, whole, early, s_ref, tm_ref, row_ref, direct_ref, *refs):
+def span_kernel(leaders, s_ref, row_ref, *refs):
     maps, out_ref = refs[:leaders], refs[leaders]
-    ns = out_ref.shape[1]
     for mine in range(leaders):
 
         @pl.when(s_ref[0] // 2 == mine)
         def _():
             current = row_ref[...]
-            for p in range(leaders if whole else mine):
-                held = maps[p ^ mine]
-                current = apply_map(current, held) + fold(held[2 * ns :, :].astype(F32))
-            if not whole:
-                current = jnp.where(tm_ref[0] < early, direct_ref[...], current)
+            for p in range(leaders):
+                current = apply_map(current, maps[p ^ mine])
             out_ref[...] = current
 
 
-def span_hop(position, span, row, direct, maps, whole, early):
+def span_hop(position, row, maps):
     leaders = len(maps)
     return pl.pallas_call(
-        functools.partial(span_kernel, leaders, whole, early),
+        functools.partial(span_kernel, leaders),
+        grid_spec=pltpu.PrefetchScalarGridSpec(
+            num_scalar_prefetch=1,
+            grid=(),
+            in_specs=vmem(1 + leaders),
+            out_specs=vmem(1)[0],
+        ),
+        out_shape=jax.ShapeDtypeStruct(row.shape, F32),
+        compiler_params=pltpu.CompilerParams(vmem_limit_bytes=VMEM_LIMIT),
+        name="span_hop",
+    )(position, row, *maps)
+
+
+def lead_kernel(leaders, early, s_ref, tm_ref, row_ref, direct_ref, *refs):
+    sets, out_ref = (refs[:leaders], refs[leaders : 2 * leaders]), refs[2 * leaders]
+
+    @pl.when(tm_ref[0] < early)
+    def _():
+        out_ref[...] = direct_ref[...]
+
+    for mine in range(leaders):
+        for late in range(2):
+            reached = (tm_ref[0] > early) if late else (tm_ref[0] == early)
+
+            @pl.when(jnp.logical_and(s_ref[0] // 2 == mine, reached))
+            def _():
+                current = row_ref[...]
+                for p in range(mine):
+                    current = apply_map(current, sets[late][p ^ mine])
+                out_ref[...] = current
+
+
+def lead(position, span, row, direct, maps, maps_late, early):
+    leaders = len(maps)
+    return pl.pallas_call(
+        functools.partial(lead_kernel, leaders, early),
         grid_spec=pltpu.PrefetchScalarGridSpec(
             num_scalar_prefetch=2,
             grid=(),
-            in_specs=vmem(2 + leaders),
+            in_specs=vmem(2 + 2 * leaders),
             out_specs=vmem(1)[0],
         ),
         out_shape=jax.ShapeDtypeStruct(row.shape, F32),
         compiler_params=pltpu.CompilerParams(vmem_limit_bytes=VMEM_LIMIT),
-        name="span_hop" if whole else "lead",
-    )(position, span, row, direct, *maps)
+        name="lead",
+    )(position, span, row, direct, *maps, *maps_late)
 
 
 def sweep_kernel(pieces, parts, s_ref, tm_ref, *refs):
-    own_ref, told_ref, prior_ref, map_ref, vec_ref = refs[:5]
-    refs = refs[5:]
+    own_ref, told_ref, prior_ref, first_map, first_vec, map_ref = refs[:6]
+    refs = refs[6:]
     elements, offsets = refs[:pieces], refs[pieces : 2 * pieces]
     outs = refs[2 * pieces : 2 * pieces + parts]
     current_ref, spread = refs[2 * pieces + parts :]
@@ -375,9 +408,13 @@
     def _():
         current_ref[...] = told_ref[...] + jnp.where(begin, prior_ref[...], 0.0)
 
-    @pl.when(s % 2 == 1)
+    @pl.when(jnp.logical_and(s % 2 == 1, tm_ref[0] == 0))
     def _():
-        current_ref[...] = apply_map(own_ref[...], map_ref) + vec_ref[...]
+        current_ref[...] = apply_map(own_ref[...], first_map) + first_vec[...]
+
+    @pl.when(jnp.logical_and(s % 2 == 1, tm_ref[0] > 0))
+    def _():
+        current_ref[...] = apply_map(own_ref[...], map_ref)
 
     current = current_ref[...]
     at = 0
@@ -402,7 +439,7 @@
         grid_spec=pltpu.PrefetchScalarGridSpec(
             num_scalar_prefetch=2,
             grid=(),
-            in_specs=vmem(5 + 2 * pieces),
+            in_specs=vmem(6 + 2 * pieces),
             out_specs=vmem(parts),
             scratch_shapes=[
                 pltpu.VMEM((1, ns), F32),
@@ -496,44 +533,45 @@
 
     leads = [2 * p + 1 for p in range(parts // 2)]
     to_lead = [((a, l - 1), (a, l)) for a in range(spans) for l in leads]
-    vec_even = send(vec, to_lead)
-    map_even = send(chunk_map, to_lead)
-    both = (map_even, vec_even, chunk_map, vec)
-    pair_vec = hop(vec_even, chunk_map, vec)
-    pair = join(map_even, chunk_map, pair_vec)
+    map_even = send(chunk_map, [pair for pair in to_lead if pair[0][0] > 0])
+    first_vec = send(vec, to_lead[:1])
+    first_map = send(chunk_map, to_lead[1 : len(leads)])
+    current = hop(first_vec, chunk_map)
+    pair = join(map_even, chunk_map)
 
     early = min(2, spans - 1)
-    maps = [pair]
+    maps, maps_late = [pair], [pair]
     for d in range(2, parts, 2):
         pairs = [((a, l), (a, l ^ d)) for a in range(early, spans) for l in leads]
-        maps.append(send(pair, pairs))
+        maps.append(send(pair, pairs[: len(leads)]))
+        maps_late.append(send(pair, pairs[len(leads) :]))
 
     direct = jnp.zeros((1, ns), F32)
     entry = jnp.zeros((1, ns), F32)
-    current = pair_vec
     for g in range(early):
+        held = (pair,) if g > 0 else (first_map, chunk_map)
         for p in range(1, len(leads)):
             arriving = send(current, [((g, leads[p - 1]), (g, leads[p]))])
             direct = direct + arriving
-            current = hop(arriving, *both)
+            current = hop(arriving, *held)
         if g + 1 < early:
             arriving = send(current, [((g, leads[-1]), (g + 1, leads[0]))])
             direct = direct + arriving
-            current = hop(arriving, *both)
+            current = hop(arriving, pair)
         else:
             for l in leads:
                 entry = entry + send(current, [((g, leads[-1]), (g + 1, l))])
 
     arriving = entry
     for h in range(early, spans - 1):
-        current = span_hop(position, span, arriving, direct, maps, True, early)
+        current = span_hop(position, arriving, maps if h == early else maps_late)
         arriving = send(current, [((h, l), (h + 1, l)) for l in leads])
         entry = entry + arriving
 
-    own = span_hop(position, span, entry, direct, maps, False, early)
+    own = lead(position, span, entry, direct, maps, maps_late, early)
     told = send(own, [(b, a) for a, b in to_lead])
     mine = sweep(
-        position, span, own, told, prior_row, (map_even, vec_even), elements, offsets, parts
+        position, span, own, told, prior_row, (first_map, first_vec, map_even), elements, offsets, parts,
     )
     got = {0: mine[0]}
     for d in order:

time: 99.3 us -> 99.6 us (level)
    ppermute x14 -> x16, waiting for transfers between devices: 23.1 us -> 21 us  [send(): lax.ppermute(x, ('tm', 'state'), [(a * parts + b, c * parts + e) for (a,...]
    ppermute x21, waiting for transfers between devices: 18.5 us -> 20.4 us  [across(): return lax.ppermute(x, 'state', [(i, i ^ d) for i in range(parts)])]
    ppermute x14 -> x16, starting transfers between devices: 13.9 us -> 14.6 us  [send(): lax.ppermute(x, ('tm', 'state'), [(a * parts + b, c * parts + e) for (a,...]
  transfers between devices with their start and end apart: 35 -> 37, of which waited for: 14 -> 14; matrix products, arithmetic and copies ran while one was open for 0% -> 0% of each run, Pallas kernels for 15% -> 16%
where the time goes in v2:
time: 99.6 us; the launch traced here: 99.3 us
  waiting for transfers between devices  41.4 us (42%)
  starting transfers between devices  32.5 us (33%)
  Pallas kernels  24.9 us (25%)
    ppermute x16, waiting for transfers between devices, send(): lax.ppermute(x, ('tm', 'state'), [(a * parts + b, c * parts + e) for (a,...  21 us
    ppermute x21, waiting for transfers between devices, across(): return lax.ppermute(x, 'state', [(i, i ^ d) for i in range(parts)])  20.4 us
    ppermute x21, starting transfers between devices, across(): return lax.ppermute(x, 'state', [(i, i ^ d) for i in range(parts)])  17.8 us
    pallas_call x5, Pallas kernels, chunk_piece(): pl.pallas_call(functools.partial(chunk_kernel, parts, pairs, bs, chunk, f...  15.1 us
    ppermute x16, starting transfers between devices, send(): lax.ppermute(x, ('tm', 'state'), [(a * parts + b, c * parts + e) for (a,...  14.6 us
    pallas_call x5, Pallas kernels, span_hop(): pl.pallas_call(functools.partial(span_kernel, leaders), grid_spec=pltpu.P...  2.57 us
    pallas_call x5, Pallas kernels, pack(): pl.pallas_call(functools.partial(pack_kernel, parts, pairs, bs, chunk, bo...  2.21 us
  transfers between devices with their start and end apart: 37, of which 14 were waited for; matrix products, arithmetic and copies ran while one was open for 0% of the time, Pallas kernels for 16%

profile of v2, /device:TPU:27, one launch (start us, length us, event | category | flops | bytes accessed | tf_op | source)
XLA Modules:
  0.0 99.3 jit_solution(15127764041088634121)
XLA Ops:
  0.0 1.5 %shard_map.95 = (bf16[2,1,320,128]{3,2,1,0:T(8,128)(2,1)S(1)}, bf16[2,1,320,128]{3,2,1,0:T(8,128)(2,1)S(1)}, bf16[2,1,320,128]{3,2,1,0:T(8,128)(2,1)S(1)}, bf16[2,1,320,128]{3,2,1,0:T(8,128)(2,1)S(1)}) custom-call(s32[1]{0:T(128)} %bitcast.s_ref, s32[1]{0:T(128)} %bitcast.1.tm_ref, bf16[32,2,64,192]{3,2,1,0:T(8,128)(2,1)} %refs_3_.9, ...), custom_call_target="tpu_custom_call" | custom-call | tf_op jit(solution)/shard_map/pallas_call | solution.py:95
  2.3 1.2 %collective-permute-start.16 = (bf16[2,1,320,128]{3,2,1,0:T(8,128)(2,1)S(1)}, bf16[2,1,320,128]{3,2,1,0:T(8,128)(2,1)S(1)}, u32[]{:S(2)}, u32[]{:S(2)}) collective-permute-start(bf16[2,1,320,128]{3,2,1,0:T(8,128)(2,1)S(1)} %get-tuple-element.75), channel_id=1, source_target_pairs={{0,2},{1,3},{2,0},{3,1},{4,6},{5,7},{6,4},{7,5},{8,10},{9,11},{10,... | collective-permute-start | bytes 491528 | tf_op jit(solution)/shard_map/ppermute | solution.py:497
  5.8 1.2 %collective-permute-start.1 = (f32[14,128]{1,0:T(8,128)S(1)}, f32[14,128]{1,0:T(8,128)S(1)}, u32[]{:S(2)}, u32[]{:S(2)}) collective-permute-start(f32[14,128]{1,0:T(8,128)S(1)} %get-tuple-element.55), channel_id=1, source_target_pairs={{0,2},{1,3},{2,0},{3,1},{4,6},{5,7},{6,4},{7,5},{8,10},{9,11},{10,... | collective-permute-start | bytes 21512 | tf_op jit(solution)/shard_map/ppermute | solution.py:497
  7.0 4.5 %collective-permute-done.1.refs_2_.refs_6_ = f32[14,128]{1,0:T(8,128)S(1)} collective-permute-done((f32[14,128]{1,0:T(8,128)S(1)}, f32[14,128]{1,0:T(8,128)S(1)}, u32[]{:S(2)}, u32[]{:S(2)}) %collective-permute-start.1) | collective-permute-done | bytes 7200 | tf_op jit(solution)/shard_map/ppermute | solution.py:497
  11.5 2.2 %collective-permute-start.2 = (f32[14,128]{1,0:T(8,128)S(1)}, f32[14,128]{1,0:T(8,128)S(1)}, u32[]{:S(2)}, u32[]{:S(2)}) collective-permute-start(f32[14,128]{1,0:T(8,128)S(1)} %get-tuple-element.56), channel_id=1, source_target_pairs={{0,3},{1,2},{2,1},{3,0},{4,7},{5,6},{6,5},{7,4},{8,11},{9,10},{10,... | collective-permute-start | bytes 21512 | tf_op jit(solution)/shard_map/ppermute | solution.py:497
  13.8 1.5 %collective-permute-done.2.refs_3_.refs_7_ = f32[14,128]{1,0:T(8,128)S(1)} collective-permute-done((f32[14,128]{1,0:T(8,128)S(1)}, f32[14,128]{1,0:T(8,128)S(1)}, u32[]{:S(2)}, u32[]{:S(2)}) %collective-permute-start.2) | collective-permute-done | bytes 7200 | tf_op jit(solution)/shard_map/ppermute | solution.py:497
  16.6 1.2 %collective-permute-start.13 = (bf16[2,1,320,128]{3,2,1,0:T(8,128)(2,1)S(1)}, bf16[2,1,320,128]{3,2,1,0:T(8,128)(2,1)S(1)}, u32[]{:S(2)}, u32[]{:S(2)}) collective-permute-start(bf16[2,1,320,128]{3,2,1,0:T(8,128)(2,1)S(1)} %get-tuple-element.71), channel_id=1, source_target_pairs={{0,2},{1,3},{2,0},{3,1},{4,6},{5,7},{6,4},{7,5},{8,10},{9,11},{10,... | collective-permute-start | bytes 491528 | tf_op jit(solution)/shard_map/ppermute | solution.py:497
  18.6 1.2 %collective-permute-start.10 = (bf16[2,1,320,128]{3,2,1,0:T(8,128)(2,1)S(1)}, bf16[2,1,320,128]{3,2,1,0:T(8,128)(2,1)S(1)}, u32[]{:S(2)}, u32[]{:S(2)}) collective-permute-start(bf16[2,1,320,128]{3,2,1,0:T(8,128)(2,1)S(1)} %get-tuple-element.67), channel_id=1, source_target_pairs={{0,2},{1,3},{2,0},{3,1},{4,6},{5,7},{6,4},{7,5},{8,10},{9,11},{10,... | collective-permute-start | bytes 491528 | tf_op jit(solution)/shard_map/ppermute | solution.py:497
  20.7 1.3 %collective-permute-done.13.refs_2_ = bf16[2,1,320,128]{3,2,1,0:T(8,128)(2,1)S(1)} collective-permute-done((bf16[2,1,320,128]{3,2,1,0:T(8,128)(2,1)S(1)}, bf16[2,1,320,128]{3,2,1,0:T(8,128)(2,1)S(1)}, u32[]{:S(2)}, u32[]{:S(2)}) %collective-permute-start.13) | collective-permute-done | bytes 163872 | tf_op jit(solution)/shard_map/ppermute | solution.py:497
  22.0 1.2 %collective-permute-start.7 = (bf16[1,1,320,128]{3,2,1,0:T(8,128)(2,1)S(1)}, bf16[1,1,320,128]{3,2,1,0:T(8,128)(2,1)S(1)}, u32[]{:S(2)}, u32[]{:S(2)}) collective-permute-start(bf16[1,1,320,128]{3,2,1,0:T(8,128)(2,1)S(1)} %get-tuple-element.63), channel_id=1, source_target_pairs={{0,2},{1,3},{2,0},{3,1},{4,6},{5,7},{6,4},{7,5},{8,10},{9,11},{10,... | collective-permute-start | bytes 245768 | tf_op jit(solution)/shard_map/ppermute | solution.py:497
  23.2 3.6 %collective-permute-done.14.refs_3_ = bf16[2,1,320,128]{3,2,1,0:T(8,128)(2,1)S(1)} collective-permute-done((bf16[2,1,320,128]{3,2,1,0:T(8,128)(2,1)S(1)}, bf16[2,1,320,128]{3,2,1,0:T(8,128)(2,1)S(1)}, u32[]{:S(2)}, u32[]{:S(2)}) %collective-permute-start.14) | collective-permute-done | bytes 163872 | tf_op jit(solution)/shard_map/ppermute | solution.py:497
  27.0 2.0 %collective-permute-done.10.refs_2_ = bf16[2,1,320,128]{3,2,1,0:T(8,128)(2,1)S(1)} collective-permute-done((bf16[2,1,320,128]{3,2,1,0:T(8,128)(2,1)S(1)}, bf16[2,1,320,128]{3,2,1,0:T(8,128)(2,1)S(1)}, u32[]{:S(2)}, u32[]{:S(2)}) %collective-permute-start.10) | collective-permute-done | bytes 163872 | tf_op jit(solution)/shard_map/ppermute | solution.py:497
  29.0 2.0 %collective-permute-start.3 = (bf16[1,1,320,128]{3,2,1,0:T(8,128)(2,1)S(1)}, bf16[1,1,320,128]{3,2,1,0:T(8,128)(2,1)S(1)}, u32[]{:S(2)}, u32[]{:S(2)}) collective-permute-start(bf16[1,1,320,128]{3,2,1,0:T(8,128)(2,1)S(1)} %get-tuple-element.58), channel_id=1, source_target_pairs={{0,1},{1,0},{2,3},{3,2},{4,5},{5,4},{6,7},{7,6},{8,9},{9,8},{10,11... | collective-permute-start | bytes 245768 | tf_op jit(solution)/shard_map/ppermute | solution.py:497
  31.0 2.8 %collective-permute-done.11.refs_3_ = bf16[2,1,320,128]{3,2,1,0:T(8,128)(2,1)S(1)} collective-permute-done((bf16[2,1,320,128]{3,2,1,0:T(8,128)(2,1)S(1)}, bf16[2,1,320,128]{3,2,1,0:T(8,128)(2,1)S(1)}, u32[]{:S(2)}, u32[]{:S(2)}) %collective-permute-start.11) | collective-permute-done | bytes 163872 | tf_op jit(solution)/shard_map/ppermute | solution.py:497
  33.9 1.2 %collective-permute-start.4 = (bf16[1,1,320,128]{3,2,1,0:T(8,128)(2,1)S(1)}, bf16[1,1,320,128]{3,2,1,0:T(8,128)(2,1)S(1)}, u32[]{:S(2)}, u32[]{:S(2)}) collective-permute-start(bf16[1,1,320,128]{3,2,1,0:T(8,128)(2,1)S(1)} %get-tuple-element.59), channel_id=1, source_target_pairs={{0,2},{1,3},{2,0},{3,1},{4,6},{5,7},{6,4},{7,5},{8,10},{9,11},{10,... | collective-permute-start | bytes 245768 | tf_op jit(solution)/shard_map/ppermute | solution.py:497
  35.3 3.1 %shard_map.96 = (bf16[2,512,512]{2,1,0:T(8,128)(2,1)S(1)}, f32[2,8,512]{2,1,0:T(8,128)S(1)}, bf16[1040,512]{1,0:T(8,128)(2,1)S(1)}, f32[1,512]{1,0:T(1,128)S(1)}) custom-call(s32[1]{0:T(128)} %bitcast.s_ref, s32[1]{0:T(128)} %bitcast.1.tm_ref, s32[27,32]{1,0:T(8,128)S(1)} %plan.1.plan_ref, bf16[2,1,320,128]{3,2,1,0:T(8,128)(2,1)S(1)} %get-tuple-element.73.refs_0_.refs_11_, ...), custom_call_target="tpu_custom_call" | custom-call | tf_op jit(solution)/shard_map/pallas_call | solution.py:260
  38.3 3.6 %shard_map.97 = (bf16[2,512,512]{2,1,0:T(8,128)(2,1)S(1)}, f32[2,8,512]{2,1,0:T(8,128)S(1)}, bf16[1040,512]{1,0:T(8,128)(2,1)S(1)}, f32[1,512]{1,0:T(1,128)S(1)}) custom-call(s32[1]{0:T(128)} %bitcast.s_ref, s32[1]{0:T(128)} %bitcast.1.tm_ref, s32[27,32]{1,0:T(8,128)S(1)} %plan.1.plan_ref, bf16[2,1,320,128]{3,2,1,0:T(8,128)(2,1)S(1)} %get-tuple-element.69.refs_0_, ...), custom_call_target="tpu_custom_call" | custom-call | tf_op jit(solution)/shard_map/pallas_call | solution.py:260
  42.0 3.6 %shard_map.98 = (bf16[2,512,512]{2,1,0:T(8,128)(2,1)S(1)}, f32[2,8,512]{2,1,0:T(8,128)S(1)}, bf16[1040,512]{1,0:T(8,128)(2,1)S(1)}, f32[1,512]{1,0:T(1,128)S(1)}) custom-call(s32[1]{0:T(128)} %bitcast.s_ref, s32[1]{0:T(128)} %bitcast.1.tm_ref, s32[27,32]{1,0:T(8,128)S(1)} %plan.1.plan_ref, bf16[2,1,320,128]{3,2,1,0:T(8,128)(2,1)S(1)} %get-tuple-element.65.refs_0_, ...), custom_call_target="tpu_custom_call" | custom-call | tf_op jit(solution)/shard_map/pallas_call | solution.py:260
  45.6 2.4 %shard_map.99 = (bf16[1,512,512]{2,1,0:T(8,128)(2,1)S(1)}, f32[1,8,512]{2,1,0:T(8,128)S(1)}, bf16[1040,512]{1,0:T(8,128)(2,1)S(1)}, f32[1,512]{1,0:T(1,128)S(1)}) custom-call(s32[1]{0:T(128)} %bitcast.s_ref, s32[1]{0:T(128)} %bitcast.1.tm_ref, s32[27,32]{1,0:T(8,128)S(1)} %plan.1.plan_ref, bf16[1,1,320,128]{3,2,1,0:T(8,128)(2,1)S(1)} %get-tuple-element.61.refs_0_, ...), custom_call_target="tpu_custom_call" | custom-call | tf_op jit(solution)/shard_map/pallas_call | solution.py:260
  48.1 2.4 %shard_map.100 = (bf16[1,512,512]{2,1,0:T(8,128)(2,1)S(1)}, f32[1,8,512]{2,1,0:T(8,128)S(1)}, bf16[1040,512]{1,0:T(8,128)(2,1)S(1)}, f32[1,512]{1,0:T(1,128)S(1)}) custom-call(s32[1]{0:T(128)} %bitcast.s_ref, s32[1]{0:T(128)} %bitcast.1.tm_ref, s32[27,32]{1,0:T(8,128)S(1)} %plan.1.plan_ref, bf16[1,1,320,128]{3,2,1,0:T(8,128)(2,1)S(1)} %get-tuple-element.57.refs_0_, ...), custom_call_target="tpu_custom_call" | custom-call | tf_op jit(solution)/shard_map/pallas_call | solution.py:260
  50.5 1.3 %collective-permute-start.22 = (bf16[1040,512]{1,0:T(8,128)(2,1)S(1)}, bf16[1040,512]{1,0:T(8,128)(2,1)S(1)}, u32[]{:S(2)}, u32[]{:S(2)}) collective-permute-start(bf16[1040,512]{1,0:T(8,128)(2,1)S(1)} %get-tuple-element.86.refs_0_.refs_1_.two), channel_id=1, source_target_pairs={{4,5},{6,7},{8,9},{10,11},{12,13},{14,15},{16,17},{18,19},{20,21},... | collective-permute-start | bytes 3194888 | tf_op jit(solution)/shard_map/ppermute | solution.py:500
  52.5 2.5 %collective-permute-done.22.one.refs_5_ = bf16[1040,512]{1,0:T(8,128)(2,1)S(1)} collective-permute-done((bf16[1040,512]{1,0:T(8,128)(2,1)S(1)}, bf16[1040,512]{1,0:T(8,128)(2,1)S(1)}, u32[]{:S(2)}, u32[]{:S(2)}) %collective-permute-start.22) | collective-permute-done | bytes 1064992 | tf_op jit(solution)/shard_map/ppermute | solution.py:500
  55.1 1.1 %join.1.refs_0_.refs_2_ = bf16[1040,512]{1,0:T(8,128)(2,1)S(1)} custom-call(bf16[1040,512]{1,0:T(8,128)(2,1)S(1)} %collective-permute-done.22.one.refs_5_, bf16[1040,512]{1,0:T(8,128)(2,1)S(1)} %get-tuple-element.86.refs_0_.refs_1_.two), custom_call_target="tpu_custom_call" | custom-call | tf_op jit(solution)/shard_map/join/pallas_call | solution.py:307
  56.2 0.9 collective-permute-start.26
  57.1 2.5 %collective-permute-start.28 = (bf16[1040,512]{1,0:T(8,128)(2,1)S(1)}, bf16[1040,512]{1,0:T(8,128)(2,1)S(1)}, u32[]{:S(2)}, u32[]{:S(2)}) collective-permute-start(bf16[1040,512]{1,0:T(8,128)(2,1)S(1)} %join.1.refs_0_.refs_2_), channel_id=1, source_target_pairs={{13,15},{15,13},{17,19},{19,17},{21,23},{23,21},{25,27},{27,25},{2... | collective-permute-start | bytes 3194888 | tf_op jit(solution)/shard_map/ppermute | solution.py:500
  66.2 6.6 %collective-permute-done.28.refs_1_.refs_3_ = bf16[1040,512]{1,0:T(8,128)(2,1)S(1)} collective-permute-done((bf16[1040,512]{1,0:T(8,128)(2,1)S(1)}, bf16[1040,512]{1,0:T(8,128)(2,1)S(1)}, u32[]{:S(2)}, u32[]{:S(2)}) %collective-permute-start.28) | collective-permute-done | bytes 1064992 | tf_op jit(solution)/shard_map/ppermute | solution.py:500
  76.9 1.3 %collective-permute-start.32 = (f32[1,512]{1,0:T(1,128)S(1)}, f32[1,512]{1,0:T(1,128)S(1)}, u32[]{:S(2)}, u32[]{:S(2)}) collective-permute-start(f32[1,512]{1,0:T(1,128)S(1)} %span_hop.9), channel_id=1, source_target_pairs={{25,29},{27,31}} | collective-permute-start | bytes 6152 | tf_op jit(solution)/shard_map/ppermute | solution.py:500
  78.3 11.1 %collective-permute-done.32 = f32[1,512]{1,0:T(1,128)S(1)} collective-permute-done((f32[1,512]{1,0:T(1,128)S(1)}, f32[1,512]{1,0:T(1,128)S(1)}, u32[]{:S(2)}, u32[]{:S(2)}) %collective-permute-start.32) | collective-permute-done | bytes 2080 | tf_op jit(solution)/shard_map/ppermute | solution.py:500
  89.4 1.3 %collective-permute-start.33 = (f32[1,512]{1,0:T(1,128)S(1)}, f32[1,512]{1,0:T(1,128)S(1)}, u32[]{:S(2)}, u32[]{:S(2)}) collective-permute-start(f32[1,512]{1,0:T(1,128)S(1)} %lead.1.refs_0_), channel_id=1, source_target_pairs={{1,0},{3,2},{5,4},{7,6},{9,8},{11,10},{13,12},{15,14},{17,16},{19,... | collective-permute-start | bytes 6152 | tf_op jit(solution)/shard_map/ppermute | solution.py:500
  91.5 1.9 %sweep.1 = (f32[8,128]{1,0:T(8,128)S(1)}, f32[8,128]{1,0:T(8,128)S(1)}, f32[8,128]{1,0:T(8,128)S(1)}, f32[8,128]{1,0:T(8,128)S(1)}) custom-call(s32[1]{0:T(128)} %bitcast.s_ref, s32[1]{0:T(128)} %bitcast.1.tm_ref, f32[1,512]{1,0:T(1,128)S(1)} %lead.1.refs_0_, f32[1,512]{1,0:T(1,128)S(1)} %collective-permute-done.33.refs_1_, f32[1,512]{1,0:T(1,128)S(1)} %bitcast.12, ...), custom_call_target="tpu_custom_call" | custom-call | tf_op jit(solution)/shard_map/sweep/pallas_call | solution.py:437
  93.6 1.8 %collective-permute-start.35 = (f32[8,128]{1,0:T(8,128)S(1)}, f32[8,128]{1,0:T(8,128)S(1)}, u32[]{:S(2)}, u32[]{:S(2)}) collective-permute-start(f32[8,128]{1,0:T(8,128)S(1)} %get-tuple-element.99), channel_id=1, source_target_pairs={{0,2},{1,3},{2,0},{3,1},{4,6},{5,7},{6,4},{7,5},{8,10},{9,11},{10,... | collective-permute-start | bytes 12296 | tf_op jit(solution)/shard_map/ppermute | solution.py:497
  96.4 2.4 %collective-permute-done.36.refs_3_ = f32[8,128]{1,0:T(8,128)S(1)} collective-permute-done((f32[8,128]{1,0:T(8,128)S(1)}, f32[8,128]{1,0:T(8,128)S(1)}, u32[]{:S(2)}, u32[]{:S(2)}) %collective-permute-start.36) | collective-permute-done | bytes 4128 | tf_op jit(solution)/shard_map/ppermute | solution.py:497
  (87 shorter events, 20.2 us)
Async XLA Ops:
  1.5 16.3 %collective-permute-start.15 = (bf16[2,1,320,128]{3,2,1,0:T(8,128)(2,1)S(1)}, bf16[2,1,320,128]{3,2,1,0:T(8,128)(2,1)S(1)}, u32[]{:S(2)}, u32[]{:S(2)}) collective-permute-start(bf16[2,1,320,128]{3,2,1,0:T(8,128)(2,1)S(1)} %get-tuple-element.74), channel_id=1, source_target_pairs={{0,1},{1,0},{2,3},{3,2},{4,5},{5,4},{6,7},{7,6},{8,9},{9,8},{10,11... | collective-permute-start | bytes 491528 | tf_op jit(solution)/shard_map/ppermute | solution.py:497
  2.3 16.3 %collective-permute-start.16 = (bf16[2,1,320,128]{3,2,1,0:T(8,128)(2,1)S(1)}, bf16[2,1,320,128]{3,2,1,0:T(8,128)(2,1)S(1)}, u32[]{:S(2)}, u32[]{:S(2)}) collective-permute-start(bf16[2,1,320,128]{3,2,1,0:T(8,128)(2,1)S(1)} %get-tuple-element.75), channel_id=1, source_target_pairs={{0,2},{1,3},{2,0},{3,1},{4,6},{5,7},{6,4},{7,5},{8,10},{9,11},{10,... | collective-permute-start | bytes 491528 | tf_op jit(solution)/shard_map/ppermute | solution.py:497
  3.5 16.3 %collective-permute-start.17 = (bf16[2,1,320,128]{3,2,1,0:T(8,128)(2,1)S(1)}, bf16[2,1,320,128]{3,2,1,0:T(8,128)(2,1)S(1)}, u32[]{:S(2)}, u32[]{:S(2)}) collective-permute-start(bf16[2,1,320,128]{3,2,1,0:T(8,128)(2,1)S(1)} %get-tuple-element.76), channel_id=1, source_target_pairs={{0,3},{1,2},{2,1},{3,0},{4,7},{5,6},{6,5},{7,4},{8,11},{9,10},{10,... | collective-permute-start | bytes 491528 | tf_op jit(solution)/shard_map/ppermute | solution.py:497
  4.3 15.9 %collective-permute-start.12 = (bf16[2,1,320,128]{3,2,1,0:T(8,128)(2,1)S(1)}, bf16[2,1,320,128]{3,2,1,0:T(8,128)(2,1)S(1)}, u32[]{:S(2)}, u32[]{:S(2)}) collective-permute-start(bf16[2,1,320,128]{3,2,1,0:T(8,128)(2,1)S(1)} %get-tuple-element.70), channel_id=1, source_target_pairs={{0,1},{1,0},{2,3},{3,2},{4,5},{5,4},{6,7},{7,6},{8,9},{9,8},{10,11... | collective-permute-start | bytes 491528 | tf_op jit(solution)/shard_map/ppermute | solution.py:497
  4.5 1.3 %collective-permute-start = (f32[14,128]{1,0:T(8,128)S(1)}, f32[14,128]{1,0:T(8,128)S(1)}, u32[]{:S(2)}, u32[]{:S(2)}) collective-permute-start(f32[14,128]{1,0:T(8,128)S(1)} %get-tuple-element.54), channel_id=1, source_target_pairs={{0,1},{1,0},{2,3},{3,2},{4,5},{5,4},{6,7},{7,6},{8,9},{9,8},{10,11... | collective-permute-start | bytes 21512 | tf_op jit(solution)/shard_map/ppermute | solution.py:497
  5.8 5.7 %collective-permute-start.1 = (f32[14,128]{1,0:T(8,128)S(1)}, f32[14,128]{1,0:T(8,128)S(1)}, u32[]{:S(2)}, u32[]{:S(2)}) collective-permute-start(f32[14,128]{1,0:T(8,128)S(1)} %get-tuple-element.55), channel_id=1, source_target_pairs={{0,2},{1,3},{2,0},{3,1},{4,6},{5,7},{6,4},{7,5},{8,10},{9,11},{10,... | collective-permute-start | bytes 21512 | tf_op jit(solution)/shard_map/ppermute | solution.py:497
  11.5 3.8 %collective-permute-start.2 = (f32[14,128]{1,0:T(8,128)S(1)}, f32[14,128]{1,0:T(8,128)S(1)}, u32[]{:S(2)}, u32[]{:S(2)}) collective-permute-start(f32[14,128]{1,0:T(8,128)S(1)} %get-tuple-element.56), channel_id=1, source_target_pairs={{0,3},{1,2},{2,1},{3,0},{4,7},{5,6},{6,5},{7,4},{8,11},{9,10},{10,... | collective-permute-start | bytes 21512 | tf_op jit(solution)/shard_map/ppermute | solution.py:497
  15.3 1.3 %collective-permute-start.6 = (bf16[1,1,320,128]{3,2,1,0:T(8,128)(2,1)S(1)}, bf16[1,1,320,128]{3,2,1,0:T(8,128)(2,1)S(1)}, u32[]{:S(2)}, u32[]{:S(2)}) collective-permute-start(bf16[1,1,320,128]{3,2,1,0:T(8,128)(2,1)S(1)} %get-tuple-element.62), channel_id=1, source_target_pairs={{0,1},{1,0},{2,3},{3,2},{4,5},{5,4},{6,7},{7,6},{8,9},{9,8},{10,11... | collective-permute-start | bytes 245768 | tf_op jit(solution)/shard_map/ppermute | solution.py:497
  16.6 5.4 %collective-permute-start.13 = (bf16[2,1,320,128]{3,2,1,0:T(8,128)(2,1)S(1)}, bf16[2,1,320,128]{3,2,1,0:T(8,128)(2,1)S(1)}, u32[]{:S(2)}, u32[]{:S(2)}) collective-permute-start(bf16[2,1,320,128]{3,2,1,0:T(8,128)(2,1)S(1)} %get-tuple-element.71), channel_id=1, source_target_pairs={{0,2},{1,3},{2,0},{3,1},{4,6},{5,7},{6,4},{7,5},{8,10},{9,11},{10,... | collective-permute-start | bytes 491528 | tf_op jit(solution)/shard_map/ppermute | solution.py:497
  17.8 9.0 %collective-permute-start.14 = (bf16[2,1,320,128]{3,2,1,0:T(8,128)(2,1)S(1)}, bf16[2,1,320,128]{3,2,1,0:T(8,128)(2,1)S(1)}, u32[]{:S(2)}, u32[]{:S(2)}) collective-permute-start(bf16[2,1,320,128]{3,2,1,0:T(8,128)(2,1)S(1)} %get-tuple-element.72), channel_id=1, source_target_pairs={{0,3},{1,2},{2,1},{3,0},{4,7},{5,6},{6,5},{7,4},{8,11},{9,10},{10,... | collective-permute-start | bytes 491528 | tf_op jit(solution)/shard_map/ppermute | solution.py:497
  18.6 10.4 %collective-permute-start.10 = (bf16[2,1,320,128]{3,2,1,0:T(8,128)(2,1)S(1)}, bf16[2,1,320,128]{3,2,1,0:T(8,128)(2,1)S(1)}, u32[]{:S(2)}, u32[]{:S(2)}) collective-permute-start(bf16[2,1,320,128]{3,2,1,0:T(8,128)(2,1)S(1)} %get-tuple-element.67), channel_id=1, source_target_pairs={{0,2},{1,3},{2,0},{3,1},{4,6},{5,7},{6,4},{7,5},{8,10},{9,11},{10,... | collective-permute-start | bytes 491528 | tf_op jit(solution)/shard_map/ppermute | solution.py:497
  19.8 14.0 %collective-permute-start.11 = (bf16[2,1,320,128]{3,2,1,0:T(8,128)(2,1)S(1)}, bf16[2,1,320,128]{3,2,1,0:T(8,128)(2,1)S(1)}, u32[]{:S(2)}, u32[]{:S(2)}) collective-permute-start(bf16[2,1,320,128]{3,2,1,0:T(8,128)(2,1)S(1)} %get-tuple-element.68), channel_id=1, source_target_pairs={{0,3},{1,2},{2,1},{3,0},{4,7},{5,6},{6,5},{7,4},{8,11},{9,10},{10,... | collective-permute-start | bytes 491528 | tf_op jit(solution)/shard_map/ppermute | solution.py:497
  20.2 14.9 %collective-permute-start.9 = (bf16[2,1,320,128]{3,2,1,0:T(8,128)(2,1)S(1)}, bf16[2,1,320,128]{3,2,1,0:T(8,128)(2,1)S(1)}, u32[]{:S(2)}, u32[]{:S(2)}) collective-permute-start(bf16[2,1,320,128]{3,2,1,0:T(8,128)(2,1)S(1)} %get-tuple-element.66), channel_id=1, source_target_pairs={{0,1},{1,0},{2,3},{3,2},{4,5},{5,4},{6,7},{7,6},{8,9},{9,8},{10,11... | collective-permute-start | bytes 491528 | tf_op jit(solution)/shard_map/ppermute | solution.py:497
  22.0 23.6 %collective-permute-start.7 = (bf16[1,1,320,128]{3,2,1,0:T(8,128)(2,1)S(1)}, bf16[1,1,320,128]{3,2,1,0:T(8,128)(2,1)S(1)}, u32[]{:S(2)}, u32[]{:S(2)}) collective-permute-start(bf16[1,1,320,128]{3,2,1,0:T(8,128)(2,1)S(1)} %get-tuple-element.63), channel_id=1, source_target_pairs={{0,2},{1,3},{2,0},{3,1},{4,6},{5,7},{6,4},{7,5},{8,10},{9,11},{10,... | collective-permute-start | bytes 245768 | tf_op jit(solution)/shard_map/ppermute | solution.py:497
  26.8 18.7 %collective-permute-start.8 = (bf16[1,1,320,128]{3,2,1,0:T(8,128)(2,1)S(1)}, bf16[1,1,320,128]{3,2,1,0:T(8,128)(2,1)S(1)}, u32[]{:S(2)}, u32[]{:S(2)}) collective-permute-start(bf16[1,1,320,128]{3,2,1,0:T(8,128)(2,1)S(1)} %get-tuple-element.64), channel_id=1, source_target_pairs={{0,3},{1,2},{2,1},{3,0},{4,7},{5,6},{6,5},{7,4},{8,11},{9,10},{10,... | collective-permute-start | bytes 245768 | tf_op jit(solution)/shard_map/ppermute | solution.py:497
  29.0 19.0 %collective-permute-start.3 = (bf16[1,1,320,128]{3,2,1,0:T(8,128)(2,1)S(1)}, bf16[1,1,320,128]{3,2,1,0:T(8,128)(2,1)S(1)}, u32[]{:S(2)}, u32[]{:S(2)}) collective-permute-start(bf16[1,1,320,128]{3,2,1,0:T(8,128)(2,1)S(1)} %get-tuple-element.58), channel_id=1, source_target_pairs={{0,1},{1,0},{2,3},{3,2},{4,5},{5,4},{6,7},{7,6},{8,9},{9,8},{10,11... | collective-permute-start | bytes 245768 | tf_op jit(solution)/shard_map/ppermute | solution.py:497
  33.9 14.2 %collective-permute-start.4 = (bf16[1,1,320,128]{3,2,1,0:T(8,128)(2,1)S(1)}, bf16[1,1,320,128]{3,2,1,0:T(8,128)(2,1)S(1)}, u32[]{:S(2)}, u32[]{:S(2)}) collective-permute-start(bf16[1,1,320,128]{3,2,1,0:T(8,128)(2,1)S(1)} %get-tuple-element.59), channel_id=1, source_target_pairs={{0,2},{1,3},{2,0},{3,1},{4,6},{5,7},{6,4},{7,5},{8,10},{9,11},{10,... | collective-permute-start | bytes 245768 | tf_op jit(solution)/shard_map/ppermute | solution.py:497
  35.1 13.0 %collective-permute-start.5 = (bf16[1,1,320,128]{3,2,1,0:T(8,128)(2,1)S(1)}, bf16[1,1,320,128]{3,2,1,0:T(8,128)(2,1)S(1)}, u32[]{:S(2)}, u32[]{:S(2)}) collective-permute-start(bf16[1,1,320,128]{3,2,1,0:T(8,128)(2,1)S(1)} %get-tuple-element.60), channel_id=1, source_target_pairs={{0,3},{1,2},{2,1},{3,0},{4,7},{5,6},{6,5},{7,4},{8,11},{9,10},{10,... | collective-permute-start | bytes 245768 | tf_op jit(solution)/shard_map/ppermute | solution.py:497
  50.5 4.6 %collective-permute-start.22 = (bf16[1040,512]{1,0:T(8,128)(2,1)S(1)}, bf16[1040,512]{1,0:T(8,128)(2,1)S(1)}, u32[]{:S(2)}, u32[]{:S(2)}) collective-permute-start(bf16[1040,512]{1,0:T(8,128)(2,1)S(1)} %get-tuple-element.86.refs_0_.refs_1_.two), channel_id=1, source_target_pairs={{4,5},{6,7},{8,9},{10,11},{12,13},{14,15},{16,17},{18,19},{20,21},... | collective-permute-start | bytes 3194888 | tf_op jit(solution)/shard_map/ppermute | solution.py:500
  51.8 9.5 %collective-permute-start.20 = (bf16[1040,512]{1,0:T(8,128)(2,1)S(1)}, bf16[1040,512]{1,0:T(8,128)(2,1)S(1)}, u32[]{:S(2)}, u32[]{:S(2)}) collective-permute-start(bf16[1040,512]{1,0:T(8,128)(2,1)S(1)} %get-tuple-element.86.refs_0_.refs_1_.two), channel_id=1, source_target_pairs={{2,3}} | collective-permute-start | bytes 3194888 | tf_op jit(solution)/shard_map/ppermute | solution.py:500
  56.2 8.9 %collective-permute-start.26 = (bf16[1040,512]{1,0:T(8,128)(2,1)S(1)}, bf16[1040,512]{1,0:T(8,128)(2,1)S(1)}, u32[]{:S(2)}, u32[]{:S(2)}) collective-permute-start(bf16[1040,512]{1,0:T(8,128)(2,1)S(1)} %join.1.refs_0_.refs_2_), channel_id=1, source_target_pairs={{9,11},{11,9}} | collective-permute-start | bytes 3194888 | tf_op jit(solution)/shard_map/ppermute | solution.py:500
  57.1 15.7 %collective-permute-start.28 = (bf16[1040,512]{1,0:T(8,128)(2,1)S(1)}, bf16[1040,512]{1,0:T(8,128)(2,1)S(1)}, u32[]{:S(2)}, u32[]{:S(2)}) collective-permute-start(bf16[1040,512]{1,0:T(8,128)(2,1)S(1)} %join.1.refs_0_.refs_2_), channel_id=1, source_target_pairs={{13,15},{15,13},{17,19},{19,17},{21,23},{23,21},{25,27},{27,25},{2... | collective-permute-start | bytes 3194888 | tf_op jit(solution)/shard_map/ppermute | solution.py:500
  61.8 0.7 collective-permute-start.21
  63.6 1.3 %collective-permute-start.24 = (f32[1,512]{1,0:T(1,128)S(1)}, f32[1,512]{1,0:T(1,128)S(1)}, u32[]{:S(2)}, u32[]{:S(2)}) collective-permute-start(f32[1,512]{1,0:T(1,128)S(1)} %hop.7), channel_id=1, source_target_pairs={{7,9}} | collective-permute-start | bytes 6152 | tf_op jit(solution)/shard_map/ppermute | solution.py:500
  64.3 0.7 collective-permute-start.25
  65.6 7.3 %collective-permute-start.27 = (f32[1,512]{1,0:T(1,128)S(1)}, f32[1,512]{1,0:T(1,128)S(1)}, u32[]{:S(2)}, u32[]{:S(2)}) collective-permute-start(f32[1,512]{1,0:T(1,128)S(1)} %span_hop.5), channel_id=1, source_target_pairs={{9,13},{11,15}} | collective-permute-start | bytes 6152 | tf_op jit(solution)/shard_map/ppermute | solution.py:500
  75.7 0.7 collective-permute-start.31
  76.9 12.4 %collective-permute-start.32 = (f32[1,512]{1,0:T(1,128)S(1)}, f32[1,512]{1,0:T(1,128)S(1)}, u32[]{:S(2)}, u32[]{:S(2)}) collective-permute-start(f32[1,512]{1,0:T(1,128)S(1)} %span_hop.9), channel_id=1, source_target_pairs={{25,29},{27,31}} | collective-permute-start | bytes 6152 | tf_op jit(solution)/shard_map/ppermute | solution.py:500
  89.4 2.1 %collective-permute-start.33 = (f32[1,512]{1,0:T(1,128)S(1)}, f32[1,512]{1,0:T(1,128)S(1)}, u32[]{:S(2)}, u32[]{:S(2)}) collective-permute-start(f32[1,512]{1,0:T(1,128)S(1)} %lead.1.refs_0_), channel_id=1, source_target_pairs={{1,0},{3,2},{5,4},{7,6},{9,8},{11,10},{13,12},{15,14},{17,16},{19,... | collective-permute-start | bytes 6152 | tf_op jit(solution)/shard_map/ppermute | solution.py:500
  93.4 2.2 %collective-permute-start.34 = (f32[8,128]{1,0:T(8,128)S(1)}, f32[8,128]{1,0:T(8,128)S(1)}, u32[]{:S(2)}, u32[]{:S(2)}) collective-permute-start(f32[8,128]{1,0:T(8,128)S(1)} %get-tuple-element.98), channel_id=1, source_target_pairs={{0,1},{1,0},{2,3},{3,2},{4,5},{5,4},{6,7},{7,6},{8,9},{9,8},{10,11... | collective-permute-start | bytes 12296 | tf_op jit(solution)/shard_map/ppermute | solution.py:497
  93.6 2.8 %collective-permute-start.35 = (f32[8,128]{1,0:T(8,128)S(1)}, f32[8,128]{1,0:T(8,128)S(1)}, u32[]{:S(2)}, u32[]{:S(2)}) collective-permute-start(f32[8,128]{1,0:T(8,128)S(1)} %get-tuple-element.99), channel_id=1, source_target_pairs={{0,2},{1,3},{2,0},{3,1},{4,6},{5,7},{6,4},{7,5},{8,10},{9,11},{10,... | collective-permute-start | bytes 12296 | tf_op jit(solution)/shard_map/ppermute | solution.py:497
  95.4 3.4 %collective-permute-start.36 = (f32[8,128]{1,0:T(8,128)S(1)}, f32[8,128]{1,0:T(8,128)S(1)}, u32[]{:S(2)}, u32[]{:S(2)}) collective-permute-start(f32[8,128]{1,0:T(8,128)S(1)} %get-tuple-element.100), channel_id=1, source_target_pairs={{0,3},{1,2},{2,1},{3,0},{4,7},{5,6},{6,5},{7,4},{8,11},{9,10},{10,... | collective-permute-start | bytes 12296 | tf_op jit(solution)/shard_map/ppermute | solution.py:497
  (14 other events, 94.6 us)

commit v3 on v2

--- a/solution.py
+++ b/solution.py
@@ -136,11 +136,12 @@
 ):
     each = 6 * pairs
     data, small = refs[:parts], refs[parts : 2 * parts]
-    op_ref, values_ref, prior_ref, map_in, vec_in = refs[2 * parts : 2 * parts + 5]
-    elements, offsets, map_ref, vec_ref = refs[2 * parts + 5 : 2 * parts + 9]
-    dyn, gains, source, chosen = refs[2 * parts + 9 :]
+    op_ref, values_ref, prior_ref, before, vec_in = refs[2 * parts : 2 * parts + 5]
+    maps, vec_ref = refs[2 * parts + 5 : 2 * parts + 7]
+    dyn, gains, source, chosen, elements, offsets = refs[2 * parts + 7 :]
     s = s_ref[0]
     ns = parts * pairs * 2 * bs
+    map_in = before.at[before.shape[0] - 1]
     lane = lax.broadcasted_iota(jnp.int32, (bs, 2 * bs), 1)
     left = lane < bs
     zero = jnp.zeros((), BF)
@@ -212,7 +213,7 @@
         shift = shift + jnp.concatenate(
             [source[g, pl.ds(here, 1), :] for g in range(parts * pairs)], axis=1
         )
-        offsets[j] = jnp.broadcast_to(shift, (8, ns))
+        offsets[j : j + 1, :] = shift
         for g in range(parts * pairs):
             rows = slice(g * 2 * bs, (g + 1) * 2 * bs)
             correction = nn(gains[rows, :], masked)
@@ -227,25 +228,26 @@
         vec = vec_in[...]
     for j in range(count):
         element = elements[j]
-        vec = fold(nt(split3(vec), element)) + offsets[j, 0:1, :]
-        held = map_in if j == 0 else map_ref
+        vec = fold(nt(split3(vec), element)) + offsets[j : j + 1, :]
+        held = map_in if j == 0 else maps.at[j - 1]
+        target = maps.at[j]
         for r in range(0, ns, step_of(ns)):
             rows, below = slice(r, r + step_of(ns)), slice(ns + r, ns + r + step_of(ns))
             if first == 0 and j == 0:
                 across = lax.broadcasted_iota(jnp.int32, (step_of(ns), ns), 1)
                 down = lax.broadcasted_iota(jnp.int32, (step_of(ns), ns), 0) + r
                 unit = jnp.where(across == down, 1.0, 0.0).astype(BF)
-                map_ref[rows, :] = nt(unit, element).astype(BF)
-                map_ref[below, :] = jnp.zeros((step_of(ns), ns), BF)
+                target[rows, :] = nt(unit, element).astype(BF)
+                target[below, :] = jnp.zeros((step_of(ns), ns), BF)
                 continue
             moved = nt(held[rows, :], element)
             if first > 0 or j > 1:
                 moved = moved + nt(held[below, :], element)
             top = moved.astype(BF)
-            map_ref[rows, :] = top
-            map_ref[below, :] = (moved - top.astype(F32)).astype(BF)
+            target[rows, :] = top
+            target[below, :] = (moved - top.astype(F32)).astype(BF)
+        target[2 * ns :, :] = split3(vec)
     vec_ref[...] = vec
-    map_ref[2 * ns :, :] = split3(vec)
 
 
 def chunk_piece(
@@ -263,18 +265,18 @@
             num_scalar_prefetch=3,
             grid=(),
             in_specs=vmem(2 * parts + 5),
-            out_specs=vmem(4),
+            out_specs=vmem(2),
             scratch_shapes=[
                 pltpu.VMEM((parts * pairs, ns, width), BF),
                 pltpu.VMEM((ns, width), BF),
                 pltpu.VMEM((parts * pairs, chunk, width), F32),
                 pltpu.VMEM((width, ns), BF),
+                pltpu.VMEM((count, ns, ns), BF),
+                pltpu.VMEM((8, ns), F32),
             ],
         ),
         out_shape=[
-            jax.ShapeDtypeStruct((count, ns, ns), BF),
-            jax.ShapeDtypeStruct((count, 8, ns), F32),
-            jax.ShapeDtypeStruct((2 * ns + ROWS, ns), BF),
+            jax.ShapeDtypeStruct((count, 2 * ns + ROWS, ns), BF),
             jax.ShapeDtypeStruct((1, ns), F32),
         ],
         compiler_params=pltpu.CompilerParams(vmem_limit_bytes=VMEM_LIMIT),
@@ -360,6 +362,28 @@
     )(position, row, *maps)
 
 
+def span_join_kernel(s_ref, own, far, out_ref):
+    @pl.when(s_ref[0] // 2 == 0)
+    def _():
+        join_kernel(own, far, out_ref)
+
+    @pl.when(s_ref[0] // 2 == 1)
+    def _():
+        join_kernel(far, own, out_ref)
+
+
+def span_join(position, own, far):
+    return pl.pallas_call(
+        span_join_kernel,
+        grid_spec=pltpu.PrefetchScalarGridSpec(
+            num_scalar_prefetch=1, grid=(), in_specs=vmem(2), out_specs=vmem(1)[0]
+        ),
+        out_shape=jax.ShapeDtypeStruct(own.shape, BF),
+        compiler_params=pltpu.CompilerParams(vmem_limit_bytes=VMEM_LIMIT),
+        name="span_join",
+    )(position, own, far)
+
+
 def lead_kernel(leaders, early, s_ref, tm_ref, row_ref, direct_ref, *refs):
     sets, out_ref = (refs[:leaders], refs[leaders : 2 * leaders]), refs[2 * leaders]
 
@@ -396,17 +420,14 @@
 
 
 def sweep_kernel(pieces, parts, s_ref, tm_ref, *refs):
-    own_ref, told_ref, prior_ref, first_map, first_vec, map_ref = refs[:6]
-    refs = refs[6:]
-    elements, offsets = refs[:pieces], refs[pieces : 2 * pieces]
-    outs = refs[2 * pieces : 2 * pieces + parts]
-    current_ref, spread = refs[2 * pieces + parts :]
+    own_ref, told_ref, first_map, first_vec, map_ref = refs[:5]
+    stages, outs = refs[5 : 5 + pieces], refs[5 + pieces : 5 + pieces + parts]
+    current_ref, spread = refs[5 + pieces + parts :]
     s = s_ref[0]
-    begin = jnp.logical_and(s == 0, tm_ref[0] == 0)
 
     @pl.when(s % 2 == 0)
     def _():
-        current_ref[...] = told_ref[...] + jnp.where(begin, prior_ref[...], 0.0)
+        current_ref[...] = told_ref[...]
 
     @pl.when(jnp.logical_and(s % 2 == 1, tm_ref[0] == 0))
     def _():
@@ -416,30 +437,30 @@
     def _():
         current_ref[...] = apply_map(own_ref[...], map_ref)
 
-    current = current_ref[...]
+    entry = current_ref[...]
     at = 0
     width = spread.shape[2]
     for p in range(pieces):
-        for j in range(elements[p].shape[0]):
-            current = fold(nt(split3(current), elements[p][j])) + offsets[p][j, 0:1, :]
+        for j in range(stages[p].shape[0]):
+            mean = apply_map(entry, stages[p].at[j])
             for d in range(parts):
-                spread[d, at : at + 1, :] = current[:, d * width : (d + 1) * width]
+                spread[d, at : at + 1, :] = mean[:, d * width : (d + 1) * width]
             at += 1
     for d in range(parts):
         outs[d][...] = spread[s ^ d]
 
 
-def sweep(position, span, own, told, prior, even, elements, offsets, parts):
+def sweep(position, span, own, told, even, stages, parts):
     ns = own.shape[1]
-    pieces = len(elements)
-    chunk = sum(e.shape[0] for e in elements)
+    pieces = len(stages)
+    chunk = sum(x.shape[0] for x in stages)
     width = ns // parts
     return pl.pallas_call(
         functools.partial(sweep_kernel, pieces, parts),
         grid_spec=pltpu.PrefetchScalarGridSpec(
             num_scalar_prefetch=2,
             grid=(),
-            in_specs=vmem(6 + 2 * pieces),
+            in_specs=vmem(5 + pieces),
             out_specs=vmem(parts),
             scratch_shapes=[
                 pltpu.VMEM((1, ns), F32),
@@ -449,7 +470,7 @@
         out_shape=[jax.ShapeDtypeStruct((chunk, width), F32)] * parts,
         compiler_params=pltpu.CompilerParams(vmem_limit_bytes=VMEM_LIMIT),
         name="sweep",
-    )(position, span, own, told, prior, *even, *elements, *offsets)
+    )(position, span, own, told, *even, *stages)
 
 
 def gather_kernel(parts, s_ref, *refs):
@@ -521,15 +542,14 @@
 
     plan = plan_of(small, obs_blocks.T, obs_counts.reshape(1, steps), chunk)
     state = None
-    elements, offsets = [], []
+    stages = []
     for first, size, data in zip(firsts, sizes, pieces):
-        element, offset, *state = chunk_piece(
-            position, span, plan, data, small, obs_op, obs_values,
-            prior_row, state, chunk, first, size,
+        state = chunk_piece(
+            position, span, plan, data, small, obs_op, obs_values, prior_row, state, chunk, first, size
         )
-        elements.append(element)
-        offsets.append(offset)
-    chunk_map, vec = state
+        stages.append(state[0])
+    vec = state[1]
+    chunk_map = state[0].reshape(state[0].shape[1:])
 
     leads = [2 * p + 1 for p in range(parts // 2)]
     to_lead = [((a, l - 1), (a, l)) for a in range(spans) for l in leads]
@@ -563,15 +583,19 @@
                 entry = entry + send(current, [((g, leads[-1]), (g + 1, l))])
 
     arriving = entry
+    joined = span_join(position, *maps_late) if len(leads) == 2 else None
     for h in range(early, spans - 1):
-        current = span_hop(position, arriving, maps if h == early else maps_late)
+        if h < early + 2 or joined is None:
+            current = span_hop(position, arriving, maps if h == early else maps_late)
+        else:
+            current = hop(arriving, joined)
         arriving = send(current, [((h, l), (h + 1, l)) for l in leads])
         entry = entry + arriving
 
     own = lead(position, span, entry, direct, maps, maps_late, early)
     told = send(own, [(b, a) for a, b in to_lead])
     mine = sweep(
-        position, span, own, told, prior_row, (first_map, first_vec, map_even), elements, offsets, parts,
+        position, span, own, told, (first_map, first_vec, map_even), stages, parts
     )
     got = {0: mine[0]}
     for d in order:

time: 99.6 us -> 97.5 us (0.979)
  waiting for transfers between devices: 41.4 us -> 39.3 us
    ppermute x21, waiting for transfers between devices: 20.4 us -> 17.9 us  [across(): return lax.ppermute(x, 'state', [(i, i ^ d) for i in range(parts)])]
    pallas_call x5 -> x2, Pallas kernels: 2.57 us -> 1.02 us  [span_hop(): pl.pallas_call(functools.partial(span_kernel, leaders), grid_spec=pltpu.P...]
    pallas_call x0 -> x1, Pallas kernels: none -> 1.12 us  [span_join(): pl.pallas_call(span_join_kernel, grid_spec=pltpu.PrefetchScalarGridSpec(n...]
    pallas_call x4 -> x7, Pallas kernels: 1.27 us -> 2.05 us  [hop(): pl.pallas_call(hop_kernel, in_specs=vmem(1 + len(maps)), out_specs=vmem(1...]
  transfers between devices with their start and end apart: 37 -> 37, of which waited for: 14 -> 14; matrix products, arithmetic and copies ran while one was open for 0% -> 0% of each run, Pallas kernels for 16% -> 18%
where the time goes in v3:
time: 97.5 us; the launch traced here: 97.1 us
  waiting for transfers between devices  39.3 us (40%)
  starting transfers between devices  32.4 us (33%)
  Pallas kernels  24.8 us (25%)
    ppermute x16, waiting for transfers between devices, send(): lax.ppermute(x, ('tm', 'state'), [(a * parts + b, c * parts + e) for (a,...  21.4 us
    ppermute x21, waiting for transfers between devices, across(): return lax.ppermute(x, 'state', [(i, i ^ d) for i in range(parts)])  17.9 us
    ppermute x21, starting transfers between devices, across(): return lax.ppermute(x, 'state', [(i, i ^ d) for i in range(parts)])  17.6 us
    pallas_call x5, Pallas kernels, chunk_piece(): pl.pallas_call(functools.partial(chunk_kernel, parts, pairs, bs, chunk, f...  15.2 us
    ppermute x16, starting transfers between devices, send(): lax.ppermute(x, ('tm', 'state'), [(a * parts + b, c * parts + e) for (a,...  14.8 us
    pallas_call x5, Pallas kernels, pack(): pl.pallas_call(functools.partial(pack_kernel, parts, pairs, bs, chunk, bo...  2.16 us
    pallas_call x7, Pallas kernels, hop(): pl.pallas_call(hop_kernel, in_specs=vmem(1 + len(maps)), out_specs=vmem(1...  2.05 us
  transfers between devices with their start and end apart: 37, of which 14 were waited for; matrix products, arithmetic and copies ran while one was open for 0% of the time, Pallas kernels for 18%

profile of v3, /device:TPU:27, one launch (start us, length us, event | category | flops | bytes accessed | tf_op | source)
XLA Modules:
  0.0 97.1 jit_solution(13624672984516048670)
XLA Ops:
  0.0 1.5 %shard_map.95 = (bf16[2,1,320,128]{3,2,1,0:T(8,128)(2,1)S(1)}, bf16[2,1,320,128]{3,2,1,0:T(8,128)(2,1)S(1)}, bf16[2,1,320,128]{3,2,1,0:T(8,128)(2,1)S(1)}, bf16[2,1,320,128]{3,2,1,0:T(8,128)(2,1)S(1)}) custom-call(s32[1]{0:T(128)} %bitcast.s_ref, s32[1]{0:T(128)} %bitcast.1.tm_ref, bf16[32,2,64,192]{3,2,1,0:T(8,128)(2,1)} %refs_3_.9, ...), custom_call_target="tpu_custom_call" | custom-call | tf_op jit(solution)/shard_map/pallas_call | solution.py:95
  2.2 1.2 %collective-permute-start.16 = (bf16[2,1,320,128]{3,2,1,0:T(8,128)(2,1)S(1)}, bf16[2,1,320,128]{3,2,1,0:T(8,128)(2,1)S(1)}, u32[]{:S(2)}, u32[]{:S(2)}) collective-permute-start(bf16[2,1,320,128]{3,2,1,0:T(8,128)(2,1)S(1)} %get-tuple-element.65), channel_id=1, source_target_pairs={{0,2},{1,3},{2,0},{3,1},{4,6},{5,7},{6,4},{7,5},{8,10},{9,11},{10,... | collective-permute-start | bytes 491528 | tf_op jit(solution)/shard_map/ppermute | solution.py:518
  5.9 1.2 %collective-permute-start.1 = (f32[14,128]{1,0:T(8,128)S(1)}, f32[14,128]{1,0:T(8,128)S(1)}, u32[]{:S(2)}, u32[]{:S(2)}) collective-permute-start(f32[14,128]{1,0:T(8,128)S(1)} %get-tuple-element.45), channel_id=1, source_target_pairs={{0,2},{1,3},{2,0},{3,1},{4,6},{5,7},{6,4},{7,5},{8,10},{9,11},{10,... | collective-permute-start | bytes 21512 | tf_op jit(solution)/shard_map/ppermute | solution.py:518
  7.2 4.3 %collective-permute-done.1.refs_2_.refs_6_ = f32[14,128]{1,0:T(8,128)S(1)} collective-permute-done((f32[14,128]{1,0:T(8,128)S(1)}, f32[14,128]{1,0:T(8,128)S(1)}, u32[]{:S(2)}, u32[]{:S(2)}) %collective-permute-start.1) | collective-permute-done | bytes 7200 | tf_op jit(solution)/shard_map/ppermute | solution.py:518
  11.4 2.2 %collective-permute-start.2 = (f32[14,128]{1,0:T(8,128)S(1)}, f32[14,128]{1,0:T(8,128)S(1)}, u32[]{:S(2)}, u32[]{:S(2)}) collective-permute-start(f32[14,128]{1,0:T(8,128)S(1)} %get-tuple-element.46), channel_id=1, source_target_pairs={{0,3},{1,2},{2,1},{3,0},{4,7},{5,6},{6,5},{7,4},{8,11},{9,10},{10,... | collective-permute-start | bytes 21512 | tf_op jit(solution)/shard_map/ppermute | solution.py:518
  13.8 1.5 %collective-permute-done.2.refs_3_.refs_7_ = f32[14,128]{1,0:T(8,128)S(1)} collective-permute-done((f32[14,128]{1,0:T(8,128)S(1)}, f32[14,128]{1,0:T(8,128)S(1)}, u32[]{:S(2)}, u32[]{:S(2)}) %collective-permute-start.2) | collective-permute-done | bytes 7200 | tf_op jit(solution)/shard_map/ppermute | solution.py:518
  15.6 0.9 collective-permute-done.6.refs_1_
  16.6 1.2 %collective-permute-start.10 = (bf16[2,1,320,128]{3,2,1,0:T(8,128)(2,1)S(1)}, bf16[2,1,320,128]{3,2,1,0:T(8,128)(2,1)S(1)}, u32[]{:S(2)}, u32[]{:S(2)}) collective-permute-start(bf16[2,1,320,128]{3,2,1,0:T(8,128)(2,1)S(1)} %get-tuple-element.57), channel_id=1, source_target_pairs={{0,2},{1,3},{2,0},{3,1},{4,6},{5,7},{6,4},{7,5},{8,10},{9,11},{10,... | collective-permute-start | bytes 491528 | tf_op jit(solution)/shard_map/ppermute | solution.py:518
  18.6 1.3 %collective-permute-start.13 = (bf16[2,1,320,128]{3,2,1,0:T(8,128)(2,1)S(1)}, bf16[2,1,320,128]{3,2,1,0:T(8,128)(2,1)S(1)}, u32[]{:S(2)}, u32[]{:S(2)}) collective-permute-start(bf16[2,1,320,128]{3,2,1,0:T(8,128)(2,1)S(1)} %get-tuple-element.61), channel_id=1, source_target_pairs={{0,2},{1,3},{2,0},{3,1},{4,6},{5,7},{6,4},{7,5},{8,10},{9,11},{10,... | collective-permute-start | bytes 491528 | tf_op jit(solution)/shard_map/ppermute | solution.py:518
  20.9 1.1 %collective-permute-done.10.refs_2_ = bf16[2,1,320,128]{3,2,1,0:T(8,128)(2,1)S(1)} collective-permute-done((bf16[2,1,320,128]{3,2,1,0:T(8,128)(2,1)S(1)}, bf16[2,1,320,128]{3,2,1,0:T(8,128)(2,1)S(1)}, u32[]{:S(2)}, u32[]{:S(2)}) %collective-permute-start.10) | collective-permute-done | bytes 163872 | tf_op jit(solution)/shard_map/ppermute | solution.py:518
  22.0 1.2 %collective-permute-start.7 = (bf16[1,1,320,128]{3,2,1,0:T(8,128)(2,1)S(1)}, bf16[1,1,320,128]{3,2,1,0:T(8,128)(2,1)S(1)}, u32[]{:S(2)}, u32[]{:S(2)}) collective-permute-start(bf16[1,1,320,128]{3,2,1,0:T(8,128)(2,1)S(1)} %get-tuple-element.53), channel_id=1, source_target_pairs={{0,2},{1,3},{2,0},{3,1},{4,6},{5,7},{6,4},{7,5},{8,10},{9,11},{10,... | collective-permute-start | bytes 245768 | tf_op jit(solution)/shard_map/ppermute | solution.py:518
  23.2 3.6 %collective-permute-done.11.refs_3_ = bf16[2,1,320,128]{3,2,1,0:T(8,128)(2,1)S(1)} collective-permute-done((bf16[2,1,320,128]{3,2,1,0:T(8,128)(2,1)S(1)}, bf16[2,1,320,128]{3,2,1,0:T(8,128)(2,1)S(1)}, u32[]{:S(2)}, u32[]{:S(2)}) %collective-permute-start.11) | collective-permute-done | bytes 163872 | tf_op jit(solution)/shard_map/ppermute | solution.py:518
  27.0 1.4 %collective-permute-start.3 = (bf16[1,1,320,128]{3,2,1,0:T(8,128)(2,1)S(1)}, bf16[1,1,320,128]{3,2,1,0:T(8,128)(2,1)S(1)}, u32[]{:S(2)}, u32[]{:S(2)}) collective-permute-start(bf16[1,1,320,128]{3,2,1,0:T(8,128)(2,1)S(1)} %get-tuple-element.48), channel_id=1, source_target_pairs={{0,1},{1,0},{2,3},{3,2},{4,5},{5,4},{6,7},{7,6},{8,9},{9,8},{10,11... | collective-permute-start | bytes 245768 | tf_op jit(solution)/shard_map/ppermute | solution.py:518
  29.0 1.2 %collective-permute-start.4 = (bf16[1,1,320,128]{3,2,1,0:T(8,128)(2,1)S(1)}, bf16[1,1,320,128]{3,2,1,0:T(8,128)(2,1)S(1)}, u32[]{:S(2)}, u32[]{:S(2)}) collective-permute-start(bf16[1,1,320,128]{3,2,1,0:T(8,128)(2,1)S(1)} %get-tuple-element.49), channel_id=1, source_target_pairs={{0,2},{1,3},{2,0},{3,1},{4,6},{5,7},{6,4},{7,5},{8,10},{9,11},{10,... | collective-permute-start | bytes 245768 | tf_op jit(solution)/shard_map/ppermute | solution.py:518
  30.2 3.6 %collective-permute-done.14.refs_3_ = bf16[2,1,320,128]{3,2,1,0:T(8,128)(2,1)S(1)} collective-permute-done((bf16[2,1,320,128]{3,2,1,0:T(8,128)(2,1)S(1)}, bf16[2,1,320,128]{3,2,1,0:T(8,128)(2,1)S(1)}, u32[]{:S(2)}, u32[]{:S(2)}) %collective-permute-start.14) | collective-permute-done | bytes 163872 | tf_op jit(solution)/shard_map/ppermute | solution.py:518
  34.0 3.1 %shard_map.96 = (bf16[2,1040,512]{2,1,0:T(8,128)(2,1)S(1)}, f32[1,512]{1,0:T(1,128)S(1)}) custom-call(s32[1]{0:T(128)} %bitcast.s_ref, s32[1]{0:T(128)} %bitcast.1.tm_ref, s32[27,32]{1,0:T(8,128)S(1)} %plan.1.plan_ref, bf16[2,1,320,128]{3,2,1,0:T(8,128)(2,1)S(1)} %get-tuple-element.63.refs_0_.refs_11_, ...), custom_call_target="tpu_custom_call" | custom-call | tf_op jit(solution)/shard_map/pallas_call | solution.py:262
  37.1 3.6 %shard_map.97 = (bf16[2,1040,512]{2,1,0:T(8,128)(2,1)S(1)}, f32[1,512]{1,0:T(1,128)S(1)}) custom-call(s32[1]{0:T(128)} %bitcast.s_ref, s32[1]{0:T(128)} %bitcast.1.tm_ref, s32[27,32]{1,0:T(8,128)S(1)} %plan.1.plan_ref, bf16[2,1,320,128]{3,2,1,0:T(8,128)(2,1)S(1)} %get-tuple-element.59.refs_0_, bf16[2,1,320,128]{3,2,1,0:T(8,128)(2,1)S(1)} %collective-permute-done.12.refs_1_, ...), custom_call_target="tpu_custom_call" | custom-call | tf_op jit(solution)/shard_map/pallas_call | solution.py:262
  40.8 3.6 %shard_map.98 = (bf16[2,1040,512]{2,1,0:T(8,128)(2,1)S(1)}, f32[1,512]{1,0:T(1,128)S(1)}) custom-call(s32[1]{0:T(128)} %bitcast.s_ref, s32[1]{0:T(128)} %bitcast.1.tm_ref, s32[27,32]{1,0:T(8,128)S(1)} %plan.1.plan_ref, bf16[2,1,320,128]{3,2,1,0:T(8,128)(2,1)S(1)} %get-tuple-element.55.refs_0_, bf16[2,1,320,128]{3,2,1,0:T(8,128)(2,1)S(1)} %collective-permute-done.9.refs_1_, ...), custom_call_target="tpu_custom_call" | custom-call | tf_op jit(solution)/shard_map/pallas_call | solution.py:262
  44.4 2.4 %shard_map.99 = (bf16[1,1040,512]{2,1,0:T(8,128)(2,1)S(1)}, f32[1,512]{1,0:T(1,128)S(1)}) custom-call(s32[1]{0:T(128)} %bitcast.s_ref, s32[1]{0:T(128)} %bitcast.1.tm_ref, s32[27,32]{1,0:T(8,128)S(1)} %plan.1.plan_ref, bf16[1,1,320,128]{3,2,1,0:T(8,128)(2,1)S(1)} %get-tuple-element.51.refs_0_, bf16[1,1,320,128]{3,2,1,0:T(8,128)(2,1)S(1)} %collective-permute-done.6.refs_1_, ...), custom_call_target="tpu_custom_call" | custom-call | tf_op jit(solution)/shard_map/pallas_call | solution.py:262
  46.9 2.4 %shard_map.100 = (bf16[1,1040,512]{2,1,0:T(8,128)(2,1)S(1)}, f32[1,512]{1,0:T(1,128)S(1)}) custom-call(s32[1]{0:T(128)} %bitcast.s_ref, s32[1]{0:T(128)} %bitcast.1.tm_ref, s32[27,32]{1,0:T(8,128)S(1)} %plan.1.plan_ref, bf16[1,1,320,128]{3,2,1,0:T(8,128)(2,1)S(1)} %get-tuple-element.47.refs_0_, bf16[1,1,320,128]{3,2,1,0:T(8,128)(2,1)S(1)} %collective-permute-done.3.refs_1_, ...), custom_call_target="tpu_custom_call" | custom-call | tf_op jit(solution)/shard_map/pallas_call | solution.py:262
  49.3 1.3 %collective-permute-start.22 = (bf16[1040,512]{1,0:T(8,128)(2,1)S(1)}, bf16[1040,512]{1,0:T(8,128)(2,1)S(1)}, u32[]{:S(2)}, u32[]{:S(2)}) collective-permute-start(bf16[1040,512]{1,0:T(8,128)(2,1)S(1)} %bitcast.7), channel_id=1, source_target_pairs={{4,5},{6,7},{8,9},{10,11},{12,13},{14,15},{16,17},{18,19},{20,21},... | collective-permute-start | bytes 3194888 | tf_op jit(solution)/shard_map/ppermute | solution.py:521
  51.3 2.9 %collective-permute-done.22.one.refs_4_ = bf16[1040,512]{1,0:T(8,128)(2,1)S(1)} collective-permute-done((bf16[1040,512]{1,0:T(8,128)(2,1)S(1)}, bf16[1040,512]{1,0:T(8,128)(2,1)S(1)}, u32[]{:S(2)}, u32[]{:S(2)}) %collective-permute-start.22) | collective-permute-done | bytes 1064992 | tf_op jit(solution)/shard_map/ppermute | solution.py:521
  54.2 1.1 %join.1.refs_0_.own.refs_2_ = bf16[1040,512]{1,0:T(8,128)(2,1)S(1)} custom-call(bf16[1040,512]{1,0:T(8,128)(2,1)S(1)} %collective-permute-done.22.one.refs_4_, bf16[1040,512]{1,0:T(8,128)(2,1)S(1)} %bitcast.9), custom_call_target="tpu_custom_call" | custom-call | tf_op jit(solution)/shard_map/join/pallas_call | solution.py:309
  56.2 2.6 %collective-permute-start.28 = (bf16[1040,512]{1,0:T(8,128)(2,1)S(1)}, bf16[1040,512]{1,0:T(8,128)(2,1)S(1)}, u32[]{:S(2)}, u32[]{:S(2)}) collective-permute-start(bf16[1040,512]{1,0:T(8,128)(2,1)S(1)} %join.1.refs_0_.own.refs_2_), channel_id=1, source_target_pairs={{13,15},{15,13},{17,19},{19,17},{21,23},{23,21},{25,27},{27,25},{2... | collective-permute-start | bytes 3194888 | tf_op jit(solution)/shard_map/ppermute | solution.py:521
  65.5 6.5 %collective-permute-done.28.refs_1_.far.refs_3_ = bf16[1040,512]{1,0:T(8,128)(2,1)S(1)} collective-permute-done((bf16[1040,512]{1,0:T(8,128)(2,1)S(1)}, bf16[1040,512]{1,0:T(8,128)(2,1)S(1)}, u32[]{:S(2)}, u32[]{:S(2)}) %collective-permute-start.28) | collective-permute-done | bytes 1064992 | tf_op jit(solution)/shard_map/ppermute | solution.py:521
  73.2 1.1 %span_join.1.refs_0_ = bf16[1040,512]{1,0:T(8,128)(2,1)S(1)} custom-call(s32[1]{0:T(128)} %bitcast.s_ref, bf16[1040,512]{1,0:T(8,128)(2,1)S(1)} %join.1.refs_0_.own.refs_2_, bf16[1040,512]{1,0:T(8,128)(2,1)S(1)} %collective-permute-done.28.refs_1_.far.refs_3_), custom_call_target="tpu_custom_call" | custom-call | tf_op jit(solution)/shard_map/span_join/pallas_call | solution.py:376
  76.5 1.3 %collective-permute-start.32 = (f32[1,512]{1,0:T(1,128)S(1)}, f32[1,512]{1,0:T(1,128)S(1)}, u32[]{:S(2)}, u32[]{:S(2)}) collective-permute-start(f32[1,512]{1,0:T(1,128)S(1)} %hop.13), channel_id=1, source_target_pairs={{25,29},{27,31}} | collective-permute-start | bytes 6152 | tf_op jit(solution)/shard_map/ppermute | solution.py:521
  77.8 11.2 %collective-permute-done.32 = f32[1,512]{1,0:T(1,128)S(1)} collective-permute-done((f32[1,512]{1,0:T(1,128)S(1)}, f32[1,512]{1,0:T(1,128)S(1)}, u32[]{:S(2)}, u32[]{:S(2)}) %collective-permute-start.32) | collective-permute-done | bytes 2080 | tf_op jit(solution)/shard_map/ppermute | solution.py:521
  89.1 1.3 %collective-permute-start.33 = (f32[1,512]{1,0:T(1,128)S(1)}, f32[1,512]{1,0:T(1,128)S(1)}, u32[]{:S(2)}, u32[]{:S(2)}) collective-permute-start(f32[1,512]{1,0:T(1,128)S(1)} %lead.1.refs_0_), channel_id=1, source_target_pairs={{1,0},{3,2},{5,4},{7,6},{9,8},{11,10},{13,12},{15,14},{17,16},{19,... | collective-permute-start | bytes 6152 | tf_op jit(solution)/shard_map/ppermute | solution.py:521
  91.2 1.5 %sweep.1 = (f32[8,128]{1,0:T(8,128)S(1)}, f32[8,128]{1,0:T(8,128)S(1)}, f32[8,128]{1,0:T(8,128)S(1)}, f32[8,128]{1,0:T(8,128)S(1)}) custom-call(s32[1]{0:T(128)} %bitcast.s_ref, s32[1]{0:T(128)} %bitcast.1.tm_ref, f32[1,512]{1,0:T(1,128)S(1)} %lead.1.refs_0_, f32[1,512]{1,0:T(1,128)S(1)} %collective-permute-done.33.refs_1_, ...), custom_call_target="tpu_custom_call" | custom-call | tf_op jit(solution)/shard_map/sweep/pallas_call | solution.py:458
  92.8 2.0 %collective-permute-start.36 = (f32[8,128]{1,0:T(8,128)S(1)}, f32[8,128]{1,0:T(8,128)S(1)}, u32[]{:S(2)}, u32[]{:S(2)}) collective-permute-start(f32[8,128]{1,0:T(8,128)S(1)} %get-tuple-element.80), channel_id=1, source_target_pairs={{0,3},{1,2},{2,1},{3,0},{4,7},{5,6},{6,5},{7,4},{8,11},{9,10},{10,... | collective-permute-start | bytes 12296 | tf_op jit(solution)/shard_map/ppermute | solution.py:518
  95.3 1.2 %collective-permute-done.36.refs_3_ = f32[8,128]{1,0:T(8,128)S(1)} collective-permute-done((f32[8,128]{1,0:T(8,128)S(1)}, f32[8,128]{1,0:T(8,128)S(1)}, u32[]{:S(2)}, u32[]{:S(2)}) %collective-permute-start.36) | collective-permute-done | bytes 4128 | tf_op jit(solution)/shard_map/ppermute | solution.py:518
  (88 shorter events, 19.8 us)
Async XLA Ops:
  1.5 16.3 %collective-permute-start.15 = (bf16[2,1,320,128]{3,2,1,0:T(8,128)(2,1)S(1)}, bf16[2,1,320,128]{3,2,1,0:T(8,128)(2,1)S(1)}, u32[]{:S(2)}, u32[]{:S(2)}) collective-permute-start(bf16[2,1,320,128]{3,2,1,0:T(8,128)(2,1)S(1)} %get-tuple-element.64), channel_id=1, source_target_pairs={{0,1},{1,0},{2,3},{3,2},{4,5},{5,4},{6,7},{7,6},{8,9},{9,8},{10,11... | collective-permute-start | bytes 491528 | tf_op jit(solution)/shard_map/ppermute | solution.py:518
  2.2 16.3 %collective-permute-start.16 = (bf16[2,1,320,128]{3,2,1,0:T(8,128)(2,1)S(1)}, bf16[2,1,320,128]{3,2,1,0:T(8,128)(2,1)S(1)}, u32[]{:S(2)}, u32[]{:S(2)}) collective-permute-start(bf16[2,1,320,128]{3,2,1,0:T(8,128)(2,1)S(1)} %get-tuple-element.65), channel_id=1, source_target_pairs={{0,2},{1,3},{2,0},{3,1},{4,6},{5,7},{6,4},{7,5},{8,10},{9,11},{10,... | collective-permute-start | bytes 491528 | tf_op jit(solution)/shard_map/ppermute | solution.py:518
  3.5 15.1 %collective-permute-start.17 = (bf16[2,1,320,128]{3,2,1,0:T(8,128)(2,1)S(1)}, bf16[2,1,320,128]{3,2,1,0:T(8,128)(2,1)S(1)}, u32[]{:S(2)}, u32[]{:S(2)}) collective-permute-start(bf16[2,1,320,128]{3,2,1,0:T(8,128)(2,1)S(1)} %get-tuple-element.66), channel_id=1, source_target_pairs={{0,3},{1,2},{2,1},{3,0},{4,7},{5,6},{6,5},{7,4},{8,11},{9,10},{10,... | collective-permute-start | bytes 491528 | tf_op jit(solution)/shard_map/ppermute | solution.py:518
  4.2 15.7 %collective-permute-start.9 = (bf16[2,1,320,128]{3,2,1,0:T(8,128)(2,1)S(1)}, bf16[2,1,320,128]{3,2,1,0:T(8,128)(2,1)S(1)}, u32[]{:S(2)}, u32[]{:S(2)}) collective-permute-start(bf16[2,1,320,128]{3,2,1,0:T(8,128)(2,1)S(1)} %get-tuple-element.56), channel_id=1, source_target_pairs={{0,1},{1,0},{2,3},{3,2},{4,5},{5,4},{6,7},{7,6},{8,9},{9,8},{10,11... | collective-permute-start | bytes 491528 | tf_op jit(solution)/shard_map/ppermute | solution.py:518
  4.7 1.3 %collective-permute-start = (f32[14,128]{1,0:T(8,128)S(1)}, f32[14,128]{1,0:T(8,128)S(1)}, u32[]{:S(2)}, u32[]{:S(2)}) collective-permute-start(f32[14,128]{1,0:T(8,128)S(1)} %get-tuple-element.44), channel_id=1, source_target_pairs={{0,1},{1,0},{2,3},{3,2},{4,5},{5,4},{6,7},{7,6},{8,9},{9,8},{10,11... | collective-permute-start | bytes 21512 | tf_op jit(solution)/shard_map/ppermute | solution.py:518
  5.9 5.5 %collective-permute-start.1 = (f32[14,128]{1,0:T(8,128)S(1)}, f32[14,128]{1,0:T(8,128)S(1)}, u32[]{:S(2)}, u32[]{:S(2)}) collective-permute-start(f32[14,128]{1,0:T(8,128)S(1)} %get-tuple-element.45), channel_id=1, source_target_pairs={{0,2},{1,3},{2,0},{3,1},{4,6},{5,7},{6,4},{7,5},{8,10},{9,11},{10,... | collective-permute-start | bytes 21512 | tf_op jit(solution)/shard_map/ppermute | solution.py:518
  11.4 3.8 %collective-permute-start.2 = (f32[14,128]{1,0:T(8,128)S(1)}, f32[14,128]{1,0:T(8,128)S(1)}, u32[]{:S(2)}, u32[]{:S(2)}) collective-permute-start(f32[14,128]{1,0:T(8,128)S(1)} %get-tuple-element.46), channel_id=1, source_target_pairs={{0,3},{1,2},{2,1},{3,0},{4,7},{5,6},{6,5},{7,4},{8,11},{9,10},{10,... | collective-permute-start | bytes 21512 | tf_op jit(solution)/shard_map/ppermute | solution.py:518
  15.2 1.3 %collective-permute-start.6 = (bf16[1,1,320,128]{3,2,1,0:T(8,128)(2,1)S(1)}, bf16[1,1,320,128]{3,2,1,0:T(8,128)(2,1)S(1)}, u32[]{:S(2)}, u32[]{:S(2)}) collective-permute-start(bf16[1,1,320,128]{3,2,1,0:T(8,128)(2,1)S(1)} %get-tuple-element.52), channel_id=1, source_target_pairs={{0,1},{1,0},{2,3},{3,2},{4,5},{5,4},{6,7},{7,6},{8,9},{9,8},{10,11... | collective-permute-start | bytes 245768 | tf_op jit(solution)/shard_map/ppermute | solution.py:518
  16.6 5.4 %collective-permute-start.10 = (bf16[2,1,320,128]{3,2,1,0:T(8,128)(2,1)S(1)}, bf16[2,1,320,128]{3,2,1,0:T(8,128)(2,1)S(1)}, u32[]{:S(2)}, u32[]{:S(2)}) collective-permute-start(bf16[2,1,320,128]{3,2,1,0:T(8,128)(2,1)S(1)} %get-tuple-element.57), channel_id=1, source_target_pairs={{0,2},{1,3},{2,0},{3,1},{4,6},{5,7},{6,4},{7,5},{8,10},{9,11},{10,... | collective-permute-start | bytes 491528 | tf_op jit(solution)/shard_map/ppermute | solution.py:518
  17.8 9.0 %collective-permute-start.11 = (bf16[2,1,320,128]{3,2,1,0:T(8,128)(2,1)S(1)}, bf16[2,1,320,128]{3,2,1,0:T(8,128)(2,1)S(1)}, u32[]{:S(2)}, u32[]{:S(2)}) collective-permute-start(bf16[2,1,320,128]{3,2,1,0:T(8,128)(2,1)S(1)} %get-tuple-element.58), channel_id=1, source_target_pairs={{0,3},{1,2},{2,1},{3,0},{4,7},{5,6},{6,5},{7,4},{8,11},{9,10},{10,... | collective-permute-start | bytes 491528 | tf_op jit(solution)/shard_map/ppermute | solution.py:518
  18.6 8.4 %collective-permute-start.12 = (bf16[2,1,320,128]{3,2,1,0:T(8,128)(2,1)S(1)}, bf16[2,1,320,128]{3,2,1,0:T(8,128)(2,1)S(1)}, u32[]{:S(2)}, u32[]{:S(2)}) collective-permute-start(bf16[2,1,320,128]{3,2,1,0:T(8,128)(2,1)S(1)} %get-tuple-element.60), channel_id=1, source_target_pairs={{0,1},{1,0},{2,3},{3,2},{4,5},{5,4},{6,7},{7,6},{8,9},{9,8},{10,11... | collective-permute-start | bytes 491528 | tf_op jit(solution)/shard_map/ppermute | solution.py:518
  18.6 10.4 %collective-permute-start.13 = (bf16[2,1,320,128]{3,2,1,0:T(8,128)(2,1)S(1)}, bf16[2,1,320,128]{3,2,1,0:T(8,128)(2,1)S(1)}, u32[]{:S(2)}, u32[]{:S(2)}) collective-permute-start(bf16[2,1,320,128]{3,2,1,0:T(8,128)(2,1)S(1)} %get-tuple-element.61), channel_id=1, source_target_pairs={{0,2},{1,3},{2,0},{3,1},{4,6},{5,7},{6,4},{7,5},{8,10},{9,11},{10,... | collective-permute-start | bytes 491528 | tf_op jit(solution)/shard_map/ppermute | solution.py:518
  19.9 13.9 %collective-permute-start.14 = (bf16[2,1,320,128]{3,2,1,0:T(8,128)(2,1)S(1)}, bf16[2,1,320,128]{3,2,1,0:T(8,128)(2,1)S(1)}, u32[]{:S(2)}, u32[]{:S(2)}) collective-permute-start(bf16[2,1,320,128]{3,2,1,0:T(8,128)(2,1)S(1)} %get-tuple-element.62), channel_id=1, source_target_pairs={{0,3},{1,2},{2,1},{3,0},{4,7},{5,6},{6,5},{7,4},{8,11},{9,10},{10,... | collective-permute-start | bytes 491528 | tf_op jit(solution)/shard_map/ppermute | solution.py:518
  22.0 22.4 %collective-permute-start.7 = (bf16[1,1,320,128]{3,2,1,0:T(8,128)(2,1)S(1)}, bf16[1,1,320,128]{3,2,1,0:T(8,128)(2,1)S(1)}, u32[]{:S(2)}, u32[]{:S(2)}) collective-permute-start(bf16[1,1,320,128]{3,2,1,0:T(8,128)(2,1)S(1)} %get-tuple-element.53), channel_id=1, source_target_pairs={{0,2},{1,3},{2,0},{3,1},{4,6},{5,7},{6,4},{7,5},{8,10},{9,11},{10,... | collective-permute-start | bytes 245768 | tf_op jit(solution)/shard_map/ppermute | solution.py:518
  26.8 17.6 %collective-permute-start.8 = (bf16[1,1,320,128]{3,2,1,0:T(8,128)(2,1)S(1)}, bf16[1,1,320,128]{3,2,1,0:T(8,128)(2,1)S(1)}, u32[]{:S(2)}, u32[]{:S(2)}) collective-permute-start(bf16[1,1,320,128]{3,2,1,0:T(8,128)(2,1)S(1)} %get-tuple-element.54), channel_id=1, source_target_pairs={{0,3},{1,2},{2,1},{3,0},{4,7},{5,6},{6,5},{7,4},{8,11},{9,10},{10,... | collective-permute-start | bytes 245768 | tf_op jit(solution)/shard_map/ppermute | solution.py:518
  27.0 19.9 %collective-permute-start.3 = (bf16[1,1,320,128]{3,2,1,0:T(8,128)(2,1)S(1)}, bf16[1,1,320,128]{3,2,1,0:T(8,128)(2,1)S(1)}, u32[]{:S(2)}, u32[]{:S(2)}) collective-permute-start(bf16[1,1,320,128]{3,2,1,0:T(8,128)(2,1)S(1)} %get-tuple-element.48), channel_id=1, source_target_pairs={{0,1},{1,0},{2,3},{3,2},{4,5},{5,4},{6,7},{7,6},{8,9},{9,8},{10,11... | collective-permute-start | bytes 245768 | tf_op jit(solution)/shard_map/ppermute | solution.py:518
  29.0 17.9 %collective-permute-start.4 = (bf16[1,1,320,128]{3,2,1,0:T(8,128)(2,1)S(1)}, bf16[1,1,320,128]{3,2,1,0:T(8,128)(2,1)S(1)}, u32[]{:S(2)}, u32[]{:S(2)}) collective-permute-start(bf16[1,1,320,128]{3,2,1,0:T(8,128)(2,1)S(1)} %get-tuple-element.49), channel_id=1, source_target_pairs={{0,2},{1,3},{2,0},{3,1},{4,6},{5,7},{6,4},{7,5},{8,10},{9,11},{10,... | collective-permute-start | bytes 245768 | tf_op jit(solution)/shard_map/ppermute | solution.py:518
  33.8 13.0 %collective-permute-start.5 = (bf16[1,1,320,128]{3,2,1,0:T(8,128)(2,1)S(1)}, bf16[1,1,320,128]{3,2,1,0:T(8,128)(2,1)S(1)}, u32[]{:S(2)}, u32[]{:S(2)}) collective-permute-start(bf16[1,1,320,128]{3,2,1,0:T(8,128)(2,1)S(1)} %get-tuple-element.50), channel_id=1, source_target_pairs={{0,3},{1,2},{2,1},{3,0},{4,7},{5,6},{6,5},{7,4},{8,11},{9,10},{10,... | collective-permute-start | bytes 245768 | tf_op jit(solution)/shard_map/ppermute | solution.py:518
  49.3 4.9 %collective-permute-start.22 = (bf16[1040,512]{1,0:T(8,128)(2,1)S(1)}, bf16[1040,512]{1,0:T(8,128)(2,1)S(1)}, u32[]{:S(2)}, u32[]{:S(2)}) collective-permute-start(bf16[1040,512]{1,0:T(8,128)(2,1)S(1)} %bitcast.7), channel_id=1, source_target_pairs={{4,5},{6,7},{8,9},{10,11},{12,13},{14,15},{16,17},{18,19},{20,21},... | collective-permute-start | bytes 3194888 | tf_op jit(solution)/shard_map/ppermute | solution.py:521
  50.6 9.9 %collective-permute-start.20 = (bf16[1040,512]{1,0:T(8,128)(2,1)S(1)}, bf16[1040,512]{1,0:T(8,128)(2,1)S(1)}, u32[]{:S(2)}, u32[]{:S(2)}) collective-permute-start(bf16[1040,512]{1,0:T(8,128)(2,1)S(1)} %bitcast.8), channel_id=1, source_target_pairs={{2,3}} | collective-permute-start | bytes 3194888 | tf_op jit(solution)/shard_map/ppermute | solution.py:521
  55.3 9.0 %collective-permute-start.26 = (bf16[1040,512]{1,0:T(8,128)(2,1)S(1)}, bf16[1040,512]{1,0:T(8,128)(2,1)S(1)}, u32[]{:S(2)}, u32[]{:S(2)}) collective-permute-start(bf16[1040,512]{1,0:T(8,128)(2,1)S(1)} %join.1.refs_0_.own.refs_2_), channel_id=1, source_target_pairs={{9,11},{11,9}} | collective-permute-start | bytes 3194888 | tf_op jit(solution)/shard_map/ppermute | solution.py:521
  56.2 15.7 %collective-permute-start.28 = (bf16[1040,512]{1,0:T(8,128)(2,1)S(1)}, bf16[1040,512]{1,0:T(8,128)(2,1)S(1)}, u32[]{:S(2)}, u32[]{:S(2)}) collective-permute-start(bf16[1040,512]{1,0:T(8,128)(2,1)S(1)} %join.1.refs_0_.own.refs_2_), channel_id=1, source_target_pairs={{13,15},{15,13},{17,19},{19,17},{21,23},{23,21},{25,27},{27,25},{2... | collective-permute-start | bytes 3194888 | tf_op jit(solution)/shard_map/ppermute | solution.py:521
  58.9 0.7 collective-permute-start.18
  62.9 1.3 %collective-permute-start.25 = (f32[1,512]{1,0:T(1,128)S(1)}, f32[1,512]{1,0:T(1,128)S(1)}, u32[]{:S(2)}, u32[]{:S(2)}) collective-permute-start(f32[1,512]{1,0:T(1,128)S(1)} %hop.10), channel_id=1, source_target_pairs={{7,11}} | collective-permute-start | bytes 6152 | tf_op jit(solution)/shard_map/ppermute | solution.py:521
  63.6 0.7 collective-permute-start.24
  64.8 7.1 %collective-permute-start.27 = (f32[1,512]{1,0:T(1,128)S(1)}, f32[1,512]{1,0:T(1,128)S(1)}, u32[]{:S(2)}, u32[]{:S(2)}) collective-permute-start(f32[1,512]{1,0:T(1,128)S(1)} %span_hop.2), channel_id=1, source_target_pairs={{9,13},{11,15}} | collective-permute-start | bytes 6152 | tf_op jit(solution)/shard_map/ppermute | solution.py:521
  72.5 1.8 %collective-permute-start.29 = (f32[1,512]{1,0:T(1,128)S(1)}, f32[1,512]{1,0:T(1,128)S(1)}, u32[]{:S(2)}, u32[]{:S(2)}) collective-permute-start(f32[1,512]{1,0:T(1,128)S(1)} %span_hop.3), channel_id=1, source_target_pairs={{13,17},{15,19}} | collective-permute-start | bytes 6152 | tf_op jit(solution)/shard_map/ppermute | solution.py:521
  76.5 12.5 %collective-permute-start.32 = (f32[1,512]{1,0:T(1,128)S(1)}, f32[1,512]{1,0:T(1,128)S(1)}, u32[]{:S(2)}, u32[]{:S(2)}) collective-permute-start(f32[1,512]{1,0:T(1,128)S(1)} %hop.13), channel_id=1, source_target_pairs={{25,29},{27,31}} | collective-permute-start | bytes 6152 | tf_op jit(solution)/shard_map/ppermute | solution.py:521
  89.1 2.1 %collective-permute-start.33 = (f32[1,512]{1,0:T(1,128)S(1)}, f32[1,512]{1,0:T(1,128)S(1)}, u32[]{:S(2)}, u32[]{:S(2)}) collective-permute-start(f32[1,512]{1,0:T(1,128)S(1)} %lead.1.refs_0_), channel_id=1, source_target_pairs={{1,0},{3,2},{5,4},{7,6},{9,8},{11,10},{13,12},{15,14},{17,16},{19,... | collective-permute-start | bytes 6152 | tf_op jit(solution)/shard_map/ppermute | solution.py:521
  92.7 2.2 %collective-permute-start.34 = (f32[8,128]{1,0:T(8,128)S(1)}, f32[8,128]{1,0:T(8,128)S(1)}, u32[]{:S(2)}, u32[]{:S(2)}) collective-permute-start(f32[8,128]{1,0:T(8,128)S(1)} %get-tuple-element.78), channel_id=1, source_target_pairs={{0,1},{1,0},{2,3},{3,2},{4,5},{5,4},{6,7},{7,6},{8,9},{9,8},{10,11... | collective-permute-start | bytes 12296 | tf_op jit(solution)/shard_map/ppermute | solution.py:518
  92.8 2.5 %collective-permute-start.35 = (f32[8,128]{1,0:T(8,128)S(1)}, f32[8,128]{1,0:T(8,128)S(1)}, u32[]{:S(2)}, u32[]{:S(2)}) collective-permute-start(f32[8,128]{1,0:T(8,128)S(1)} %get-tuple-element.79), channel_id=1, source_target_pairs={{0,2},{1,3},{2,0},{3,1},{4,6},{5,7},{6,4},{7,5},{8,10},{9,11},{10,... | collective-permute-start | bytes 12296 | tf_op jit(solution)/shard_map/ppermute | solution.py:518
  92.8 3.6 %collective-permute-start.36 = (f32[8,128]{1,0:T(8,128)S(1)}, f32[8,128]{1,0:T(8,128)S(1)}, u32[]{:S(2)}, u32[]{:S(2)}) collective-permute-start(f32[8,128]{1,0:T(8,128)S(1)} %get-tuple-element.80), channel_id=1, source_target_pairs={{0,3},{1,2},{2,1},{3,0},{4,7},{5,6},{6,5},{7,4},{8,11},{9,10},{10,... | collective-permute-start | bytes 12296 | tf_op jit(solution)/shard_map/ppermute | solution.py:518
  (14 other events, 83.9 us)

commit v4 on v3

--- a/solution.py
+++ b/solution.py
@@ -419,48 +419,55 @@
     )(position, span, row, direct, *maps, *maps_late)
 
 
-def sweep_kernel(pieces, parts, s_ref, tm_ref, *refs):
-    own_ref, told_ref, first_map, first_vec, map_ref = refs[:5]
-    stages, outs = refs[5 : 5 + pieces], refs[5 + pieces : 5 + pieces + parts]
-    current_ref, spread = refs[5 + pieces + parts :]
+def sweep_kernel(leader, pieces, parts, s_ref, tm_ref, *refs):
+    if leader:
+        own_ref, first_map, first_vec, map_ref = refs[:4]
+        refs = refs[4:]
+    else:
+        told_ref, refs = refs[0], refs[1 + parts :]
+    stages, outs = refs[:pieces], refs[pieces : pieces + parts]
+    current_ref, spread = refs[pieces + parts :]
     s = s_ref[0]
 
-    @pl.when(s % 2 == 0)
+    @pl.when(s % 2 == int(leader))
     def _():
-        current_ref[...] = told_ref[...]
-
-    @pl.when(jnp.logical_and(s % 2 == 1, tm_ref[0] == 0))
-    def _():
-        current_ref[...] = apply_map(own_ref[...], first_map) + first_vec[...]
-
-    @pl.when(jnp.logical_and(s % 2 == 1, tm_ref[0] > 0))
-    def _():
-        current_ref[...] = apply_map(own_ref[...], map_ref)
-
-    entry = current_ref[...]
-    at = 0
-    width = spread.shape[2]
-    for p in range(pieces):
-        for j in range(stages[p].shape[0]):
-            mean = apply_map(entry, stages[p].at[j])
-            for d in range(parts):
-                spread[d, at : at + 1, :] = mean[:, d * width : (d + 1) * width]
-            at += 1
-    for d in range(parts):
-        outs[d][...] = spread[s ^ d]
-
-
-def sweep(position, span, own, told, even, stages, parts):
-    ns = own.shape[1]
+        if leader:
+
+            @pl.when(tm_ref[0] == 0)
+            def _():
+                current_ref[...] = apply_map(own_ref[...], first_map) + first_vec[...]
+
+            @pl.when(tm_ref[0] > 0)
+            def _():
+                current_ref[...] = apply_map(own_ref[...], map_ref)
+
+            entry = current_ref[...]
+        else:
+            entry = told_ref[...]
+        at = 0
+        width = spread.shape[2]
+        for p in range(pieces):
+            for j in range(stages[p].shape[0]):
+                mean = apply_map(entry, stages[p].at[j])
+                for d in range(parts):
+                    spread[d, at : at + 1, :] = mean[:, d * width : (d + 1) * width]
+                at += 1
+        for d in range(parts):
+            outs[d][...] = spread[s ^ d]
+
+
+def sweep(position, span, entry, stages, parts, even=(), filled=()):
+    ns = entry.shape[1]
     pieces = len(stages)
     chunk = sum(x.shape[0] for x in stages)
     width = ns // parts
-    return pl.pallas_call(
-        functools.partial(sweep_kernel, pieces, parts),
+    leader = bool(even)
+    return pl.pallas_call(
+        functools.partial(sweep_kernel, leader, pieces, parts),
         grid_spec=pltpu.PrefetchScalarGridSpec(
             num_scalar_prefetch=2,
             grid=(),
-            in_specs=vmem(5 + pieces),
+            in_specs=vmem(1 + len(even) + len(filled) + pieces),
             out_specs=vmem(parts),
             scratch_shapes=[
                 pltpu.VMEM((1, ns), F32),
@@ -468,9 +475,10 @@
             ],
         ),
         out_shape=[jax.ShapeDtypeStruct((chunk, width), F32)] * parts,
-        compiler_params=pltpu.CompilerParams(vmem_limit_bytes=VMEM_LIMIT),
-        name="sweep",
-    )(position, span, own, told, *even, *stages)
+        input_output_aliases={3 + n: n for n in range(len(filled))},
+        compiler_params=pltpu.CompilerParams(vmem_limit_bytes=VMEM_LIMIT),
+        name="sweep_lead" if leader else "sweep",
+    )(position, span, entry, *even, *filled, *stages)
 
 
 def gather_kernel(parts, s_ref, *refs):
@@ -499,7 +507,7 @@
 
 def piece_sizes(chunk):
     base, more = divmod(chunk - 2, PIECES - 2)
-    return [base + 1] * more + [base] * (PIECES - 2 - more) + [1, 1]
+    return [1] + [base + 1] * more + [base] * (PIECES - 2 - more) + [1]
 
 
 def means(dyn_cols, dyn_vals, obs_blocks, obs_op, obs_counts, obs_values, gain, sources, prior):
@@ -594,9 +602,8 @@
 
     own = lead(position, span, entry, direct, maps, maps_late, early)
     told = send(own, [(b, a) for a, b in to_lead])
-    mine = sweep(
-        position, span, own, told, (first_map, first_vec, map_even), stages, parts
-    )
+    filled = sweep(position, span, own, stages, parts, even=(first_map, first_vec, map_even))
+    mine = sweep(position, span, told, stages, parts, filled=filled)
     got = {0: mine[0]}
     for d in order:
         got[d] = across(mine[d], d)

time: 97.5 us -> 94.8 us (0.972)
  waiting for transfers between devices: 39.3 us -> 34.7 us
  starting transfers between devices: 32.4 us -> 34.4 us
    ppermute x21, waiting for transfers between devices: 17.9 us -> 14.3 us  [across(): return lax.ppermute(x, 'state', [(i, i ^ d) for i in range(parts)])]
    ppermute x21, starting transfers between devices: 17.6 us -> 19.7 us  [across(): return lax.ppermute(x, 'state', [(i, i ^ d) for i in range(parts)])]
    ppermute x16, waiting for transfers between devices: 21.4 us -> 20.3 us  [send(): lax.ppermute(x, ('tm', 'state'), [(a * parts + b, c * parts + e) for (a,...]
  transfers between devices with their start and end apart: 37 -> 37, of which waited for: 14 -> 13; matrix products, arithmetic and copies ran while one was open for 0% -> 0% of each run, Pallas kernels for 18% -> 20%
where the time goes in v4:
time: 94.8 us; the launch traced here: 94.5 us
  waiting for transfers between devices  34.7 us (37%)
  starting transfers between devices  34.4 us (36%)
  Pallas kernels  24.9 us (26%)
    ppermute x16, waiting for transfers between devices, send(): lax.ppermute(x, ('tm', 'state'), [(a * parts + b, c * parts + e) for (a,...  20.3 us
    ppermute x21, starting transfers between devices, across(): return lax.ppermute(x, 'state', [(i, i ^ d) for i in range(parts)])  19.7 us
    pallas_call x5, Pallas kernels, chunk_piece(): pl.pallas_call(functools.partial(chunk_kernel, parts, pairs, bs, chunk, f...  15.4 us
    ppermute x16, starting transfers between devices, send(): lax.ppermute(x, ('tm', 'state'), [(a * parts + b, c * parts + e) for (a,...  14.7 us
    ppermute x21, waiting for transfers between devices, across(): return lax.ppermute(x, 'state', [(i, i ^ d) for i in range(parts)])  14.3 us
    pallas_call x7, Pallas kernels, hop(): pl.pallas_call(hop_kernel, in_specs=vmem(1 + len(maps)), out_specs=vmem(1...  2.05 us
    pallas_call x5, Pallas kernels, pack(): pl.pallas_call(functools.partial(pack_kernel, parts, pairs, bs, chunk, bo...  2 us
  transfers between devices with their start and end apart: 37, of which 13 were waited for; matrix products, arithmetic and copies ran while one was open for 0% of the time, Pallas kernels for 20%

profile of v4, /device:TPU:27, one launch (start us, length us, event | category | flops | bytes accessed | tf_op | source)
XLA Modules:
  0.0 94.5 jit_solution(603206294453354781)
XLA Ops:
  0.0 1.2 %shard_map.95 = (bf16[1,1,320,128]{3,2,1,0:T(8,128)(2,1)S(1)}, bf16[1,1,320,128]{3,2,1,0:T(8,128)(2,1)S(1)}, bf16[1,1,320,128]{3,2,1,0:T(8,128)(2,1)S(1)}, bf16[1,1,320,128]{3,2,1,0:T(8,128)(2,1)S(1)}) custom-call(s32[1]{0:T(128)} %bitcast.s_ref, s32[1]{0:T(128)} %bitcast.1.tm_ref, bf16[32,2,64,192]{3,2,1,0:T(8,128)(2,1)} %refs_3_.9, ...), custom_call_target="tpu_custom_call" | custom-call | tf_op jit(solution)/shard_map/pallas_call | solution.py:95
  2.0 1.2 %collective-permute-start.16 = (bf16[1,1,320,128]{3,2,1,0:T(8,128)(2,1)S(1)}, bf16[1,1,320,128]{3,2,1,0:T(8,128)(2,1)S(1)}, u32[]{:S(2)}, u32[]{:S(2)}) collective-permute-start(bf16[1,1,320,128]{3,2,1,0:T(8,128)(2,1)S(1)} %get-tuple-element.69), channel_id=1, source_target_pairs={{0,2},{1,3},{2,0},{3,1},{4,6},{5,7},{6,4},{7,5},{8,10},{9,11},{10,... | collective-permute-start | bytes 245768 | tf_op jit(solution)/shard_map/ppermute | solution.py:526
  6.2 2.1 %collective-permute-done.1.refs_2_.refs_6_ = f32[14,128]{1,0:T(8,128)S(1)} collective-permute-done((f32[14,128]{1,0:T(8,128)S(1)}, f32[14,128]{1,0:T(8,128)S(1)}, u32[]{:S(2)}, u32[]{:S(2)}) %collective-permute-start.1) | collective-permute-done | bytes 7200 | tf_op jit(solution)/shard_map/ppermute | solution.py:526
  8.3 1.8 %collective-permute-start.2 = (f32[14,128]{1,0:T(8,128)S(1)}, f32[14,128]{1,0:T(8,128)S(1)}, u32[]{:S(2)}, u32[]{:S(2)}) collective-permute-start(f32[14,128]{1,0:T(8,128)S(1)} %get-tuple-element.50), channel_id=1, source_target_pairs={{0,3},{1,2},{2,1},{3,0},{4,7},{5,6},{6,5},{7,4},{8,11},{9,10},{10,... | collective-permute-start | bytes 21512 | tf_op jit(solution)/shard_map/ppermute | solution.py:526
  10.1 1.3 %collective-permute-done.2.refs_3_.refs_7_ = f32[14,128]{1,0:T(8,128)S(1)} collective-permute-done((f32[14,128]{1,0:T(8,128)S(1)}, f32[14,128]{1,0:T(8,128)S(1)}, u32[]{:S(2)}, u32[]{:S(2)}) %collective-permute-start.2) | collective-permute-done | bytes 7200 | tf_op jit(solution)/shard_map/ppermute | solution.py:526
  11.4 1.7 %collective-permute-start.17 = (bf16[1,1,320,128]{3,2,1,0:T(8,128)(2,1)S(1)}, bf16[1,1,320,128]{3,2,1,0:T(8,128)(2,1)S(1)}, u32[]{:S(2)}, u32[]{:S(2)}) collective-permute-start(bf16[1,1,320,128]{3,2,1,0:T(8,128)(2,1)S(1)} %get-tuple-element.70), channel_id=1, source_target_pairs={{0,3},{1,2},{2,1},{3,0},{4,7},{5,6},{6,5},{7,4},{8,11},{9,10},{10,... | collective-permute-start | bytes 245768 | tf_op jit(solution)/shard_map/ppermute | solution.py:526
  13.2 1.1 %collective-permute-start.10 = (bf16[2,1,320,128]{3,2,1,0:T(8,128)(2,1)S(1)}, bf16[2,1,320,128]{3,2,1,0:T(8,128)(2,1)S(1)}, u32[]{:S(2)}, u32[]{:S(2)}) collective-permute-start(bf16[2,1,320,128]{3,2,1,0:T(8,128)(2,1)S(1)} %get-tuple-element.61), channel_id=1, source_target_pairs={{0,2},{1,3},{2,0},{3,1},{4,6},{5,7},{6,4},{7,5},{8,10},{9,11},{10,... | collective-permute-start | bytes 491528 | tf_op jit(solution)/shard_map/ppermute | solution.py:526
  14.6 1.1 %collective-permute-done.17.refs_3_ = bf16[1,1,320,128]{3,2,1,0:T(8,128)(2,1)S(1)} collective-permute-done((bf16[1,1,320,128]{3,2,1,0:T(8,128)(2,1)S(1)}, bf16[1,1,320,128]{3,2,1,0:T(8,128)(2,1)S(1)}, u32[]{:S(2)}, u32[]{:S(2)}) %collective-permute-start.17) | collective-permute-done | bytes 81952 | tf_op jit(solution)/shard_map/ppermute | solution.py:526
  15.7 1.6 %collective-permute-start.12 = (bf16[2,1,320,128]{3,2,1,0:T(8,128)(2,1)S(1)}, bf16[2,1,320,128]{3,2,1,0:T(8,128)(2,1)S(1)}, u32[]{:S(2)}, u32[]{:S(2)}) collective-permute-start(bf16[2,1,320,128]{3,2,1,0:T(8,128)(2,1)S(1)} %get-tuple-element.64), channel_id=1, source_target_pairs={{0,1},{1,0},{2,3},{3,2},{4,5},{5,4},{6,7},{7,6},{8,9},{9,8},{10,11... | collective-permute-start | bytes 491528 | tf_op jit(solution)/shard_map/ppermute | solution.py:526
  18.9 1.2 %collective-permute-done.10.refs_2_ = bf16[2,1,320,128]{3,2,1,0:T(8,128)(2,1)S(1)} collective-permute-done((bf16[2,1,320,128]{3,2,1,0:T(8,128)(2,1)S(1)}, bf16[2,1,320,128]{3,2,1,0:T(8,128)(2,1)S(1)}, u32[]{:S(2)}, u32[]{:S(2)}) %collective-permute-start.10) | collective-permute-done | bytes 163872 | tf_op jit(solution)/shard_map/ppermute | solution.py:526
  21.0 2.1 %collective-permute-done.11.refs_3_ = bf16[2,1,320,128]{3,2,1,0:T(8,128)(2,1)S(1)} collective-permute-done((bf16[2,1,320,128]{3,2,1,0:T(8,128)(2,1)S(1)}, bf16[2,1,320,128]{3,2,1,0:T(8,128)(2,1)S(1)}, u32[]{:S(2)}, u32[]{:S(2)}) %collective-permute-start.11) | collective-permute-done | bytes 163872 | tf_op jit(solution)/shard_map/ppermute | solution.py:526
  23.1 1.9 %collective-permute-start.8 = (bf16[2,1,320,128]{3,2,1,0:T(8,128)(2,1)S(1)}, bf16[2,1,320,128]{3,2,1,0:T(8,128)(2,1)S(1)}, u32[]{:S(2)}, u32[]{:S(2)}) collective-permute-start(bf16[2,1,320,128]{3,2,1,0:T(8,128)(2,1)S(1)} %get-tuple-element.58), channel_id=1, source_target_pairs={{0,3},{1,2},{2,1},{3,0},{4,7},{5,6},{6,5},{7,4},{8,11},{9,10},{10,... | collective-permute-start | bytes 491528 | tf_op jit(solution)/shard_map/ppermute | solution.py:526
  25.2 1.9 %collective-permute-done.13.refs_2_ = bf16[2,1,320,128]{3,2,1,0:T(8,128)(2,1)S(1)} collective-permute-done((bf16[2,1,320,128]{3,2,1,0:T(8,128)(2,1)S(1)}, bf16[2,1,320,128]{3,2,1,0:T(8,128)(2,1)S(1)}, u32[]{:S(2)}, u32[]{:S(2)}) %collective-permute-start.13) | collective-permute-done | bytes 163872 | tf_op jit(solution)/shard_map/ppermute | solution.py:526
  28.0 2.1 %collective-permute-done.14.refs_3_ = bf16[2,1,320,128]{3,2,1,0:T(8,128)(2,1)S(1)} collective-permute-done((bf16[2,1,320,128]{3,2,1,0:T(8,128)(2,1)S(1)}, bf16[2,1,320,128]{3,2,1,0:T(8,128)(2,1)S(1)}, u32[]{:S(2)}, u32[]{:S(2)}) %collective-permute-start.14) | collective-permute-done | bytes 163872 | tf_op jit(solution)/shard_map/ppermute | solution.py:526
  30.1 1.8 %collective-permute-start.5 = (bf16[1,1,320,128]{3,2,1,0:T(8,128)(2,1)S(1)}, bf16[1,1,320,128]{3,2,1,0:T(8,128)(2,1)S(1)}, u32[]{:S(2)}, u32[]{:S(2)}) collective-permute-start(bf16[1,1,320,128]{3,2,1,0:T(8,128)(2,1)S(1)} %get-tuple-element.54), channel_id=1, source_target_pairs={{0,3},{1,2},{2,1},{3,0},{4,7},{5,6},{6,5},{7,4},{8,11},{9,10},{10,... | collective-permute-start | bytes 245768 | tf_op jit(solution)/shard_map/ppermute | solution.py:526
  32.0 2.2 %shard_map.96 = (bf16[1,1040,512]{2,1,0:T(8,128)(2,1)S(1)}, f32[1,512]{1,0:T(1,128)S(1)}) custom-call(s32[1]{0:T(128)} %bitcast.s_ref, s32[1]{0:T(128)} %bitcast.1.tm_ref, s32[27,32]{1,0:T(8,128)S(1)} %plan.1.plan_ref, bf16[1,1,320,128]{3,2,1,0:T(8,128)(2,1)S(1)} %get-tuple-element.67.refs_0_.refs_11_, ...), custom_call_target="tpu_custom_call" | custom-call | tf_op jit(solution)/shard_map/pallas_call | solution.py:262
  34.2 3.6 %shard_map.97 = (bf16[2,1040,512]{2,1,0:T(8,128)(2,1)S(1)}, f32[1,512]{1,0:T(1,128)S(1)}) custom-call(s32[1]{0:T(128)} %bitcast.s_ref, s32[1]{0:T(128)} %bitcast.1.tm_ref, s32[27,32]{1,0:T(8,128)S(1)} %plan.1.plan_ref, bf16[2,1,320,128]{3,2,1,0:T(8,128)(2,1)S(1)} %get-tuple-element.63.refs_0_, bf16[2,1,320,128]{3,2,1,0:T(8,128)(2,1)S(1)} %collective-permute-done.12.refs_1_, ...), custom_call_target="tpu_custom_call" | custom-call | tf_op jit(solution)/shard_map/pallas_call | solution.py:262
  37.8 3.6 %shard_map.98 = (bf16[2,1040,512]{2,1,0:T(8,128)(2,1)S(1)}, f32[1,512]{1,0:T(1,128)S(1)}) custom-call(s32[1]{0:T(128)} %bitcast.s_ref, s32[1]{0:T(128)} %bitcast.1.tm_ref, s32[27,32]{1,0:T(8,128)S(1)} %plan.1.plan_ref, bf16[2,1,320,128]{3,2,1,0:T(8,128)(2,1)S(1)} %get-tuple-element.59.refs_0_, bf16[2,1,320,128]{3,2,1,0:T(8,128)(2,1)S(1)} %collective-permute-done.9.refs_1_, ...), custom_call_target="tpu_custom_call" | custom-call | tf_op jit(solution)/shard_map/pallas_call | solution.py:262
  41.4 3.6 %shard_map.99 = (bf16[2,1040,512]{2,1,0:T(8,128)(2,1)S(1)}, f32[1,512]{1,0:T(1,128)S(1)}) custom-call(s32[1]{0:T(128)} %bitcast.s_ref, s32[1]{0:T(128)} %bitcast.1.tm_ref, s32[27,32]{1,0:T(8,128)S(1)} %plan.1.plan_ref, bf16[2,1,320,128]{3,2,1,0:T(8,128)(2,1)S(1)} %get-tuple-element.55.refs_0_, bf16[2,1,320,128]{3,2,1,0:T(8,128)(2,1)S(1)} %collective-permute-done.6.refs_1_, ...), custom_call_target="tpu_custom_call" | custom-call | tf_op jit(solution)/shard_map/pallas_call | solution.py:262
  45.0 2.4 %shard_map.100 = (bf16[1,1040,512]{2,1,0:T(8,128)(2,1)S(1)}, f32[1,512]{1,0:T(1,128)S(1)}) custom-call(s32[1]{0:T(128)} %bitcast.s_ref, s32[1]{0:T(128)} %bitcast.1.tm_ref, s32[27,32]{1,0:T(8,128)S(1)} %plan.1.plan_ref, bf16[1,1,320,128]{3,2,1,0:T(8,128)(2,1)S(1)} %get-tuple-element.51.refs_0_, bf16[1,1,320,128]{3,2,1,0:T(8,128)(2,1)S(1)} %collective-permute-done.3.refs_1_, ...), custom_call_target="tpu_custom_call" | custom-call | tf_op jit(solution)/shard_map/pallas_call | solution.py:262
  47.5 1.3 %collective-permute-start.22 = (bf16[1040,512]{1,0:T(8,128)(2,1)S(1)}, bf16[1040,512]{1,0:T(8,128)(2,1)S(1)}, u32[]{:S(2)}, u32[]{:S(2)}) collective-permute-start(bf16[1040,512]{1,0:T(8,128)(2,1)S(1)} %bitcast.7), channel_id=1, source_target_pairs={{4,5},{6,7},{8,9},{10,11},{12,13},{14,15},{16,17},{18,19},{20,21},... | collective-permute-start | bytes 3194888 | tf_op jit(solution)/shard_map/ppermute | solution.py:529
  49.5 2.5 %collective-permute-done.22.one.refs_3_ = bf16[1040,512]{1,0:T(8,128)(2,1)S(1)} collective-permute-done((bf16[1040,512]{1,0:T(8,128)(2,1)S(1)}, bf16[1040,512]{1,0:T(8,128)(2,1)S(1)}, u32[]{:S(2)}, u32[]{:S(2)}) %collective-permute-start.22) | collective-permute-done | bytes 1064992 | tf_op jit(solution)/shard_map/ppermute | solution.py:529
  52.0 1.1 %join.1.refs_0_.own.refs_2_ = bf16[1040,512]{1,0:T(8,128)(2,1)S(1)} custom-call(bf16[1040,512]{1,0:T(8,128)(2,1)S(1)} %collective-permute-done.22.one.refs_3_, bf16[1040,512]{1,0:T(8,128)(2,1)S(1)} %bitcast.9), custom_call_target="tpu_custom_call" | custom-call | tf_op jit(solution)/shard_map/join/pallas_call | solution.py:309
  53.2 0.9 collective-permute-start.26
  54.1 2.6 %collective-permute-start.28 = (bf16[1040,512]{1,0:T(8,128)(2,1)S(1)}, bf16[1040,512]{1,0:T(8,128)(2,1)S(1)}, u32[]{:S(2)}, u32[]{:S(2)}) collective-permute-start(bf16[1040,512]{1,0:T(8,128)(2,1)S(1)} %join.1.refs_0_.own.refs_2_), channel_id=1, source_target_pairs={{13,15},{15,13},{17,19},{19,17},{21,23},{23,21},{25,27},{27,25},{2... | collective-permute-start | bytes 3194888 | tf_op jit(solution)/shard_map/ppermute | solution.py:529
  63.3 6.5 %collective-permute-done.28.refs_1_.far.refs_3_ = bf16[1040,512]{1,0:T(8,128)(2,1)S(1)} collective-permute-done((bf16[1040,512]{1,0:T(8,128)(2,1)S(1)}, bf16[1040,512]{1,0:T(8,128)(2,1)S(1)}, u32[]{:S(2)}, u32[]{:S(2)}) %collective-permute-start.28) | collective-permute-done | bytes 1064992 | tf_op jit(solution)/shard_map/ppermute | solution.py:529
  71.0 1.1 %span_join.1.refs_0_ = bf16[1040,512]{1,0:T(8,128)(2,1)S(1)} custom-call(s32[1]{0:T(128)} %bitcast.s_ref, bf16[1040,512]{1,0:T(8,128)(2,1)S(1)} %join.1.refs_0_.own.refs_2_, bf16[1040,512]{1,0:T(8,128)(2,1)S(1)} %collective-permute-done.28.refs_1_.far.refs_3_), custom_call_target="tpu_custom_call" | custom-call | tf_op jit(solution)/shard_map/span_join/pallas_call | solution.py:376
  74.3 1.3 %collective-permute-start.32 = (f32[1,512]{1,0:T(1,128)S(1)}, f32[1,512]{1,0:T(1,128)S(1)}, u32[]{:S(2)}, u32[]{:S(2)}) collective-permute-start(f32[1,512]{1,0:T(1,128)S(1)} %hop.13), channel_id=1, source_target_pairs={{25,29},{27,31}} | collective-permute-start | bytes 6152 | tf_op jit(solution)/shard_map/ppermute | solution.py:529
  75.6 11.2 %collective-permute-done.32 = f32[1,512]{1,0:T(1,128)S(1)} collective-permute-done((f32[1,512]{1,0:T(1,128)S(1)}, f32[1,512]{1,0:T(1,128)S(1)}, u32[]{:S(2)}, u32[]{:S(2)}) %collective-permute-start.32) | collective-permute-done | bytes 2080 | tf_op jit(solution)/shard_map/ppermute | solution.py:529
  86.9 1.3 %collective-permute-start.33 = (f32[1,512]{1,0:T(1,128)S(1)}, f32[1,512]{1,0:T(1,128)S(1)}, u32[]{:S(2)}, u32[]{:S(2)}) collective-permute-start(f32[1,512]{1,0:T(1,128)S(1)} %lead.1.refs_0_), channel_id=1, source_target_pairs={{1,0},{3,2},{5,4},{7,6},{9,8},{11,10},{13,12},{15,14},{17,16},{19,... | collective-permute-start | bytes 6152 | tf_op jit(solution)/shard_map/ppermute | solution.py:529
  88.2 1.5 %sweep_lead.1 = (f32[8,128]{1,0:T(8,128)S(1)}, f32[8,128]{1,0:T(8,128)S(1)}, f32[8,128]{1,0:T(8,128)S(1)}, f32[8,128]{1,0:T(8,128)S(1)}) custom-call(s32[1]{0:T(128)} %bitcast.s_ref, s32[1]{0:T(128)} %bitcast.1.tm_ref, f32[1,512]{1,0:T(1,128)S(1)} %lead.1.refs_0_, bf16[1040,512]{1,0:T(8,128)(2,1)S(1)} %collective-permute-done.20.refs_0_.refs_1_, ...), custom_call_target="tpu_custom_call" | custom-call | tf_op jit(solution)/shard_map/sweep_lead/pallas_call | solution.py:465
  90.7 1.7 %collective-permute-start.36 = (f32[8,128]{1,0:T(8,128)S(1)}, f32[8,128]{1,0:T(8,128)S(1)}, u32[]{:S(2)}, u32[]{:S(2)}) collective-permute-start(f32[8,128]{1,0:T(8,128)S(1)} %get-tuple-element.88), channel_id=1, source_target_pairs={{0,3},{1,2},{2,1},{3,0},{4,7},{5,6},{6,5},{7,4},{8,11},{9,10},{10,... | collective-permute-start | bytes 12296 | tf_op jit(solution)/shard_map/ppermute | solution.py:526
  (89 shorter events, 21.3 us)
Async XLA Ops:
  1.2 12.0 %collective-permute-start.15 = (bf16[1,1,320,128]{3,2,1,0:T(8,128)(2,1)S(1)}, bf16[1,1,320,128]{3,2,1,0:T(8,128)(2,1)S(1)}, u32[]{:S(2)}, u32[]{:S(2)}) collective-permute-start(bf16[1,1,320,128]{3,2,1,0:T(8,128)(2,1)S(1)} %get-tuple-element.68), channel_id=1, source_target_pairs={{0,1},{1,0},{2,3},{3,2},{4,5},{5,4},{6,7},{7,6},{8,9},{9,8},{10,11... | collective-permute-start | bytes 245768 | tf_op jit(solution)/shard_map/ppermute | solution.py:526
  2.0 12.3 %collective-permute-start.16 = (bf16[1,1,320,128]{3,2,1,0:T(8,128)(2,1)S(1)}, bf16[1,1,320,128]{3,2,1,0:T(8,128)(2,1)S(1)}, u32[]{:S(2)}, u32[]{:S(2)}) collective-permute-start(bf16[1,1,320,128]{3,2,1,0:T(8,128)(2,1)S(1)} %get-tuple-element.69), channel_id=1, source_target_pairs={{0,2},{1,3},{2,0},{3,1},{4,6},{5,7},{6,4},{7,5},{8,10},{9,11},{10,... | collective-permute-start | bytes 245768 | tf_op jit(solution)/shard_map/ppermute | solution.py:526
  3.5 13.8 %collective-permute-start.6 = (bf16[2,1,320,128]{3,2,1,0:T(8,128)(2,1)S(1)}, bf16[2,1,320,128]{3,2,1,0:T(8,128)(2,1)S(1)}, u32[]{:S(2)}, u32[]{:S(2)}) collective-permute-start(bf16[2,1,320,128]{3,2,1,0:T(8,128)(2,1)S(1)} %get-tuple-element.56), channel_id=1, source_target_pairs={{0,1},{1,0},{2,3},{3,2},{4,5},{5,4},{6,7},{7,6},{8,9},{9,8},{10,11... | collective-permute-start | bytes 491528 | tf_op jit(solution)/shard_map/ppermute | solution.py:526
  4.1 13.9 %collective-permute-start.9 = (bf16[2,1,320,128]{3,2,1,0:T(8,128)(2,1)S(1)}, bf16[2,1,320,128]{3,2,1,0:T(8,128)(2,1)S(1)}, u32[]{:S(2)}, u32[]{:S(2)}) collective-permute-start(bf16[2,1,320,128]{3,2,1,0:T(8,128)(2,1)S(1)} %get-tuple-element.60), channel_id=1, source_target_pairs={{0,1},{1,0},{2,3},{3,2},{4,5},{5,4},{6,7},{7,6},{8,9},{9,8},{10,11... | collective-permute-start | bytes 491528 | tf_op jit(solution)/shard_map/ppermute | solution.py:526
  4.6 1.3 %collective-permute-start = (f32[14,128]{1,0:T(8,128)S(1)}, f32[14,128]{1,0:T(8,128)S(1)}, u32[]{:S(2)}, u32[]{:S(2)}) collective-permute-start(f32[14,128]{1,0:T(8,128)S(1)} %get-tuple-element.48), channel_id=1, source_target_pairs={{0,1},{1,0},{2,3},{3,2},{4,5},{5,4},{6,7},{7,6},{8,9},{9,8},{10,11... | collective-permute-start | bytes 21512 | tf_op jit(solution)/shard_map/ppermute | solution.py:526
  5.8 2.5 %collective-permute-start.1 = (f32[14,128]{1,0:T(8,128)S(1)}, f32[14,128]{1,0:T(8,128)S(1)}, u32[]{:S(2)}, u32[]{:S(2)}) collective-permute-start(f32[14,128]{1,0:T(8,128)S(1)} %get-tuple-element.49), channel_id=1, source_target_pairs={{0,2},{1,3},{2,0},{3,1},{4,6},{5,7},{6,4},{7,5},{8,10},{9,11},{10,... | collective-permute-start | bytes 21512 | tf_op jit(solution)/shard_map/ppermute | solution.py:526
  8.3 3.1 %collective-permute-start.2 = (f32[14,128]{1,0:T(8,128)S(1)}, f32[14,128]{1,0:T(8,128)S(1)}, u32[]{:S(2)}, u32[]{:S(2)}) collective-permute-start(f32[14,128]{1,0:T(8,128)S(1)} %get-tuple-element.50), channel_id=1, source_target_pairs={{0,3},{1,2},{2,1},{3,0},{4,7},{5,6},{6,5},{7,4},{8,11},{9,10},{10,... | collective-permute-start | bytes 21512 | tf_op jit(solution)/shard_map/ppermute | solution.py:526
  11.4 4.3 %collective-permute-start.17 = (bf16[1,1,320,128]{3,2,1,0:T(8,128)(2,1)S(1)}, bf16[1,1,320,128]{3,2,1,0:T(8,128)(2,1)S(1)}, u32[]{:S(2)}, u32[]{:S(2)}) collective-permute-start(bf16[1,1,320,128]{3,2,1,0:T(8,128)(2,1)S(1)} %get-tuple-element.70), channel_id=1, source_target_pairs={{0,3},{1,2},{2,1},{3,0},{4,7},{5,6},{6,5},{7,4},{8,11},{9,10},{10,... | collective-permute-start | bytes 245768 | tf_op jit(solution)/shard_map/ppermute | solution.py:526
  13.2 6.9 %collective-permute-start.10 = (bf16[2,1,320,128]{3,2,1,0:T(8,128)(2,1)S(1)}, bf16[2,1,320,128]{3,2,1,0:T(8,128)(2,1)S(1)}, u32[]{:S(2)}, u32[]{:S(2)}) collective-permute-start(bf16[2,1,320,128]{3,2,1,0:T(8,128)(2,1)S(1)} %get-tuple-element.61), channel_id=1, source_target_pairs={{0,2},{1,3},{2,0},{3,1},{4,6},{5,7},{6,4},{7,5},{8,10},{9,11},{10,... | collective-permute-start | bytes 491528 | tf_op jit(solution)/shard_map/ppermute | solution.py:526
  14.3 8.8 %collective-permute-start.11 = (bf16[2,1,320,128]{3,2,1,0:T(8,128)(2,1)S(1)}, bf16[2,1,320,128]{3,2,1,0:T(8,128)(2,1)S(1)}, u32[]{:S(2)}, u32[]{:S(2)}) collective-permute-start(bf16[2,1,320,128]{3,2,1,0:T(8,128)(2,1)S(1)} %get-tuple-element.62), channel_id=1, source_target_pairs={{0,3},{1,2},{2,1},{3,0},{4,7},{5,6},{6,5},{7,4},{8,11},{9,10},{10,... | collective-permute-start | bytes 491528 | tf_op jit(solution)/shard_map/ppermute | solution.py:526
  15.7 9.5 %collective-permute-start.12 = (bf16[2,1,320,128]{3,2,1,0:T(8,128)(2,1)S(1)}, bf16[2,1,320,128]{3,2,1,0:T(8,128)(2,1)S(1)}, u32[]{:S(2)}, u32[]{:S(2)}) collective-permute-start(bf16[2,1,320,128]{3,2,1,0:T(8,128)(2,1)S(1)} %get-tuple-element.64), channel_id=1, source_target_pairs={{0,1},{1,0},{2,3},{3,2},{4,5},{5,4},{6,7},{7,6},{8,9},{9,8},{10,11... | collective-permute-start | bytes 491528 | tf_op jit(solution)/shard_map/ppermute | solution.py:526
  17.3 9.8 %collective-permute-start.13 = (bf16[2,1,320,128]{3,2,1,0:T(8,128)(2,1)S(1)}, bf16[2,1,320,128]{3,2,1,0:T(8,128)(2,1)S(1)}, u32[]{:S(2)}, u32[]{:S(2)}) collective-permute-start(bf16[2,1,320,128]{3,2,1,0:T(8,128)(2,1)S(1)} %get-tuple-element.65), channel_id=1, source_target_pairs={{0,2},{1,3},{2,0},{3,1},{4,6},{5,7},{6,4},{7,5},{8,10},{9,11},{10,... | collective-permute-start | bytes 491528 | tf_op jit(solution)/shard_map/ppermute | solution.py:526
  18.0 12.1 %collective-permute-start.14 = (bf16[2,1,320,128]{3,2,1,0:T(8,128)(2,1)S(1)}, bf16[2,1,320,128]{3,2,1,0:T(8,128)(2,1)S(1)}, u32[]{:S(2)}, u32[]{:S(2)}) collective-permute-start(bf16[2,1,320,128]{3,2,1,0:T(8,128)(2,1)S(1)} %get-tuple-element.66), channel_id=1, source_target_pairs={{0,3},{1,2},{2,1},{3,0},{4,7},{5,6},{6,5},{7,4},{8,11},{9,10},{10,... | collective-permute-start | bytes 491528 | tf_op jit(solution)/shard_map/ppermute | solution.py:526
  20.1 21.3 %collective-permute-start.7 = (bf16[2,1,320,128]{3,2,1,0:T(8,128)(2,1)S(1)}, bf16[2,1,320,128]{3,2,1,0:T(8,128)(2,1)S(1)}, u32[]{:S(2)}, u32[]{:S(2)}) collective-permute-start(bf16[2,1,320,128]{3,2,1,0:T(8,128)(2,1)S(1)} %get-tuple-element.57), channel_id=1, source_target_pairs={{0,2},{1,3},{2,0},{3,1},{4,6},{5,7},{6,4},{7,5},{8,10},{9,11},{10,... | collective-permute-start | bytes 491528 | tf_op jit(solution)/shard_map/ppermute | solution.py:526
  23.1 18.3 %collective-permute-start.8 = (bf16[2,1,320,128]{3,2,1,0:T(8,128)(2,1)S(1)}, bf16[2,1,320,128]{3,2,1,0:T(8,128)(2,1)S(1)}, u32[]{:S(2)}, u32[]{:S(2)}) collective-permute-start(bf16[2,1,320,128]{3,2,1,0:T(8,128)(2,1)S(1)} %get-tuple-element.58), channel_id=1, source_target_pairs={{0,3},{1,2},{2,1},{3,0},{4,7},{5,6},{6,5},{7,4},{8,11},{9,10},{10,... | collective-permute-start | bytes 491528 | tf_op jit(solution)/shard_map/ppermute | solution.py:526
  25.2 19.9 %collective-permute-start.3 = (bf16[1,1,320,128]{3,2,1,0:T(8,128)(2,1)S(1)}, bf16[1,1,320,128]{3,2,1,0:T(8,128)(2,1)S(1)}, u32[]{:S(2)}, u32[]{:S(2)}) collective-permute-start(bf16[1,1,320,128]{3,2,1,0:T(8,128)(2,1)S(1)} %get-tuple-element.52), channel_id=1, source_target_pairs={{0,1},{1,0},{2,3},{3,2},{4,5},{5,4},{6,7},{7,6},{8,9},{9,8},{10,11... | collective-permute-start | bytes 245768 | tf_op jit(solution)/shard_map/ppermute | solution.py:526
  27.1 17.9 %collective-permute-start.4 = (bf16[1,1,320,128]{3,2,1,0:T(8,128)(2,1)S(1)}, bf16[1,1,320,128]{3,2,1,0:T(8,128)(2,1)S(1)}, u32[]{:S(2)}, u32[]{:S(2)}) collective-permute-start(bf16[1,1,320,128]{3,2,1,0:T(8,128)(2,1)S(1)} %get-tuple-element.53), channel_id=1, source_target_pairs={{0,2},{1,3},{2,0},{3,1},{4,6},{5,7},{6,4},{7,5},{8,10},{9,11},{10,... | collective-permute-start | bytes 245768 | tf_op jit(solution)/shard_map/ppermute | solution.py:526
  30.1 14.9 %collective-permute-start.5 = (bf16[1,1,320,128]{3,2,1,0:T(8,128)(2,1)S(1)}, bf16[1,1,320,128]{3,2,1,0:T(8,128)(2,1)S(1)}, u32[]{:S(2)}, u32[]{:S(2)}) collective-permute-start(bf16[1,1,320,128]{3,2,1,0:T(8,128)(2,1)S(1)} %get-tuple-element.54), channel_id=1, source_target_pairs={{0,3},{1,2},{2,1},{3,0},{4,7},{5,6},{6,5},{7,4},{8,11},{9,10},{10,... | collective-permute-start | bytes 245768 | tf_op jit(solution)/shard_map/ppermute | solution.py:526
  47.5 4.6 %collective-permute-start.22 = (bf16[1040,512]{1,0:T(8,128)(2,1)S(1)}, bf16[1040,512]{1,0:T(8,128)(2,1)S(1)}, u32[]{:S(2)}, u32[]{:S(2)}) collective-permute-start(bf16[1040,512]{1,0:T(8,128)(2,1)S(1)} %bitcast.7), channel_id=1, source_target_pairs={{4,5},{6,7},{8,9},{10,11},{12,13},{14,15},{16,17},{18,19},{20,21},... | collective-permute-start | bytes 3194888 | tf_op jit(solution)/shard_map/ppermute | solution.py:529
  48.8 9.5 %collective-permute-start.20 = (bf16[1040,512]{1,0:T(8,128)(2,1)S(1)}, bf16[1040,512]{1,0:T(8,128)(2,1)S(1)}, u32[]{:S(2)}, u32[]{:S(2)}) collective-permute-start(bf16[1040,512]{1,0:T(8,128)(2,1)S(1)} %bitcast.8), channel_id=1, source_target_pairs={{2,3}} | collective-permute-start | bytes 3194888 | tf_op jit(solution)/shard_map/ppermute | solution.py:529
  53.2 8.9 %collective-permute-start.26 = (bf16[1040,512]{1,0:T(8,128)(2,1)S(1)}, bf16[1040,512]{1,0:T(8,128)(2,1)S(1)}, u32[]{:S(2)}, u32[]{:S(2)}) collective-permute-start(bf16[1040,512]{1,0:T(8,128)(2,1)S(1)} %join.1.refs_0_.own.refs_2_), channel_id=1, source_target_pairs={{9,11},{11,9}} | collective-permute-start | bytes 3194888 | tf_op jit(solution)/shard_map/ppermute | solution.py:529
  54.1 15.7 %collective-permute-start.28 = (bf16[1040,512]{1,0:T(8,128)(2,1)S(1)}, bf16[1040,512]{1,0:T(8,128)(2,1)S(1)}, u32[]{:S(2)}, u32[]{:S(2)}) collective-permute-start(bf16[1040,512]{1,0:T(8,128)(2,1)S(1)} %join.1.refs_0_.own.refs_2_), channel_id=1, source_target_pairs={{13,15},{15,13},{17,19},{19,17},{21,23},{23,21},{25,27},{27,25},{2... | collective-permute-start | bytes 3194888 | tf_op jit(solution)/shard_map/ppermute | solution.py:529
  58.8 0.7 collective-permute-start.21
  60.7 1.3 %collective-permute-start.25 = (f32[1,512]{1,0:T(1,128)S(1)}, f32[1,512]{1,0:T(1,128)S(1)}, u32[]{:S(2)}, u32[]{:S(2)}) collective-permute-start(f32[1,512]{1,0:T(1,128)S(1)} %hop.10), channel_id=1, source_target_pairs={{7,11}} | collective-permute-start | bytes 6152 | tf_op jit(solution)/shard_map/ppermute | solution.py:529
  61.4 0.7 collective-permute-start.24
  62.6 7.2 %collective-permute-start.27 = (f32[1,512]{1,0:T(1,128)S(1)}, f32[1,512]{1,0:T(1,128)S(1)}, u32[]{:S(2)}, u32[]{:S(2)}) collective-permute-start(f32[1,512]{1,0:T(1,128)S(1)} %span_hop.2), channel_id=1, source_target_pairs={{9,13},{11,15}} | collective-permute-start | bytes 6152 | tf_op jit(solution)/shard_map/ppermute | solution.py:529
  70.3 1.8 %collective-permute-start.29 = (f32[1,512]{1,0:T(1,128)S(1)}, f32[1,512]{1,0:T(1,128)S(1)}, u32[]{:S(2)}, u32[]{:S(2)}) collective-permute-start(f32[1,512]{1,0:T(1,128)S(1)} %span_hop.3), channel_id=1, source_target_pairs={{13,17},{15,19}} | collective-permute-start | bytes 6152 | tf_op jit(solution)/shard_map/ppermute | solution.py:529
  74.3 12.6 %collective-permute-start.32 = (f32[1,512]{1,0:T(1,128)S(1)}, f32[1,512]{1,0:T(1,128)S(1)}, u32[]{:S(2)}, u32[]{:S(2)}) collective-permute-start(f32[1,512]{1,0:T(1,128)S(1)} %hop.13), channel_id=1, source_target_pairs={{25,29},{27,31}} | collective-permute-start | bytes 6152 | tf_op jit(solution)/shard_map/ppermute | solution.py:529
  86.9 2.8 %collective-permute-start.33 = (f32[1,512]{1,0:T(1,128)S(1)}, f32[1,512]{1,0:T(1,128)S(1)}, u32[]{:S(2)}, u32[]{:S(2)}) collective-permute-start(f32[1,512]{1,0:T(1,128)S(1)} %lead.1.refs_0_), channel_id=1, source_target_pairs={{1,0},{3,2},{5,4},{7,6},{9,8},{11,10},{13,12},{15,14},{17,16},{19,... | collective-permute-start | bytes 6152 | tf_op jit(solution)/shard_map/ppermute | solution.py:529
  89.8 2.6 %collective-permute-start.34 = (f32[8,128]{1,0:T(8,128)S(1)}, f32[8,128]{1,0:T(8,128)S(1)}, u32[]{:S(2)}, u32[]{:S(2)}) collective-permute-start(f32[8,128]{1,0:T(8,128)S(1)} %get-tuple-element.86), channel_id=1, source_target_pairs={{0,1},{1,0},{2,3},{3,2},{4,5},{5,4},{6,7},{7,6},{8,9},{9,8},{10,11... | collective-permute-start | bytes 12296 | tf_op jit(solution)/shard_map/ppermute | solution.py:526
  90.6 2.5 %collective-permute-start.35 = (f32[8,128]{1,0:T(8,128)S(1)}, f32[8,128]{1,0:T(8,128)S(1)}, u32[]{:S(2)}, u32[]{:S(2)}) collective-permute-start(f32[8,128]{1,0:T(8,128)S(1)} %get-tuple-element.87), channel_id=1, source_target_pairs={{0,2},{1,3},{2,0},{3,1},{4,6},{5,7},{6,4},{7,5},{8,10},{9,11},{10,... | collective-permute-start | bytes 12296 | tf_op jit(solution)/shard_map/ppermute | solution.py:526
  90.7 3.3 %collective-permute-start.36 = (f32[8,128]{1,0:T(8,128)S(1)}, f32[8,128]{1,0:T(8,128)S(1)}, u32[]{:S(2)}, u32[]{:S(2)}) collective-permute-start(f32[8,128]{1,0:T(8,128)S(1)} %get-tuple-element.88), channel_id=1, source_target_pairs={{0,3},{1,2},{2,1},{3,0},{4,7},{5,6},{6,5},{7,4},{8,11},{9,10},{10,... | collective-permute-start | bytes 12296 | tf_op jit(solution)/shard_map/ppermute | solution.py:526
  (14 other events, 56.0 us)
